TPU v7x, 1024 devices: a whole 8x8x8 slice. The times are simulated.
1024 devices in a mesh: dp: 16 (over z, core), ctx: 4 (over x_lo), tp: 16 (over y, x_hi).
Axes of the slice: x: 8 (x_hi: 2, x_lo: 4; x = x_hi * 4 + x_lo), y: 8, z: 8, core: 2. Of those that a mesh axis runs over, the one named last changes fastest.
Arguments:
- routed_experts: int32 [16384, 8], P(('dp', 'ctx', 'tp')), may hold values from 0 to 63, all different within a row; in each aligned block of 16 rows (0 to 15, 16 to 31, ...) at most 3 rows name the same one
- route_gates: float32 [16384, 8], P(('dp', 'ctx', 'tp')), may hold values from 0.03 to 0.4
- expert_hidden: bfloat16 [64, 16, 64, 3, 768], P(('ctx', 'tp'), 'dp'), may hold values from -6 to 6
- down_weight: bfloat16 [64, 768, 4096], P(('ctx', 'tp'), None, 'dp'), may hold values from -0.21875 to 0.21875
- output_grad: bfloat16 [16384, 4096], P(('dp', 'ctx', 'tp')), may hold values from -1.5 to 1.5
Outputs:
- combined: bfloat16 [16384, 4096], P(('dp', 'ctx', 'tp'))
- down_gradient: float32 [64, 768, 4096], P(('ctx', 'tp'), None, 'dp')
Inputs may be any that keep to these rules, and one draw needn't show every extreme that they name: `routed_experts`: each row names 8 different experts. Among the routes of one device's 16 tokens (aligned blocks of rows) no expert is named more than 3 times, and in every draw some block names some expert exactly 3 times.
All inputs are finite; a program needn't handle non-finite values.
Results may differ from a plain program's by a relative error of at most 0.0049.
Values may be sent and summed in bfloat16 or wider, within the bound.
No kernel may reach another device: no remote copies, remote signals or barrier semaphores. Data moves between devices by JAX's collectives and lax.ppermute only.
A program may use at most 32 MiB of HBM per device.

v0:
```python
import jax
import jax.numpy as jnp
from jax import lax
from jax.sharding import PartitionSpec as P


def slot_ranks(flat_experts):
    count = flat_experts.shape[-1]
    same = flat_experts[..., :, None] == flat_experts[..., None, :]
    before = lax.broadcasted_iota(jnp.int32, (count, count), 1) < lax.broadcasted_iota(
        jnp.int32, (count, count), 0
    )
    return jnp.sum(jnp.logical_and(same, before), axis=-1)


def expert_move(buffer):
    return lax.all_to_all(buffer, ("ctx", "tp"), split_axis=0, concat_axis=0, tiled=True)


def body(routed_experts, route_gates, expert_hidden, down_weight, output_grad):
    replicas = lax.axis_size("dp")
    sources = lax.axis_size("ctx") * lax.axis_size("tp")
    tok_own, topk = routed_experts.shape
    routes = tok_own * topk
    capacity = expert_hidden.shape[3]
    width = output_grad.shape[1]
    column_part = width // replicas
    hidden_rows = expert_hidden[0]
    weight = down_weight[0]
    slot_count = sources * capacity
    expert_table, gate_table = (
        lax.all_gather(routed_experts.astype(jnp.float32), "dp", axis=0, tiled=True),
        lax.all_gather(route_gates, "dp", axis=0, tiled=True),
    )
    all_experts = expert_table.astype(jnp.int32).reshape(replicas, routes)
    all_gates = gate_table.reshape(replicas, tok_own, topk)
    grad_columns = lax.all_to_all(
        output_grad, "dp", split_axis=1, concat_axis=0, tiled=True
    ).reshape(replicas, tok_own, 1, column_part)
    ranks = slot_ranks(all_experts)
    target = all_experts * capacity + ranks
    placer = (
        lax.broadcasted_iota(jnp.int32, (1, slot_count, routes), 1) == target[:, None, :]
    ).astype(jnp.bfloat16)
    scaled = (
        (all_gates[:, :, :, None] * grad_columns.astype(jnp.float32))
        .reshape(replicas, routes, column_part)
        .astype(jnp.bfloat16)
    )
    outgoing = jnp.einsum("rpq,rqd->prd", placer, scaled, preferred_element_type=jnp.float32)
    outgoing = outgoing.astype(jnp.bfloat16).reshape(sources, capacity, replicas, column_part)
    grad_rows = expert_move(outgoing)
    piece = lax.all_gather(hidden_rows, "dp", axis=0, tiled=True)
    produced = jnp.einsum(
        "rsjf,fd->srjd", piece, weight, preferred_element_type=jnp.float32
    ).astype(jnp.bfloat16)
    outputs = produced
    gradient = jnp.einsum("rsjf,sjrd->fd", piece, grad_rows, preferred_element_type=jnp.float32)
    outputs, gradient = (outputs, gradient)
    returned = expert_move(outputs).reshape(sources * replicas * capacity, column_part)
    replica_index = lax.broadcasted_iota(jnp.int32, (replicas, routes), 0)
    position = all_experts * (replicas * capacity) + replica_index * capacity + ranks
    picked = (
        jnp.take(returned, position, axis=0)
        .astype(jnp.float32)
        .reshape(replicas, tok_own, topk, column_part)
    )
    partial_rows = jnp.sum(all_gates[:, :, :, None] * picked, axis=2).astype(jnp.bfloat16)
    combined = lax.all_to_all(partial_rows, "dp", split_axis=0, concat_axis=2, tiled=True)[0]
    return (combined, gradient[None])


def solution(mesh):
    in_specs = (
        P(("dp", "ctx", "tp"), None),
        P(("dp", "ctx", "tp"), None),
        P(("ctx", "tp"), "dp", None, None, None),
        P(("ctx", "tp"), None, "dp"),
        P(("dp", "ctx", "tp"), None),
    )
    out_specs = (P(("dp", "ctx", "tp"), None), P(("ctx", "tp"), None, "dp"))
    return jax.shard_map(body, mesh=mesh, in_specs=in_specs, out_specs=out_specs, check_vma=False)
```

profile of v0, /device:TPU:16, one launch (start us, length us, event | category | flops | bytes accessed | tf_op | source)
XLA Modules:
  0.0 200.6 jit_solution(17684255604260512443)
XLA Ops:
  7.2 0.7 all-gather.5.cloned.1.call-update
  7.9 1.6 copy.128
  9.5 16.8 %all-to-all-start.2 = ((bf16[16,16,256]{2,0,1:T(8,128)(2,1)}), bf16[16,16,256]{2,0,1:T(8,128)(2,1)S(1)}, u32[]{:S(2)}, u32[]{:S(2)}) async-start(bf16[16,16,256]{2,0,1:T(8,128)(2,1)} %bitcast.65), calls=%async_computation.2 | async-start | bytes 262144 | tf_op jit(solution)/shard_map/all_to_all | solution.py:37
  26.3 45.1 %all-gather.5.cloned.1.call-done = bf16[16,1,64,3,768]{4,2,3,1,0:T(8,128)(2,1)} async-done(((bf16[1,1,64,3,768]{4,2,3,1,0:T(8,128)(2,1)}), bf16[16,1,64,3,768]{4,2,3,1,0:T(8,128)(2,1)}) %all-gather.5.cloned.1.call-update) | async-done | bytes 4718608 | tf_op jit(solution)/shard_map/all_gather | solution.py:53
  71.4 3.7 %fusion.5 = bf16[64,16,3,256]{3,0,2,1:T(8,128)(2,1)S(1)} fusion(bf16[1,768,256]{2,1,0:T(8,128)(2,1)S(1)} %copy-done, bf16[16,1,64,3,768]{4,2,3,1,0:T(8,128)(2,1)} %all-gather.5.cloned.1.call-done), kind=kOutput, calls=%fused_computation.11 | convolution fusion | flops 1208745984 | bytes 6684672 | tf_op jit(solution)/shard_map/rsjf,fd->srjd/dot_general | solution.py:54
  75.1 2.1 %copy.102 = bf16[64,16,3,256]{3,1,2,0:T(8,128)(2,1)} copy(bf16[64,16,3,256]{3,0,2,1:T(8,128)(2,1)S(1)} %fusion.5) | data formatting | bytes 3145728 | tf_op jit(solution)/shard_map/convert_element_type | solution.py:56
  77.2 12.9 %all-to-all-start = ((bf16[64,16,3,256]{3,1,2,0:T(8,128)(2,1)}), bf16[64,16,3,256]{3,1,2,0:T(8,128)(2,1)S(1)}, u32[]{:S(2)}, u32[]{:S(2)}) async-start(bf16[64,16,3,256]{3,1,2,0:T(8,128)(2,1)} %copy.102), calls=%async_computation | async-start | bytes 3145728 | tf_op jit(solution)/shard_map/all_to_all | solution.py:17
  90.1 15.9 %all-gather.2 = f32[16,16,8]{1,2,0:T(8,128)S(1)} all-gather(f32[1,16,8]{1,2,0:T(8,128)S(1)} %convert_bitcast_fusion.2), channel_id=1, replica_groups=mesh['dp'=16,'ctx'=4,'tp'=16] {'dp'}, dimensions={0}, use_global_device_ids=true | all-gather | bytes 8704 | tf_op jit(solution)/shard_map/all_gather | solution.py:32
  105.9 0.1 copy.97
  106.0 14.7 %all-gather.1 = f32[16,16,8]{1,2,0:T(8,128)S(1)} all-gather(f32[1,16,8]{1,2,0:T(8,128)S(1)} %bitcast.70), channel_id=1, replica_groups=mesh['dp'=16,'ctx'=4,'tp'=16] {'dp'}, dimensions={0}, use_global_device_ids=true | all-gather | bytes 8704 | tf_op jit(solution)/shard_map/all_gather | solution.py:33
  120.8 0.1 copy.106
  120.9 0.1 copy.107
  121.0 0.6 convert_reduce_fusion
  121.7 0.7 fusion.4
  122.4 2.1 %copy.110 = bf16[192,16,256]{2,1,0:T(8,128)(2,1)} copy(bf16[192,16,256]{2,0,1:T(8,128)(2,1)S(1)} %fusion.4) | data formatting | bytes 3145728 | tf_op jit(solution)/shard_map/convert_element_type | solution.py:51
  124.5 8.4 %all-to-all-done = bf16[64,16,3,256]{3,1,2,0:T(8,128)(2,1)S(1)} async-done(((bf16[64,16,3,256]{3,1,2,0:T(8,128)(2,1)}), bf16[64,16,3,256]{3,1,2,0:T(8,128)(2,1)S(1)}, u32[]{:S(2)}, u32[]{:S(2)}) %all-to-all-start) | async-done | bytes 1572896 | tf_op jit(solution)/shard_map/all_to_all | solution.py:17
  132.9 5.1 %all-to-all-start.3 = ((bf16[64,3,16,256]{3,2,1,0:T(8,128)(2,1)}), bf16[64,3,16,256]{3,2,1,0:T(8,128)(2,1)}, u32[]{:S(2)}, u32[]{:S(2)}) async-start(bf16[64,3,16,256]{3,2,1,0:T(8,128)(2,1)} %bitcast.19), calls=%async_computation.3 | async-start | bytes 3145728 | tf_op jit(solution)/shard_map/all_to_all | solution.py:17
  138.0 0.1 copy.96
  138.1 0.1 copy.100
  138.3 0.1 compare_and_fusion
  138.3 0.1 copy.101
  138.5 0.1 fusion.18
  138.6 2.5 %copy.103 = bf16[64,16,3,256]{3,2,1,0:T(4,128)(2,1)} copy(bf16[64,16,3,256]{3,1,2,0:T(8,128)(2,1)S(1)} %all-to-all-done) | data formatting | bytes 3145728 | tf_op jit(solution)/shard_map/all_to_all | solution.py:17
  141.0 3.9 %reshape.121 = bf16[3072,256]{1,0:T(8,128)(2,1)S(1)} reshape(bf16[64,16,3,256]{3,2,1,0:T(4,128)(2,1)} %copy.103) | data formatting | bytes 3145728 | tf_op jit(solution)/shard_map/reshape | solution.py:60
  144.9 7.5 %gather_fusion = bf16[2048,256]{1,0:T(8,128)(2,1)S(1)} fusion(bf16[3072,256]{1,0:T(8,128)(2,1)S(1)} %reshape.121, s32[2048]{0:T(1024)S(1)} %fusion.18), kind=kCustom, calls=%fused_computation | custom fusion | bytes 2105344 | tf_op jit(solution)/shard_map/jit(_take)/gather | solution.py:64
  152.5 1.6 multiply_reduce_fusion
  154.0 26.2 %all-to-all-done.3 = bf16[64,3,16,256]{3,2,1,0:T(8,128)(2,1)} async-done(((bf16[64,3,16,256]{3,2,1,0:T(8,128)(2,1)}), bf16[64,3,16,256]{3,2,1,0:T(8,128)(2,1)}, u32[]{:S(2)}, u32[]{:S(2)}) %all-to-all-start.3) | async-done | bytes 1572896 | tf_op jit(solution)/shard_map/all_to_all | solution.py:17
  180.3 4.2 %all-to-all-start.1 = ((bf16[16,16,256]{2,1,0:T(8,128)(2,1)}), bf16[16,16,256]{2,1,0:T(8,128)(2,1)S(1)}, u32[]{:S(2)}, u32[]{:S(2)}) async-start(bf16[16,16,256]{2,1,0:T(8,128)(2,1)} %multiply_reduce_fusion), calls=%async_computation.1 | async-start | bytes 262144 | tf_op jit(solution)/shard_map/all_to_all | solution.py:69
  184.5 5.9 %fusion.6 = f32[1,768,256]{1,2,0:T(8,128)S(1)} fusion(bf16[16,64,3,768]{3,1,2,0:T(8,128)(2,1)} %bitcast.71, bf16[64,3,16,256]{3,2,1,0:T(8,128)(2,1)} %all-to-all-done.3), kind=kOutput, calls=%fused_computation.12 | convolution fusion | flops 1207959552 | bytes 7077888 | tf_op jit(solution)/shard_map/rsjf,sjrd->fd/dot_general | solution.py:58
  190.4 1.1 copy.113
  191.5 1.6 all-to-all-done.1
  193.1 0.7 copy.117
  (17 shorter events, 0.3 us)
Async XLA Ops:
  7.2 64.2 %copy-start = (bf16[1,768,256]{2,1,0:T(8,128)(2,1)S(1)}, bf16[1,768,256]{2,1,0:T(8,128)(2,1)}, u32[]{:S(2)}) copy-start(bf16[1,768,256]{2,1,0:T(8,128)(2,1)} %param.8) | copy-start | bytes 1179652
  7.2 64.2 %all-gather.5.cloned.1.call-start = ((), (), s32[]{:S(2)}) async-start(), calls=%async_computation.4 | async-start | bytes 5013504 | tf_op jit(solution)/shard_map/all_gather | solution.py:53
  9.5 67.7 %all-to-all-start.2 = ((bf16[16,16,256]{2,0,1:T(8,128)(2,1)}), bf16[16,16,256]{2,0,1:T(8,128)(2,1)S(1)}, u32[]{:S(2)}, u32[]{:S(2)}) async-start(bf16[16,16,256]{2,0,1:T(8,128)(2,1)} %bitcast.65), calls=%async_computation.2 | async-start | bytes 262144 | tf_op jit(solution)/shard_map/all_to_all | solution.py:37
  77.2 12.9 %copy-start.2 = (s32[16,8]{0,1:T(8,128)S(1)}, s32[16,8]{0,1:T(8,128)}, u32[]{:S(2)}) copy-start(s32[16,8]{0,1:T(8,128)} %param.5) | copy-start | bytes 1540
  77.2 28.9 %copy-start.1 = (f32[16,8]{0,1:T(8,128)S(1)}, f32[16,8]{0,1:T(8,128)}, u32[]{:S(2)}) copy-start(f32[16,8]{0,1:T(8,128)} %param.6) | copy-start | bytes 1540
  77.2 55.7 %all-to-all-start = ((bf16[64,16,3,256]{3,1,2,0:T(8,128)(2,1)}), bf16[64,16,3,256]{3,1,2,0:T(8,128)(2,1)S(1)}, u32[]{:S(2)}, u32[]{:S(2)}) async-start(bf16[64,16,3,256]{3,1,2,0:T(8,128)(2,1)} %copy.102), calls=%async_computation | async-start | bytes 3145728 | tf_op jit(solution)/shard_map/all_to_all | solution.py:17
  132.9 47.4 %all-to-all-start.3 = ((bf16[64,3,16,256]{3,2,1,0:T(8,128)(2,1)}), bf16[64,3,16,256]{3,2,1,0:T(8,128)(2,1)}, u32[]{:S(2)}, u32[]{:S(2)}) async-start(bf16[64,3,16,256]{3,2,1,0:T(8,128)(2,1)} %bitcast.19), calls=%async_computation.3 | async-start | bytes 3145728 | tf_op jit(solution)/shard_map/all_to_all | solution.py:17
  180.3 12.8 %all-to-all-start.1 = ((bf16[16,16,256]{2,1,0:T(8,128)(2,1)}), bf16[16,16,256]{2,1,0:T(8,128)(2,1)S(1)}, u32[]{:S(2)}, u32[]{:S(2)}) async-start(bf16[16,16,256]{2,1,0:T(8,128)(2,1)} %multiply_reduce_fusion), calls=%async_computation.1 | async-start | bytes 262144 | tf_op jit(solution)/shard_map/all_to_all | solution.py:69
Sparse Core Ops, SparseCore 0:
  10.7 60.6 all-gather.4
where the time goes:
time: 202 us; the launch traced here: 201 us
  waiting for transfers between devices  81.9 us (41%)
  starting transfers between devices  39 us (19%)
  blocking collectives  30.6 us (15%)
  local copies, waits for them, and re-layouts  22.1 us (11%)
  between operations  14.2 us (7%)
  matrix products  10.3 us (5%)
  other arithmetic  2.46 us (1%)
    all_gather x1, waiting for transfers between devices, body(): piece = lax.all_gather(hidden_rows, 'dp', axis=0, tiled=True)  45.1 us
    all_to_all x2, waiting for transfers between devices, expert_move(): lax.all_to_all(buffer, ('ctx', 'tp'), split_axis=0, concat_axis=0, tiled=...  34.6 us
    all_to_all x2, starting transfers between devices, expert_move(): lax.all_to_all(buffer, ('ctx', 'tp'), split_axis=0, concat_axis=0, tiled=...  18 us
    all_to_all x1, starting transfers between devices, body(): lax.all_to_all(output_grad, 'dp', split_axis=1, concat_axis=0, tiled=True)  16.8 us
    all_gather x1, blocking collectives, body(): lax.all_gather(routed_experts.astype(jnp.float32), 'dp', axis=0, tiled=True)  15.9 us
    all_gather x1, blocking collectives, body(): lax.all_gather(route_gates, 'dp', axis=0, tiled=True)  14.7 us
    gather x1, local copies, waits for them, and re-layouts, body(): jnp.take(returned, position, axis=0).astype(jnp.float32)  7.5 us
    dot_general x1, matrix products, body(): jnp.einsum('rsjf,sjrd->fd', piece, grad_rows, preferred_element_type=jnp....  5.93 us
  transfers between devices with their start and end apart: 5, of which 4 were waited for; matrix products, arithmetic and copies ran while one was open for 17% of the time, Pallas kernels for 0%

commit v1 on v0

v1 whole, which is shorter than its diff:
```python
import jax
import jax.numpy as jnp
from jax import lax
from jax.sharding import PartitionSpec as P

CORES = 2
LANES = 128
F32 = jnp.float32
BF16 = jnp.bfloat16


def expert_move(buffer):
    return lax.all_to_all(buffer, ("ctx", "tp"), split_axis=0, concat_axis=0, tiled=True)


def parts_of(values):
    high = values.astype(BF16)
    low = (values - high.astype(F32)).astype(BF16)
    return high, low


def three_parts(values):
    high, low = parts_of(values)
    last = (values - high.astype(F32) - low.astype(F32)).astype(BF16)
    return high, low, last


def body(routed_experts, route_gates, expert_hidden, down_weight, output_grad):
    dp = lax.axis_size("dp")
    chips = dp // CORES
    experts = lax.axis_size("ctx") * lax.axis_size("tp")
    own, topk = routed_experts.shape
    capacity, depth = expert_hidden.shape[3:]
    width = output_grad.shape[1]
    half = width // dp
    part = half * CORES
    tokens = chips * own
    column = [[z * CORES + c for z in range(chips)] for c in range(CORES)]
    swap = [(d, d ^ 1) for d in range(dp)]
    core = lax.axis_index("dp") & 1

    def chip_move(blocks):
        return lax.all_to_all(
            blocks, "dp", split_axis=0, concat_axis=0, tiled=True, axis_index_groups=column
        )

    rows = jnp.swapaxes(expert_hidden[0, 0], 0, 1).reshape(capacity * experts, depth)
    gathered = lax.all_gather(rows, "dp", axis=0, tiled=False, axis_index_groups=column)
    weight = down_weight[0]
    other = lax.ppermute(weight, "dp", swap)
    weight = jnp.concatenate(
        [jnp.where(core == 0, weight, other), jnp.where(core == 0, other, weight)], axis=1
    )

    table = jnp.concatenate(
        [routed_experts.astype(F32).astype(BF16), *three_parts(route_gates)], axis=1
    )
    table = jnp.pad(table, ((0, 0), (0, LANES - table.shape[1])))
    blocks = jnp.swapaxes(output_grad.reshape(own, chips, part), 0, 1)
    blocks = jnp.concatenate([blocks, jnp.broadcast_to(table, (chips, own, LANES))], axis=2)
    arrived = chip_move(blocks)
    grads = arrived[:, :, :part].reshape(tokens, part)
    table = arrived[:, :, part:].reshape(tokens, LANES).astype(F32)
    named = table[:, :topk]
    gates = sum(table[:, topk * i : topk * (i + 1)] for i in (1, 2, 3))

    ids = lax.broadcasted_iota(jnp.int32, (experts, tokens), 0).astype(F32)
    hit = named.T[:, None, :] == ids[None]
    names = jnp.any(hit, axis=0)
    gate_of = jnp.sum(jnp.where(hit, gates.T[:, None, :], 0.0), axis=0)
    at = lax.broadcasted_iota(jnp.int32, (tokens, tokens), 0)
    to = lax.broadcasted_iota(jnp.int32, (tokens, tokens), 1)
    earlier = jnp.logical_and(at // own == to // own, at < to).astype(BF16)
    rank = jnp.dot(names.astype(BF16), earlier, preferred_element_type=F32)
    replica = (lax.broadcasted_iota(jnp.int32, (experts, tokens), 1) // own).astype(F32)
    code = jnp.where(names, replica * capacity + rank, -1.0)
    lines = capacity * chips
    place = code[:, None, :] == lax.broadcasted_iota(jnp.int32, (1, lines, tokens), 1).astype(F32)
    placer = jnp.concatenate(
        [jnp.where(place, p.astype(F32)[:, None, :], 0.0).astype(BF16) for p in parts_of(gate_of)],
        axis=2,
    ).reshape(experts * lines, 2 * tokens)

    outgoing = jnp.dot(placer, jnp.concatenate([grads, grads], axis=0), preferred_element_type=F32)
    grad_rows = expert_move(outgoing.astype(BF16).reshape(experts, lines, part))

    hidden = gathered.reshape(lines * experts, depth)
    produced = jnp.dot(hidden, weight, preferred_element_type=F32).astype(BF16)
    returned = expert_move(jnp.swapaxes(produced.reshape(lines, experts, part), 0, 1))

    grad_rows = jnp.swapaxes(grad_rows, 0, 1).reshape(lines * experts, part)
    gradient = lax.dot_general(
        hidden, grad_rows, (((0,), (0,)), ((), ())), preferred_element_type=F32
    )
    kept = lax.dynamic_slice_in_dim(gradient, core * half, half, 1)
    gradient = kept + lax.ppermute(
        lax.dynamic_slice_in_dim(gradient, (1 - core) * half, half, 1), "dp", swap
    )

    mixed = lax.dot_general(
        placer,
        returned.reshape(experts * lines, part),
        (((0,), (0,)), ((), ())),
        preferred_element_type=F32,
    )
    mixed = (mixed[:tokens] + mixed[tokens:]).astype(BF16).reshape(chips, own, part)
    combined = jnp.swapaxes(chip_move(mixed), 0, 1).reshape(own, width)
    return (combined, gradient[None])


def solution(mesh):
    in_specs = (
        P(("dp", "ctx", "tp"), None),
        P(("dp", "ctx", "tp"), None),
        P(("ctx", "tp"), "dp", None, None, None),
        P(("ctx", "tp"), None, "dp"),
        P(("dp", "ctx", "tp"), None),
    )
    out_specs = (P(("dp", "ctx", "tp"), None), P(("ctx", "tp"), None, "dp"))
    return jax.shard_map(body, mesh=mesh, in_specs=in_specs, out_specs=out_specs, check_vma=False)
```

time: 202 us -> 166 us (0.82)
  blocking collectives: 30.6 us -> 0 us
  local copies, waits for them, and re-layouts: 22.1 us -> 10.9 us
  starting transfers between devices: 39 us -> 42.5 us
  other arithmetic: 2.46 us -> 5.83 us
    all_gather x1, waiting for transfers between devices: 45.1 us -> 12.3 us  [body(): lax.all_gather(rows, 'dp', axis=0, tiled=False, axis_index_groups=column)]
    all_gather x2 -> x0, blocking collectives: 30.6 us -> none  [the longest x1 15.9 us: body(): lax.all_gather(routed_experts.astype(jnp.float32), 'dp', axis=0, tiled=True)]
    all_to_all x2, waiting for transfers between devices: 34.6 us -> 51.6 us  [expert_move(): lax.all_to_all(buffer, ('ctx', 'tp'), split_axis=0, concat_axis=0, tiled=...]
    all_to_all x2, waiting for transfers between devices: 1.55 us -> 15.7 us  [chip_move(): lax.all_to_all(blocks, 'dp', split_axis=0, concat_axis=0, tiled=True, axi...]
    gather x1 -> x0, local copies, waits for them, and re-layouts: 7.5 us -> none  [body(): jnp.take(returned, position, axis=0).astype(jnp.float32)]
    convert_element_type x1 -> x9, other arithmetic: 0.02 us -> 4.17 us  [the longest x2 1.99 us: body(): jnp.where(place, p.astype(F32)[:, None, :], 0.0).astype(BF16)]
    ppermute x0 -> x2, starting transfers between devices: none -> 3.83 us  [the longest x1 1.92 us: body(): other = lax.ppermute(weight, 'dp', swap)]
    reshape x2 -> x1, local copies, waits for them, and re-layouts: 3.96 us -> 0.66 us  [body(): combined = jnp.swapaxes(chip_move(mixed), 0, 1).reshape(own, width)]
  transfers between devices with their start and end apart: 5 -> 7, of which waited for: 4 -> 6; matrix products, arithmetic and copies ran while one was open for 17% -> 14% of each run, Pallas kernels for 0% -> 0%
where the time goes in v1:
time: 166 us; the launch traced here: 165 us
  waiting for transfers between devices  82 us (49%)
  starting transfers between devices  42.5 us (26%)
  between operations  14.3 us (9%)
  local copies, waits for them, and re-layouts  10.9 us (7%)
  matrix products  9.42 us (6%)
  other arithmetic  5.83 us (4%)
    all_to_all x2, waiting for transfers between devices, expert_move(): lax.all_to_all(buffer, ('ctx', 'tp'), split_axis=0, concat_axis=0, tiled=...  51.6 us
    all_to_all x2, starting transfers between devices, chip_move(): lax.all_to_all(blocks, 'dp', split_axis=0, concat_axis=0, tiled=True, axi...  20.1 us
    all_to_all x2, starting transfers between devices, expert_move(): lax.all_to_all(buffer, ('ctx', 'tp'), split_axis=0, concat_axis=0, tiled=...  18.6 us
    all_to_all x2, waiting for transfers between devices, chip_move(): lax.all_to_all(blocks, 'dp', split_axis=0, concat_axis=0, tiled=True, axi...  15.7 us
    all_gather x1, waiting for transfers between devices, body(): lax.all_gather(rows, 'dp', axis=0, tiled=False, axis_index_groups=column)  12.3 us
    dot_general x1, matrix products, body(): produced = jnp.dot(hidden, weight, preferred_element_type=F32).astype(BF16)  4.25 us
    unnamed x13, local copies, waits for them, and re-layouts  4.17 us
  transfers between devices with their start and end apart: 7, of which 6 were waited for; matrix products, arithmetic and copies ran while one was open for 14% of the time, Pallas kernels for 0%

profile of v1, /device:TPU:16, one launch (start us, length us, event | category | flops | bytes accessed | tf_op | source)
XLA Modules:
  0.0 164.9 jit_solution(10739479994652118241)
XLA Ops:
  7.2 0.7 all-gather.2.cloned.1.call-update
  7.9 0.8 fusion.41
  8.7 0.7 convert_convert_fusion.1
  9.4 1.0 copy.67
  10.5 0.7 copy.49
  11.1 16.7 %all-to-all-start = ((bf16[8,16,640]{2,1,0:T(8,128)(2,1)}), bf16[8,16,640]{2,1,0:T(8,128)(2,1)S(1)}, u32[]{:S(2)}, u32[]{:S(2)}) async-start(bf16[8,16,640]{2,1,0:T(8,128)(2,1)} %copy.49), calls=%async_computation | async-start | bytes 327680 | tf_op jit(solution)/shard_map/all_to_all | solution.py:43
  27.8 0.5 copy-done.4
  28.5 9.1 %all-to-all-done = bf16[8,16,640]{2,1,0:T(8,128)(2,1)S(1)} async-done(((bf16[8,16,640]{2,1,0:T(8,128)(2,1)}), bf16[8,16,640]{2,1,0:T(8,128)(2,1)S(1)}, u32[]{:S(2)}, u32[]{:S(2)}) %all-to-all-start) | async-done | bytes 163872 | tf_op jit(solution)/shard_map/all_to_all | solution.py:43
  39.0 1.8 %convolution_convert_fusion = bf16[1536,512]{1,0:T(8,128)(2,1)} fusion(bf16[1536,128]{1,0:T(8,128)(2,1)S(1)} %get-tuple-element.17, bf16[1536,128]{1,0:T(8,128)(2,1)S(1)} %get-tuple-element.16, bf16[128,512]{1,0:T(8,128)(2,1)S(1)} %bitcast.72), kind=kOutput, calls=%fused_computation | convolution fusion | flops 405536768 | bytes 2490368 | tf_op jit(solution)/shard_map/dot_general | solution.py:84
  40.7 13.5 %all-to-all-start.3 = ((bf16[64,24,512]{2,1,0:T(8,128)(2,1)}), bf16[64,24,512]{2,1,0:T(8,128)(2,1)S(1)}, u32[]{:S(2)}, u32[]{:S(2)}) async-start(bf16[64,24,512]{2,1,0:T(8,128)(2,1)} %bitcast.20), calls=%async_computation.3 | async-start | bytes 3145728 | tf_op jit(solution)/shard_map/all_to_all | solution.py:13
  54.2 1.9 %collective-permute-start = (bf16[768,256]{1,0:T(8,128)(2,1)S(1)}, bf16[768,256]{1,0:T(8,128)(2,1)S(1)}, u32[]{:S(2)}, u32[]{:S(2)}) collective-permute-start(bf16[768,256]{1,0:T(8,128)(2,1)S(1)} %bitcast.68), channel_id=1, source_target_pairs={{0,64},{64,0},{128,192},{192,128},{256,320},{320,256},{384,448},{4... | collective-permute-start | bytes 1179656 | tf_op jit(solution)/shard_map/ppermute | solution.py:50
  56.2 1.7 %collective-permute-done = bf16[768,256]{1,0:T(8,128)(2,1)S(1)} collective-permute-done((bf16[768,256]{1,0:T(8,128)(2,1)S(1)}, bf16[768,256]{1,0:T(8,128)(2,1)S(1)}, u32[]{:S(2)}, u32[]{:S(2)}) %collective-permute-start) | collective-permute-done | bytes 393248 | tf_op jit(solution)/shard_map/ppermute | solution.py:50
  57.9 12.3 %all-gather.2.cloned.1.call-done = bf16[8,192,768]{2,1,0:T(8,128)(2,1)} async-done(((bf16[1,192,768]{2,1,0:T(8,128)(2,1)}), bf16[8,192,768]{2,1,0:T(8,128)(2,1)}) %all-gather.2.cloned.1.call-update) | async-done | bytes 2359312 | tf_op jit(solution)/shard_map/all_gather | solution.py:48
  70.2 4.3 %fusion = bf16[1536,512]{0,1:T(8,128)(2,1)} fusion(bf16[1536,768]{1,0:T(8,128)(2,1)} %bitcast.64, bf16[768,256]{1,0:T(8,128)(2,1)S(1)} %get-tuple-element.13, bf16[768,256]{1,0:T(8,128)(2,1)S(1)} %get-tuple-element.12), kind=kOutput, calls=%fused_computation.2 | convolution fusion | flops 1210318848 | bytes 4718592 | tf_op jit(solution)/shard_map/dot_general | solution.py:88
  74.5 1.7 %copy.52 = bf16[1536,512]{1,0:T(8,128)(2,1)S(1)} copy(bf16[1536,512]{0,1:T(8,128)(2,1)} %fusion) | data formatting | bytes 3145728 | tf_op jit(solution)/shard_map/convert_element_type | solution.py:88
  76.2 2.0 %copy.53 = bf16[64,24,512]{2,1,0:T(8,128)(2,1)} copy(bf16[64,24,512]{2,0,1:T(8,128)(2,1)S(1)} %bitcast.62) | data formatting | bytes 3145728 | tf_op jit(solution)/shard_map/transpose | solution.py:89
  78.2 16.8 %all-to-all-done.3 = bf16[64,24,512]{2,1,0:T(8,128)(2,1)S(1)} async-done(((bf16[64,24,512]{2,1,0:T(8,128)(2,1)}), bf16[64,24,512]{2,1,0:T(8,128)(2,1)S(1)}, u32[]{:S(2)}, u32[]{:S(2)}) %all-to-all-start.3) | async-done | bytes 1572896 | tf_op jit(solution)/shard_map/all_to_all | solution.py:13
  95.0 5.1 %all-to-all-start.1 = ((bf16[64,24,512]{2,1,0:T(8,128)(2,1)}), bf16[64,24,512]{2,1,0:T(8,128)(2,1)S(1)}, u32[]{:S(2)}, u32[]{:S(2)}) async-start(bf16[64,24,512]{2,1,0:T(8,128)(2,1)} %copy.53), calls=%async_computation.1 | async-start | bytes 3145728 | tf_op jit(solution)/shard_map/all_to_all | solution.py:13
  100.1 0.5 copy.59
  100.6 1.2 copy-done
  101.8 1.4 fusion.42
  103.3 0.9 dynamic-slice_bitcast_fusion
  104.2 1.9 %collective-permute-start.1 = (f32[768,256]{0,1:T(8,128)}, f32[768,256]{0,1:T(8,128)}, u32[]{:S(2)}, u32[]{:S(2)}) collective-permute-start(f32[768,256]{0,1:T(8,128)} %dynamic-slice_bitcast_fusion), channel_id=1, source_target_pairs={{0,64},{64,0},{128,192},{192,128},{256,320},{320,256},{384,448},{4... | collective-permute-start | bytes 2359304 | tf_op jit(solution)/shard_map/ppermute | solution.py:96
  106.1 1.7 %fusion.7 = (bf16[64,24,128]{2,0,1:T(8,128)(2,1)S(1)}, bf16[64,24,128]{2,0,1:T(8,128)(2,1)}) fusion(bf16[64,128]{1,0:T(8,128)(2,1)S(1)} %get-tuple-element.20, f32[64,128]{1,0:T(8,128)} %copy-done.3, f32[24]{0:T(128)} %copy-done.4, bf16[64,128]{1,0:T(8,128)(2,1)} %copy-done.2), kind=kLoop, calls=%fused_computation.10 | loop fusion | flops 589824 | bytes 852064 | tf_op jit(solution)/shard_map/convert_element_type | solution.py:80
  107.8 34.8 %all-to-all-done.1 = bf16[64,24,512]{2,1,0:T(8,128)(2,1)S(1)} async-done(((bf16[64,24,512]{2,1,0:T(8,128)(2,1)}), bf16[64,24,512]{2,1,0:T(8,128)(2,1)S(1)}, u32[]{:S(2)}, u32[]{:S(2)}) %all-to-all-start.1) | async-done | bytes 1572896 | tf_op jit(solution)/shard_map/all_to_all | solution.py:13
  142.6 1.7 %fusion.3 = f32[256,512]{1,0:T(8,128)S(1)} fusion(bf16[64,24,512]{2,1,0:T(8,128)(2,1)S(1)} %all-to-all-done.1, bf16[64,24,128]{2,0,1:T(8,128)(2,1)} %get-tuple-element.19, bf16[64,24,128]{2,0,1:T(8,128)(2,1)S(1)} %get-tuple-element.18), kind=kOutput, calls=%fused_computation.5 | convolution fusion | flops 404226048 | bytes 2883584 | tf_op jit(solution)/shard_map/dot_general | solution.py:100
  144.4 0.7 fusion.22
  145.1 3.4 %all-to-all-start.2 = ((bf16[8,16,512]{2,1,0:T(8,128)(2,1)}), bf16[8,16,512]{2,1,0:T(8,128)(2,1)S(1)}, u32[]{:S(2)}, u32[]{:S(2)}) async-start(bf16[8,16,512]{2,1,0:T(8,128)(2,1)} %bitcast.14), calls=%async_computation.2 | async-start | bytes 262144 | tf_op jit(solution)/shard_map/all_to_all | solution.py:43
  148.4 1.2 fusion.18
  149.7 1.1 copy.60
  150.8 6.6 %all-to-all-done.2 = bf16[8,16,512]{2,1,0:T(8,128)(2,1)S(1)} async-done(((bf16[8,16,512]{2,1,0:T(8,128)(2,1)}), bf16[8,16,512]{2,1,0:T(8,128)(2,1)S(1)}, u32[]{:S(2)}, u32[]{:S(2)}) %all-to-all-start.2) | async-done | bytes 131104 | tf_op jit(solution)/shard_map/all_to_all | solution.py:43
  157.4 0.7 copy.66
  (33 shorter events, 1.6 us)
Async XLA Ops:
  7.2 63.1 %all-gather.2.cloned.1.call-start = ((), (), s32[]{:S(2)}) async-start(), calls=%async_computation.4 | async-start | bytes 2654208 | tf_op jit(solution)/shard_map/all_gather | solution.py:48
  11.1 26.5 %all-to-all-start = ((bf16[8,16,640]{2,1,0:T(8,128)(2,1)}), bf16[8,16,640]{2,1,0:T(8,128)(2,1)S(1)}, u32[]{:S(2)}, u32[]{:S(2)}) async-start(bf16[8,16,640]{2,1,0:T(8,128)(2,1)} %copy.49), calls=%async_computation | async-start | bytes 327680 | tf_op jit(solution)/shard_map/all_to_all | solution.py:43
  27.8 0.5 copy-start.4
  38.3 0.6 copy-start.3
  38.3 0.6 copy-start.2
  40.7 13.5 %copy-start.1 = (bf16[1,768,256]{2,1,0:T(8,128)(2,1)S(1)}, bf16[1,768,256]{2,1,0:T(8,128)(2,1)}, u32[]{:S(2)}) copy-start(bf16[1,768,256]{2,1,0:T(8,128)(2,1)} %param.8) | copy-start | bytes 1179652
  40.7 54.3 %all-to-all-start.3 = ((bf16[64,24,512]{2,1,0:T(8,128)(2,1)}), bf16[64,24,512]{2,1,0:T(8,128)(2,1)S(1)}, u32[]{:S(2)}, u32[]{:S(2)}) async-start(bf16[64,24,512]{2,1,0:T(8,128)(2,1)} %bitcast.20), calls=%async_computation.3 | async-start | bytes 3145728 | tf_op jit(solution)/shard_map/all_to_all | solution.py:13
  54.2 3.6 %collective-permute-start = (bf16[768,256]{1,0:T(8,128)(2,1)S(1)}, bf16[768,256]{1,0:T(8,128)(2,1)S(1)}, u32[]{:S(2)}, u32[]{:S(2)}) collective-permute-start(bf16[768,256]{1,0:T(8,128)(2,1)S(1)} %bitcast.68), channel_id=1, source_target_pairs={{0,64},{64,0},{128,192},{192,128},{256,320},{320,256},{384,448},{4... | collective-permute-start | bytes 1179656 | tf_op jit(solution)/shard_map/ppermute | solution.py:50
  95.0 47.6 %all-to-all-start.1 = ((bf16[64,24,512]{2,1,0:T(8,128)(2,1)}), bf16[64,24,512]{2,1,0:T(8,128)(2,1)S(1)}, u32[]{:S(2)}, u32[]{:S(2)}) async-start(bf16[64,24,512]{2,1,0:T(8,128)(2,1)} %copy.53), calls=%async_computation.1 | async-start | bytes 3145728 | tf_op jit(solution)/shard_map/all_to_all | solution.py:13
  100.1 1.7 %copy-start = (bf16[8,192,768]{2,1,0:T(8,128)(2,1)S(1)}, bf16[8,192,768]{2,1,0:T(8,128)(2,1)}, u32[]{:S(2)}) copy-start(bf16[8,192,768]{2,1,0:T(8,128)(2,1)} %all-gather.2.cloned.1.call-done) | copy-start | bytes 7077892
  104.2 44.2 %collective-permute-start.1 = (f32[768,256]{0,1:T(8,128)}, f32[768,256]{0,1:T(8,128)}, u32[]{:S(2)}, u32[]{:S(2)}) collective-permute-start(f32[768,256]{0,1:T(8,128)} %dynamic-slice_bitcast_fusion), channel_id=1, source_target_pairs={{0,64},{64,0},{128,192},{192,128},{256,320},{320,256},{384,448},{4... | collective-permute-start | bytes 2359304 | tf_op jit(solution)/shard_map/ppermute | solution.py:96
  145.1 12.4 %all-to-all-start.2 = ((bf16[8,16,512]{2,1,0:T(8,128)(2,1)}), bf16[8,16,512]{2,1,0:T(8,128)(2,1)S(1)}, u32[]{:S(2)}, u32[]{:S(2)}) async-start(bf16[8,16,512]{2,1,0:T(8,128)(2,1)} %bitcast.14), calls=%async_computation.2 | async-start | bytes 262144 | tf_op jit(solution)/shard_map/all_to_all | solution.py:43
Sparse Core Ops, SparseCore 0:
  10.6 59.5 all-gather.1

commit v2 on v1

v2 whole, which is shorter than its diff:
```python
import jax
import jax.numpy as jnp
from jax import lax
from jax.experimental.layout import Layout, with_layout_constraint
from jax.sharding import PartitionSpec as P

CORES = 2
LANES = 128
F32 = jnp.float32
BF16 = jnp.bfloat16


def expert_move(buffer):
    return lax.all_to_all(buffer, ("ctx", "tp"), split_axis=0, concat_axis=0, tiled=True)


def parts_of(values, count):
    parts = []
    for _ in range(count):
        part = lax.reduce_precision(values, 8, 7)
        parts.append(part.astype(BF16))
        values = values - part
    return parts


def placer_of(named, gates, experts, own, capacity, place_of):
    tokens = named.shape[0]
    groups = tokens // own
    shape = (experts, tokens)
    ids = lax.broadcasted_iota(jnp.int32, shape, 0).astype(F32)
    hit = named.T[:, None, :] == ids[None]
    names = jnp.any(hit, axis=0)
    gate_of = jnp.sum(jnp.where(hit, gates.T[:, None, :], 0.0), axis=0)
    at = lax.broadcasted_iota(jnp.int32, (tokens, tokens), 0)
    to = lax.broadcasted_iota(jnp.int32, (tokens, tokens), 1)
    earlier = jnp.logical_and(at // own == to // own, at < to).astype(BF16)
    rank = jnp.dot(names.astype(BF16), earlier, preferred_element_type=F32)
    group = place_of(lax.broadcasted_iota(jnp.int32, shape, 1) // own)
    code = jnp.where(names, group.astype(F32) * capacity + rank, -1.0)
    lines = capacity * groups
    place = code[:, None, :] == lax.broadcasted_iota(jnp.int32, (1, lines, tokens), 1).astype(F32)
    return jnp.concatenate(
        [jnp.where(place, p[:, None, :], jnp.zeros((), BF16)) for p in parts_of(gate_of, 2)], axis=2
    ).reshape(experts * lines, 2 * tokens)


def body(routed_experts, route_gates, expert_hidden, down_weight, output_grad):
    dp = lax.axis_size("dp")
    chips = dp // CORES
    experts = lax.axis_size("ctx") * lax.axis_size("tp")
    own, topk = routed_experts.shape
    capacity, depth = expert_hidden.shape[3:]
    width = output_grad.shape[1]
    half = width // dp
    part = half * CORES
    tokens = chips * own
    lines = chips * capacity
    held = capacity * experts
    column = [[z * CORES + c for z in range(chips)] for c in range(CORES)]
    swap = [(d, d ^ 1) for d in range(dp)]
    core = lax.axis_index("dp") & 1
    chip = lax.axis_index("dp") // CORES

    def shift(block, by):
        moved = lax.ppermute(block, "dp", [(d, (d + CORES * by) % dp) for d in range(dp)])
        return with_layout_constraint(moved, Layout((0, 1)))

    def chip_move(blocks):
        return lax.all_to_all(
            blocks, "dp", split_axis=0, concat_axis=0, tiled=True, axis_index_groups=column
        )

    def along(group):
        return (group + chips - chip) % chips

    def in_order(group):
        ahead = along(group)
        return jnp.where(
            ahead > chips // 2, 2 * (chips - ahead), jnp.maximum(2 * ahead - 1, 0)
        )

    named = routed_experts.astype(F32)
    blocks = jnp.swapaxes(output_grad.reshape(own, chips, part), 0, 1).reshape(tokens, part)
    placer = placer_of(
        jnp.tile(named, (chips, 1)), jnp.tile(route_gates, (chips, 1)), experts, own, capacity, along
    )
    outgoing = jnp.dot(placer, jnp.concatenate([blocks, blocks], axis=0), preferred_element_type=F32)
    outgoing = outgoing.astype(BF16).reshape(experts, lines, part)

    table = jnp.concatenate([named.astype(BF16), *parts_of(route_gates, 3)], axis=1)
    table = jnp.pad(table, ((0, 0), (0, depth - table.shape[1])))
    rows = jnp.swapaxes(expert_hidden[0, 0], 0, 1).reshape(held, depth)
    mine = with_layout_constraint(jnp.concatenate([rows, table], axis=0), Layout((0, 1)))
    order = [0]
    up = down = mine
    around = [mine]
    for step in range(1, chips // 2):
        up, down = shift(up, 1), shift(down, -1)
        if step == 1:
            up, down, _ = lax.optimization_barrier((up, down, outgoing))
        order += [step, chips - step]
        around += [down, up]
    middle = mine.shape[0] // 2
    order.append(chips // 2)
    around.append(jnp.concatenate([shift(up[:middle], 1), shift(down[middle:], -1)], axis=0))

    scaled = jnp.swapaxes(expert_move(outgoing), 0, 1)
    scaled = scaled.reshape(chips, held, part)

    weight = down_weight[0]
    other = lax.ppermute(weight, "dp", swap)
    weight = jnp.concatenate(
        [jnp.where(core == 0, weight, other), jnp.where(core == 0, other, weight)], axis=1
    )
    weight = lax.optimization_barrier(weight)
    early = chips // 2 + 1
    hidden = [
        jnp.concatenate([block[:held] for block in blocks], axis=0)
        for blocks in (around[:early], around[early:])
    ]
    produced = [jnp.dot(h, weight, preferred_element_type=F32).astype(BF16) for h in hidden]
    produced = jnp.concatenate([p.reshape(-1, experts, part) for p in produced], axis=0)
    tables = jnp.concatenate([block[held:, :LANES] for block in around], axis=0)
    produced, scaled, tables = lax.optimization_barrier(
        (jnp.swapaxes(produced, 0, 1), scaled, tables)
    )
    returned = expert_move(produced)

    wanted = lax.broadcasted_iota(jnp.int32, (tokens, tokens), 0)
    source = in_order(wanted // own) * own + wanted % own
    turn = (source == lax.broadcasted_iota(jnp.int32, (tokens, tokens), 1)).astype(BF16)
    tables = jnp.dot(turn, tables, preferred_element_type=F32)
    gates = sum(tables[:, topk * i : topk * (i + 1)] for i in (1, 2, 3))
    mixer = placer_of(tables[:, :topk], gates, experts, own, capacity, in_order)
    mixed = lax.dot_general(
        mixer,
        returned.reshape(experts * lines, part),
        (((0,), (0,)), ((), ())),
        preferred_element_type=F32,
    )
    mixed = (mixed[:tokens] + mixed[tokens:]).astype(BF16).reshape(chips, own, part)
    combined = jnp.swapaxes(chip_move(mixed), 0, 1).reshape(own, width)

    grad_rows = [scaled[0]] + [shift(scaled[(chips - i) % chips], -i) for i in order[1:]]
    gradient = sum(
        lax.dot_general(
            h, jnp.concatenate(g, axis=0), (((0,), (0,)), ((), ())), preferred_element_type=F32
        )
        for h, g in zip(hidden, (grad_rows[:early], grad_rows[early:]))
    )
    kept = lax.dynamic_slice_in_dim(gradient, core * half, half, 1)
    gradient = kept + lax.ppermute(
        lax.dynamic_slice_in_dim(gradient, (1 - core) * half, half, 1), "dp", swap
    )
    return (combined, gradient[None])


def solution(mesh):
    in_specs = (
        P(("dp", "ctx", "tp"), None),
        P(("dp", "ctx", "tp"), None),
        P(("ctx", "tp"), "dp", None, None, None),
        P(("ctx", "tp"), None, "dp"),
        P(("dp", "ctx", "tp"), None),
    )
    out_specs = (P(("dp", "ctx", "tp"), None), P(("ctx", "tp"), None, "dp"))
    return jax.shard_map(body, mesh=mesh, in_specs=in_specs, out_specs=out_specs, check_vma=False)
```

time: 166 us -> 162 us (0.976)
  the two profiles are of different devices: /device:TPU:16 before, /device:TPU:6 now
where the time goes in v2:
time: 162 us; the launch traced here: 160 us
  starting transfers between devices  101 us (62%)
  waiting for transfers between devices  34.1 us (21%)
  other arithmetic  8.76 us (5%)
  local copies, waits for them, and re-layouts  8.19 us (5%)
  matrix products  7.6 us (5%)
    ppermute x15, starting transfers between devices, shift(): lax.ppermute(block, 'dp', [(d, (d + CORES * by) % dp) for d in range(dp)])  63.9 us
    ppermute x15, waiting for transfers between devices, shift(): lax.ppermute(block, 'dp', [(d, (d + CORES * by) % dp) for d in range(dp)])  26.5 us
    all_to_all x2, starting transfers between devices, expert_move(): lax.all_to_all(buffer, ('ctx', 'tp'), split_axis=0, concat_axis=0, tiled=...  26.4 us
    all_to_all x1, waiting for transfers between devices, chip_move(): lax.all_to_all(blocks, 'dp', split_axis=0, concat_axis=0, tiled=True, axi...  7.57 us
    all_to_all x1, starting transfers between devices, chip_move(): lax.all_to_all(blocks, 'dp', split_axis=0, concat_axis=0, tiled=True, axi...  6.45 us
    unnamed x37, local copies, waits for them, and re-layouts  3.81 us
  transfers between devices with their start and end apart: 20, of which 10 were waited for; matrix products, arithmetic and copies ran while one was open for 12% of the time, Pallas kernels for 0%

profile of v2, /device:TPU:6, one launch (start us, length us, event | category | flops | bytes accessed | tf_op | source)
XLA Modules:
  0.0 160.5 jit_solution(2411737736830384761)
XLA Ops:
  4.0 5.2 %collective-permute-start = (bf16[208,768]{1,0:T(8,128)(2,1)S(1)}, bf16[208,768]{1,0:T(8,128)(2,1)S(1)}, u32[]{:S(2)}, u32[]{:S(2)}) collective-permute-start(bf16[208,768]{1,0:T(8,128)(2,1)S(1)} %pad_maximum_fusion.2), channel_id=1, source_target_pairs={{0,128},{64,192},{128,256},{192,320},{256,384},{320,448},{384,512}... | collective-permute-start | bytes 958472 | tf_op jit(solution)/shard_map/ppermute | solution.py:65
  9.2 14.0 %collective-permute-start.1 = (bf16[208,768]{1,0:T(8,128)(2,1)S(1)}, bf16[208,768]{1,0:T(8,128)(2,1)}, u32[]{:S(2)}, u32[]{:S(2)}) collective-permute-start(bf16[208,768]{1,0:T(8,128)(2,1)S(1)} %pad_maximum_fusion.2), channel_id=1, source_target_pairs={{0,896},{64,960},{128,0},{192,64},{256,128},{320,192},{384,256},{4... | collective-permute-start | bytes 958472 | tf_op jit(solution)/shard_map/ppermute | solution.py:65
  23.2 1.9 %collective-permute-start.4 = (bf16[768,256]{1,0:T(8,128)(2,1)}, bf16[768,256]{1,0:T(8,128)(2,1)S(1)}, u32[]{:S(2)}, u32[]{:S(2)}) collective-permute-start(bf16[768,256]{1,0:T(8,128)(2,1)} %bitcast.81), channel_id=1, source_target_pairs={{0,64},{64,0},{128,192},{192,128},{256,320},{320,256},{384,448},{4... | collective-permute-start | bytes 1179656 | tf_op jit(solution)/shard_map/ppermute | solution.py:111
  27.9 1.7 %convolution_convert_fusion = bf16[1536,512]{1,0:T(8,128)(2,1)} fusion(bf16[1536,128]{1,0:T(8,128)(2,1)S(1)} %get-tuple-element.24, bf16[1536,128]{1,0:T(8,128)(2,1)S(1)} %get-tuple-element.23, bf16[128,512]{1,0:T(8,128)(2,1)S(1)} %bitcast.83), kind=kOutput, calls=%fused_computation | convolution fusion | flops 405536768 | bytes 2490368 | tf_op jit(solution)/shard_map/dot_general | solution.py:87
  29.7 13.9 %all-to-all-start = ((bf16[64,24,512]{2,1,0:T(8,128)(2,1)}), bf16[64,24,512]{2,1,0:T(8,128)(2,1)S(1)}, u32[]{:S(2)}, u32[]{:S(2)}) async-start(bf16[64,24,512]{2,1,0:T(8,128)(2,1)} %bitcast.10), calls=%async_computation | async-start | bytes 3145728 | tf_op jit(solution)/shard_map/all_to_all | solution.py:14
  43.6 4.1 %collective-permute-start.2 = (bf16[208,768]{1,0:T(8,128)(2,1)}, bf16[208,768]{1,0:T(8,128)(2,1)S(1)}, u32[]{:S(2)}, u32[]{:S(2)}) collective-permute-start(bf16[208,768]{1,0:T(8,128)(2,1)} %collective-permute-done.1), channel_id=1, source_target_pairs={{0,896},{64,960},{128,0},{192,64},{256,128},{320,192},{384,256},{4... | collective-permute-start | bytes 958472 | tf_op jit(solution)/shard_map/ppermute | solution.py:65
  48.4 1.9 %collective-permute-start.3 = (bf16[208,768]{1,0:T(8,128)(2,1)S(1)}, bf16[208,768]{1,0:T(8,128)(2,1)S(1)}, u32[]{:S(2)}, u32[]{:S(2)}) collective-permute-start(bf16[208,768]{1,0:T(8,128)(2,1)S(1)} %collective-permute-done), channel_id=1, source_target_pairs={{0,128},{64,192},{128,256},{192,320},{256,384},{320,448},{384,512}... | collective-permute-start | bytes 958472 | tf_op jit(solution)/shard_map/ppermute | solution.py:65
  51.5 3.8 %collective-permute-done.2 = bf16[208,768]{1,0:T(8,128)(2,1)S(1)} collective-permute-done((bf16[208,768]{1,0:T(8,128)(2,1)}, bf16[208,768]{1,0:T(8,128)(2,1)S(1)}, u32[]{:S(2)}, u32[]{:S(2)}) %collective-permute-start.2) | collective-permute-done | bytes 319520 | tf_op jit(solution)/shard_map/ppermute | solution.py:65
  55.2 5.1 %collective-permute-start.5 = (bf16[208,768]{1,0:T(8,128)(2,1)S(1)}, bf16[208,768]{1,0:T(8,128)(2,1)S(1)}, u32[]{:S(2)}, u32[]{:S(2)}) collective-permute-start(bf16[208,768]{1,0:T(8,128)(2,1)S(1)} %collective-permute-done.2), channel_id=1, source_target_pairs={{0,896},{64,960},{128,0},{192,64},{256,128},{320,192},{384,256},{4... | collective-permute-start | bytes 958472 | tf_op jit(solution)/shard_map/ppermute | solution.py:65
  60.6 1.9 %collective-permute-start.6 = (bf16[208,768]{1,0:T(8,128)(2,1)S(1)}, bf16[208,768]{1,0:T(8,128)(2,1)S(1)}, u32[]{:S(2)}, u32[]{:S(2)}) collective-permute-start(bf16[208,768]{1,0:T(8,128)(2,1)S(1)} %collective-permute-done.3), channel_id=1, source_target_pairs={{0,128},{64,192},{128,256},{192,320},{256,384},{320,448},{384,512}... | collective-permute-start | bytes 958472 | tf_op jit(solution)/shard_map/ppermute | solution.py:65
  64.2 2.1 %collective-permute-done.5 = bf16[208,768]{1,0:T(8,128)(2,1)S(1)} collective-permute-done((bf16[208,768]{1,0:T(8,128)(2,1)S(1)}, bf16[208,768]{1,0:T(8,128)(2,1)S(1)}, u32[]{:S(2)}, u32[]{:S(2)}) %collective-permute-start.5) | collective-permute-done | bytes 319520 | tf_op jit(solution)/shard_map/ppermute | solution.py:65
  66.4 5.6 %collective-permute-start.8 = (bf16[104,768]{1,0:T(8,128)(2,1)S(1)}, bf16[104,768]{1,0:T(8,128)(2,1)S(1)}, u32[]{:S(2)}, u32[]{:S(2)}) collective-permute-start(bf16[104,768]{1,0:T(8,128)(2,1)S(1)} %slice.134), channel_id=1, source_target_pairs={{0,896},{64,960},{128,0},{192,64},{256,128},{320,192},{384,256},{4... | collective-permute-start | bytes 479240 | tf_op jit(solution)/shard_map/ppermute | solution.py:65
  72.0 1.9 %collective-permute-start.7 = (bf16[104,768]{1,0:T(8,128)(2,1)S(1)}, bf16[104,768]{1,0:T(8,128)(2,1)S(1)}, u32[]{:S(2)}, u32[]{:S(2)}) collective-permute-start(bf16[104,768]{1,0:T(8,128)(2,1)S(1)} %slice.133), channel_id=1, source_target_pairs={{0,128},{64,192},{128,256},{192,320},{256,384},{320,448},{384,512}... | collective-permute-start | bytes 479240 | tf_op jit(solution)/shard_map/ppermute | solution.py:65
  74.8 5.6 %collective-permute-done.7 = bf16[104,768]{1,0:T(8,128)(2,1)S(1)} collective-permute-done((bf16[104,768]{1,0:T(8,128)(2,1)S(1)}, bf16[104,768]{1,0:T(8,128)(2,1)S(1)}, u32[]{:S(2)}, u32[]{:S(2)}) %collective-permute-start.7) | collective-permute-done | bytes 159776 | tf_op jit(solution)/shard_map/ppermute | solution.py:65
  81.4 1.7 %maximum_bitcast_fusion = bf16[64,24,512]{2,1,0:T(8,128)(2,1)} fusion(bf16[9,64,512]{2,0,1:T(8,128)(2,1)S(1)} %copy.52, bf16[15,64,512]{2,0,1:T(8,128)(2,1)S(1)} %copy.51), kind=kLoop, calls=%fused_computation.1 | loop fusion | flops 3145728 | bytes 3145728 | tf_op jit(solution)/shard_map/transpose | solution.py:125
  83.7 12.5 %all-to-all-start.1 = ((bf16[64,24,512]{2,1,0:T(8,128)(2,1)}), bf16[64,24,512]{2,1,0:T(8,128)(2,1)S(1)}, u32[]{:S(2)}, u32[]{:S(2)}) async-start(bf16[64,24,512]{2,1,0:T(8,128)(2,1)} %maximum_bitcast_fusion), calls=%async_computation.1 | async-start | bytes 3145728 | tf_op jit(solution)/shard_map/all_to_all | solution.py:14
  96.4 2.1 %collective-permute-start.9 = (bf16[192,512]{1,0:T(8,128)(2,1)S(1)}, bf16[192,512]{1,0:T(8,128)(2,1)S(1)}, u32[]{:S(2)}, u32[]{:S(2)}) collective-permute-start(bf16[192,512]{1,0:T(8,128)(2,1)S(1)} %get-tuple-element.18), channel_id=1, source_target_pairs={{0,896},{64,960},{128,0},{192,64},{256,128},{320,192},{384,256},{4... | collective-permute-start | bytes 589832 | tf_op jit(solution)/shard_map/ppermute | solution.py:65
  98.5 3.9 %collective-permute-start.10 = (bf16[192,512]{1,0:T(8,128)(2,1)S(1)}, bf16[192,512]{1,0:T(8,128)(2,1)S(1)}, u32[]{:S(2)}, u32[]{:S(2)}) collective-permute-start(bf16[192,512]{1,0:T(8,128)(2,1)S(1)} %get-tuple-element.17), channel_id=1, source_target_pairs={{0,128},{64,192},{128,256},{192,320},{256,384},{320,448},{384,512}... | collective-permute-start | bytes 589832 | tf_op jit(solution)/shard_map/ppermute | solution.py:65
  102.4 1.9 %collective-permute-start.11 = (bf16[192,512]{1,0:T(8,128)(2,1)S(1)}, bf16[192,512]{1,0:T(8,128)(2,1)S(1)}, u32[]{:S(2)}, u32[]{:S(2)}) collective-permute-start(bf16[192,512]{1,0:T(8,128)(2,1)S(1)} %get-tuple-element.16), channel_id=1, source_target_pairs={{0,768},{64,832},{128,896},{192,960},{256,0},{320,64},{384,128},{4... | collective-permute-start | bytes 589832 | tf_op jit(solution)/shard_map/ppermute | solution.py:65
  104.3 4.8 %collective-permute-start.12 = (bf16[192,512]{1,0:T(8,128)(2,1)S(1)}, bf16[192,512]{1,0:T(8,128)(2,1)S(1)}, u32[]{:S(2)}, u32[]{:S(2)}) collective-permute-start(bf16[192,512]{1,0:T(8,128)(2,1)S(1)} %get-tuple-element.12), channel_id=1, source_target_pairs={{0,256},{64,320},{128,384},{192,448},{256,512},{320,576},{384,640}... | collective-permute-start | bytes 589832 | tf_op jit(solution)/shard_map/ppermute | solution.py:65
  109.2 2.6 %collective-permute-start.13 = (bf16[192,512]{1,0:T(8,128)(2,1)S(1)}, bf16[192,512]{1,0:T(8,128)(2,1)S(1)}, u32[]{:S(2)}, u32[]{:S(2)}) collective-permute-start(bf16[192,512]{1,0:T(8,128)(2,1)S(1)} %get-tuple-element.15), channel_id=1, source_target_pairs={{0,640},{64,704},{128,768},{192,832},{256,896},{320,960},{384,0},{... | collective-permute-start | bytes 589832 | tf_op jit(solution)/shard_map/ppermute | solution.py:65
  112.4 5.1 %collective-permute-start.14 = (bf16[192,512]{1,0:T(8,128)(2,1)S(1)}, bf16[192,512]{1,0:T(8,128)(2,1)S(1)}, u32[]{:S(2)}, u32[]{:S(2)}) collective-permute-start(bf16[192,512]{1,0:T(8,128)(2,1)S(1)} %get-tuple-element.14), channel_id=1, source_target_pairs={{0,384},{64,448},{128,512},{192,576},{256,640},{320,704},{384,768}... | collective-permute-start | bytes 589832 | tf_op jit(solution)/shard_map/ppermute | solution.py:65
  117.5 3.8 %collective-permute-start.15 = (bf16[192,512]{1,0:T(8,128)(2,1)S(1)}, bf16[192,512]{1,0:T(8,128)(2,1)S(1)}, u32[]{:S(2)}, u32[]{:S(2)}) collective-permute-start(bf16[192,512]{1,0:T(8,128)(2,1)S(1)} %get-tuple-element.13), channel_id=1, source_target_pairs={{0,512},{64,576},{128,640},{192,704},{256,768},{320,832},{384,896}... | collective-permute-start | bytes 589832 | tf_op jit(solution)/shard_map/ppermute | solution.py:65
  121.4 6.1 %collective-permute-done.13 = bf16[192,512]{1,0:T(8,128)(2,1)S(1)} collective-permute-done((bf16[192,512]{1,0:T(8,128)(2,1)S(1)}, bf16[192,512]{1,0:T(8,128)(2,1)S(1)}, u32[]{:S(2)}, u32[]{:S(2)}) %collective-permute-start.13) | collective-permute-done | bytes 196640 | tf_op jit(solution)/shard_map/ppermute | solution.py:65
  127.4 5.8 %collective-permute-done.14 = bf16[192,512]{1,0:T(8,128)(2,1)S(1)} collective-permute-done((bf16[192,512]{1,0:T(8,128)(2,1)S(1)}, bf16[192,512]{1,0:T(8,128)(2,1)S(1)}, u32[]{:S(2)}, u32[]{:S(2)}) %collective-permute-start.14) | collective-permute-done | bytes 196640 | tf_op jit(solution)/shard_map/ppermute | solution.py:65
  133.2 2.1 %collective-permute-done.15 = bf16[192,512]{1,0:T(8,128)(2,1)S(1)} collective-permute-done((bf16[192,512]{1,0:T(8,128)(2,1)S(1)}, bf16[192,512]{1,0:T(8,128)(2,1)S(1)}, u32[]{:S(2)}, u32[]{:S(2)}) %collective-permute-start.15) | collective-permute-done | bytes 196640 | tf_op jit(solution)/shard_map/ppermute | solution.py:65
  136.2 1.0 convolution_add_fusion
  138.1 1.9 %collective-permute-start.16 = (f32[768,256]{1,0:T(8,128)}, f32[768,256]{1,0:T(8,128)}, u32[]{:S(2)}, u32[]{:S(2)}) collective-permute-start(f32[768,256]{1,0:T(8,128)} %constant_dynamic-slice_fusion), channel_id=1, source_target_pairs={{0,64},{64,0},{128,192},{192,128},{256,320},{320,256},{384,448},{4... | collective-permute-start | bytes 2359304 | tf_op jit(solution)/shard_map/ppermute | solution.py:152
  141.2 1.7 %fusion.2 = f32[256,512]{1,0:T(8,128)S(1)} fusion(bf16[64,24,512]{2,1,0:T(8,128)(2,1)S(1)} %all-to-all-done.1, bf16[64,24,128]{2,0,1:T(8,128)(2,1)} %get-tuple-element.26, bf16[64,24,128]{2,0,1:T(8,128)(2,1)S(1)} %get-tuple-element.25), kind=kOutput, calls=%fused_computation.7 | convolution fusion | flops 404226048 | bytes 2883584 | tf_op jit(solution)/shard_map/dot_general | solution.py:135
  143.6 6.4 %all-to-all-start.2 = ((bf16[8,16,512]{2,1,0:T(8,128)(2,1)}), bf16[8,16,512]{2,1,0:T(8,128)(2,1)S(1)}, u32[]{:S(2)}, u32[]{:S(2)}) async-start(bf16[8,16,512]{2,1,0:T(8,128)(2,1)} %bitcast.20), calls=%async_computation.2 | async-start | bytes 262144 | tf_op jit(solution)/shard_map/all_to_all | solution.py:69
  150.1 2.2 %add_bitcast_fusion = f32[1,768,256]{2,1,0:T(8,128)} fusion(f32[768,256]{1,0:T(8,128)} %collective-permute-done.16, f32[768,512]{1,0:T(8,128)S(1)} %convolution_add_fusion, s32[]{:T(128)S(6)} %select_n.119), kind=kLoop, calls=%fused_computation.26 | loop fusion | flops 196608 | bytes 2359300 | tf_op jit(solution)/shard_map/broadcast_in_dim | solution.py:155
  152.3 7.6 %all-to-all-done.2 = bf16[8,16,512]{2,1,0:T(8,128)(2,1)S(1)} async-done(((bf16[8,16,512]{2,1,0:T(8,128)(2,1)}), bf16[8,16,512]{2,1,0:T(8,128)(2,1)S(1)}, u32[]{:S(2)}, u32[]{:S(2)}) %all-to-all-start.2) | async-done | bytes 131104 | tf_op jit(solution)/shard_map/all_to_all | solution.py:69
  (100 shorter events, 17.3 us)
Async XLA Ops:
  4.0 39.6 %collective-permute-start = (bf16[208,768]{1,0:T(8,128)(2,1)S(1)}, bf16[208,768]{1,0:T(8,128)(2,1)S(1)}, u32[]{:S(2)}, u32[]{:S(2)}) collective-permute-start(bf16[208,768]{1,0:T(8,128)(2,1)S(1)} %pad_maximum_fusion.2), channel_id=1, source_target_pairs={{0,128},{64,192},{128,256},{192,320},{256,384},{320,448},{384,512}... | collective-permute-start | bytes 958472 | tf_op jit(solution)/shard_map/ppermute | solution.py:65
  9.2 34.4 %collective-permute-start.1 = (bf16[208,768]{1,0:T(8,128)(2,1)S(1)}, bf16[208,768]{1,0:T(8,128)(2,1)}, u32[]{:S(2)}, u32[]{:S(2)}) collective-permute-start(bf16[208,768]{1,0:T(8,128)(2,1)S(1)} %pad_maximum_fusion.2), channel_id=1, source_target_pairs={{0,896},{64,960},{128,0},{192,64},{256,128},{320,192},{384,256},{4... | collective-permute-start | bytes 958472 | tf_op jit(solution)/shard_map/ppermute | solution.py:65
  23.2 28.1 %collective-permute-start.4 = (bf16[768,256]{1,0:T(8,128)(2,1)}, bf16[768,256]{1,0:T(8,128)(2,1)S(1)}, u32[]{:S(2)}, u32[]{:S(2)}) collective-permute-start(bf16[768,256]{1,0:T(8,128)(2,1)} %bitcast.81), channel_id=1, source_target_pairs={{0,64},{64,0},{128,192},{192,128},{256,320},{320,256},{384,448},{4... | collective-permute-start | bytes 1179656 | tf_op jit(solution)/shard_map/ppermute | solution.py:111
  29.7 13.9 %copy-start = (bf16[1,1,64,3,768]{4,2,3,1,0:T(8,128)(2,1)S(1)}, bf16[1,1,64,3,768]{4,2,3,1,0:T(8,128)(2,1)}, u32[]{:S(2)}) copy-start(bf16[1,1,64,3,768]{4,2,3,1,0:T(8,128)(2,1)} %param.7) | copy-start | bytes 884740
  29.7 53.6 %all-to-all-start = ((bf16[64,24,512]{2,1,0:T(8,128)(2,1)}), bf16[64,24,512]{2,1,0:T(8,128)(2,1)S(1)}, u32[]{:S(2)}, u32[]{:S(2)}) async-start(bf16[64,24,512]{2,1,0:T(8,128)(2,1)} %bitcast.10), calls=%async_computation | async-start | bytes 3145728 | tf_op jit(solution)/shard_map/all_to_all | solution.py:14
  43.5 7.8 %copy-start.1 = (bf16[1,768,256]{2,1,0:T(8,128)(2,1)S(1)}, bf16[1,768,256]{2,1,0:T(8,128)(2,1)}, u32[]{:S(2)}) copy-start(bf16[1,768,256]{2,1,0:T(8,128)(2,1)} %param.8) | copy-start | bytes 1179652
  43.6 11.6 %collective-permute-start.2 = (bf16[208,768]{1,0:T(8,128)(2,1)}, bf16[208,768]{1,0:T(8,128)(2,1)S(1)}, u32[]{:S(2)}, u32[]{:S(2)}) collective-permute-start(bf16[208,768]{1,0:T(8,128)(2,1)} %collective-permute-done.1), channel_id=1, source_target_pairs={{0,896},{64,960},{128,0},{192,64},{256,128},{320,192},{384,256},{4... | collective-permute-start | bytes 958472 | tf_op jit(solution)/shard_map/ppermute | solution.py:65
  48.4 12.2 %collective-permute-start.3 = (bf16[208,768]{1,0:T(8,128)(2,1)S(1)}, bf16[208,768]{1,0:T(8,128)(2,1)S(1)}, u32[]{:S(2)}, u32[]{:S(2)}) collective-permute-start(bf16[208,768]{1,0:T(8,128)(2,1)S(1)} %collective-permute-done), channel_id=1, source_target_pairs={{0,128},{64,192},{128,256},{192,320},{256,384},{320,448},{384,512}... | collective-permute-start | bytes 958472 | tf_op jit(solution)/shard_map/ppermute | solution.py:65
  55.2 11.1 %collective-permute-start.5 = (bf16[208,768]{1,0:T(8,128)(2,1)S(1)}, bf16[208,768]{1,0:T(8,128)(2,1)S(1)}, u32[]{:S(2)}, u32[]{:S(2)}) collective-permute-start(bf16[208,768]{1,0:T(8,128)(2,1)S(1)} %collective-permute-done.2), channel_id=1, source_target_pairs={{0,896},{64,960},{128,0},{192,64},{256,128},{320,192},{384,256},{4... | collective-permute-start | bytes 958472 | tf_op jit(solution)/shard_map/ppermute | solution.py:65
  60.6 11.4 %collective-permute-start.6 = (bf16[208,768]{1,0:T(8,128)(2,1)S(1)}, bf16[208,768]{1,0:T(8,128)(2,1)S(1)}, u32[]{:S(2)}, u32[]{:S(2)}) collective-permute-start(bf16[208,768]{1,0:T(8,128)(2,1)S(1)} %collective-permute-done.3), channel_id=1, source_target_pairs={{0,128},{64,192},{128,256},{192,320},{256,384},{320,448},{384,512}... | collective-permute-start | bytes 958472 | tf_op jit(solution)/shard_map/ppermute | solution.py:65
  62.5 1.1 copy-start.4
  66.4 8.4 %collective-permute-start.8 = (bf16[104,768]{1,0:T(8,128)(2,1)S(1)}, bf16[104,768]{1,0:T(8,128)(2,1)S(1)}, u32[]{:S(2)}, u32[]{:S(2)}) collective-permute-start(bf16[104,768]{1,0:T(8,128)(2,1)S(1)} %slice.134), channel_id=1, source_target_pairs={{0,896},{64,960},{128,0},{192,64},{256,128},{320,192},{384,256},{4... | collective-permute-start | bytes 479240 | tf_op jit(solution)/shard_map/ppermute | solution.py:65
  72.0 8.4 %collective-permute-start.7 = (bf16[104,768]{1,0:T(8,128)(2,1)S(1)}, bf16[104,768]{1,0:T(8,128)(2,1)S(1)}, u32[]{:S(2)}, u32[]{:S(2)}) collective-permute-start(bf16[104,768]{1,0:T(8,128)(2,1)S(1)} %slice.133), channel_id=1, source_target_pairs={{0,128},{64,192},{128,256},{192,320},{256,384},{320,448},{384,512}... | collective-permute-start | bytes 479240 | tf_op jit(solution)/shard_map/ppermute | solution.py:65
  74.0 7.0 %copy-start.2 = (bf16[192,768]{1,0:T(8,128)(2,1)}, bf16[192,768]{1,0:T(8,128)(2,1)S(1)}, u32[]{:S(2)}) copy-start(bf16[192,768]{1,0:T(8,128)(2,1)S(1)} %slice.132) | copy-start | bytes 884740
  74.8 8.4 %copy-start.6 = (bf16[104,768]{1,0:T(8,128)(2,1)}, bf16[104,768]{1,0:T(8,128)(2,1)S(1)}, u32[]{:S(2)}) copy-start(bf16[104,768]{1,0:T(8,128)(2,1)S(1)} %collective-permute-done.8) | copy-start | bytes 479236
  80.4 0.7 copy-start.8
  83.7 57.5 %all-to-all-start.1 = ((bf16[64,24,512]{2,1,0:T(8,128)(2,1)}), bf16[64,24,512]{2,1,0:T(8,128)(2,1)S(1)}, u32[]{:S(2)}, u32[]{:S(2)}) async-start(bf16[64,24,512]{2,1,0:T(8,128)(2,1)} %maximum_bitcast_fusion), calls=%async_computation.1 | async-start | bytes 3145728 | tf_op jit(solution)/shard_map/all_to_all | solution.py:14
  96.4 39.0 %copy-start.3 = (bf16[192,768]{1,0:T(8,128)(2,1)S(1)}, bf16[192,768]{1,0:T(8,128)(2,1)}, u32[]{:S(2)}) copy-start(bf16[192,768]{1,0:T(8,128)(2,1)} %copy-done.2) | copy-start | bytes 884740
  96.4 38.9 %copy-start.7 = (bf16[104,768]{1,0:T(8,128)(2,1)S(1)}, bf16[104,768]{1,0:T(8,128)(2,1)}, u32[]{:S(2)}) copy-start(bf16[104,768]{1,0:T(8,128)(2,1)} %copy-done.6) | copy-start | bytes 479236
  96.4 38.9 %copy-start.9 = (bf16[104,768]{1,0:T(8,128)(2,1)S(1)}, bf16[104,768]{1,0:T(8,128)(2,1)}, u32[]{:S(2)}) copy-start(bf16[104,768]{1,0:T(8,128)(2,1)} %copy-done.8) | copy-start | bytes 479236
  96.4 15.9 %collective-permute-start.9 = (bf16[192,512]{1,0:T(8,128)(2,1)S(1)}, bf16[192,512]{1,0:T(8,128)(2,1)S(1)}, u32[]{:S(2)}, u32[]{:S(2)}) collective-permute-start(bf16[192,512]{1,0:T(8,128)(2,1)S(1)} %get-tuple-element.18), channel_id=1, source_target_pairs={{0,896},{64,960},{128,0},{192,64},{256,128},{320,192},{384,256},{4... | collective-permute-start | bytes 589832 | tf_op jit(solution)/shard_map/ppermute | solution.py:65
  98.5 19.0 %collective-permute-start.10 = (bf16[192,512]{1,0:T(8,128)(2,1)S(1)}, bf16[192,512]{1,0:T(8,128)(2,1)S(1)}, u32[]{:S(2)}, u32[]{:S(2)}) collective-permute-start(bf16[192,512]{1,0:T(8,128)(2,1)S(1)} %get-tuple-element.17), channel_id=1, source_target_pairs={{0,128},{64,192},{128,256},{192,320},{256,384},{320,448},{384,512}... | collective-permute-start | bytes 589832 | tf_op jit(solution)/shard_map/ppermute | solution.py:65
  102.4 18.9 %collective-permute-start.11 = (bf16[192,512]{1,0:T(8,128)(2,1)S(1)}, bf16[192,512]{1,0:T(8,128)(2,1)S(1)}, u32[]{:S(2)}, u32[]{:S(2)}) collective-permute-start(bf16[192,512]{1,0:T(8,128)(2,1)S(1)} %get-tuple-element.16), channel_id=1, source_target_pairs={{0,768},{64,832},{128,896},{192,960},{256,0},{320,64},{384,128},{4... | collective-permute-start | bytes 589832 | tf_op jit(solution)/shard_map/ppermute | solution.py:65
  104.3 17.0 %collective-permute-start.12 = (bf16[192,512]{1,0:T(8,128)(2,1)S(1)}, bf16[192,512]{1,0:T(8,128)(2,1)S(1)}, u32[]{:S(2)}, u32[]{:S(2)}) collective-permute-start(bf16[192,512]{1,0:T(8,128)(2,1)S(1)} %get-tuple-element.12), channel_id=1, source_target_pairs={{0,256},{64,320},{128,384},{192,448},{256,512},{320,576},{384,640}... | collective-permute-start | bytes 589832 | tf_op jit(solution)/shard_map/ppermute | solution.py:65
  109.2 18.3 %collective-permute-start.13 = (bf16[192,512]{1,0:T(8,128)(2,1)S(1)}, bf16[192,512]{1,0:T(8,128)(2,1)S(1)}, u32[]{:S(2)}, u32[]{:S(2)}) collective-permute-start(bf16[192,512]{1,0:T(8,128)(2,1)S(1)} %get-tuple-element.15), channel_id=1, source_target_pairs={{0,640},{64,704},{128,768},{192,832},{256,896},{320,960},{384,0},{... | collective-permute-start | bytes 589832 | tf_op jit(solution)/shard_map/ppermute | solution.py:65
  112.4 20.9 %collective-permute-start.14 = (bf16[192,512]{1,0:T(8,128)(2,1)S(1)}, bf16[192,512]{1,0:T(8,128)(2,1)S(1)}, u32[]{:S(2)}, u32[]{:S(2)}) collective-permute-start(bf16[192,512]{1,0:T(8,128)(2,1)S(1)} %get-tuple-element.14), channel_id=1, source_target_pairs={{0,384},{64,448},{128,512},{192,576},{256,640},{320,704},{384,768}... | collective-permute-start | bytes 589832 | tf_op jit(solution)/shard_map/ppermute | solution.py:65
  117.5 17.9 %collective-permute-start.15 = (bf16[192,512]{1,0:T(8,128)(2,1)S(1)}, bf16[192,512]{1,0:T(8,128)(2,1)S(1)}, u32[]{:S(2)}, u32[]{:S(2)}) collective-permute-start(bf16[192,512]{1,0:T(8,128)(2,1)S(1)} %get-tuple-element.13), channel_id=1, source_target_pairs={{0,512},{64,576},{128,640},{192,704},{256,768},{320,832},{384,896}... | collective-permute-start | bytes 589832 | tf_op jit(solution)/shard_map/ppermute | solution.py:65
  121.3 14.8 %copy-start.5 = (bf16[960,768]{1,0:T(8,128)(2,1)S(1)}, bf16[960,768]{1,0:T(8,128)(2,1)}, u32[]{:S(2)}) copy-start(bf16[960,768]{1,0:T(8,128)(2,1)} %copy-done.4) | copy-start | bytes 4423684
  138.1 12.0 %collective-permute-start.16 = (f32[768,256]{1,0:T(8,128)}, f32[768,256]{1,0:T(8,128)}, u32[]{:S(2)}, u32[]{:S(2)}) collective-permute-start(f32[768,256]{1,0:T(8,128)} %constant_dynamic-slice_fusion), channel_id=1, source_target_pairs={{0,64},{64,0},{128,192},{192,128},{256,320},{320,256},{384,448},{4... | collective-permute-start | bytes 2359304 | tf_op jit(solution)/shard_map/ppermute | solution.py:152
  143.6 16.2 %all-to-all-start.2 = ((bf16[8,16,512]{2,1,0:T(8,128)(2,1)}), bf16[8,16,512]{2,1,0:T(8,128)(2,1)S(1)}, u32[]{:S(2)}, u32[]{:S(2)}) async-start(bf16[8,16,512]{2,1,0:T(8,128)(2,1)} %bitcast.20), calls=%async_computation.2 | async-start | bytes 262144 | tf_op jit(solution)/shard_map/all_to_all | solution.py:69

commit v3 on v2

--- a/solution.py
+++ b/solution.py
@@ -3,6 +3,7 @@
 from jax import lax
 from jax.experimental.layout import Layout, with_layout_constraint
 from jax.sharding import PartitionSpec as P
+
 
 CORES = 2
 LANES = 128
@@ -44,7 +45,7 @@
     ).reshape(experts * lines, 2 * tokens)
 
 
-def body(routed_experts, route_gates, expert_hidden, down_weight, output_grad):
+def layer(routed_experts, route_gates, expert_hidden, down_weight, output_grad):
     dp = lax.axis_size("dp")
     chips = dp // CORES
     experts = lax.axis_size("ctx") * lax.axis_size("tp")
@@ -80,6 +81,7 @@
         )
 
     named = routed_experts.astype(F32)
+
     blocks = jnp.swapaxes(output_grad.reshape(own, chips, part), 0, 1).reshape(tokens, part)
     placer = placer_of(
         jnp.tile(named, (chips, 1)), jnp.tile(route_gates, (chips, 1)), experts, own, capacity, along
@@ -96,15 +98,14 @@
     around = [mine]
     for step in range(1, chips // 2):
         up, down = shift(up, 1), shift(down, -1)
-        if step == 1:
-            up, down, _ = lax.optimization_barrier((up, down, outgoing))
         order += [step, chips - step]
         around += [down, up]
     middle = mine.shape[0] // 2
     order.append(chips // 2)
     around.append(jnp.concatenate([shift(up[:middle], 1), shift(down[middle:], -1)], axis=0))
 
-    scaled = jnp.swapaxes(expert_move(outgoing), 0, 1)
+    scaled = expert_move(outgoing)
+    scaled = jnp.swapaxes(scaled, 0, 1)
     scaled = scaled.reshape(chips, held, part)
 
     weight = down_weight[0]
@@ -139,9 +140,11 @@
         preferred_element_type=F32,
     )
     mixed = (mixed[:tokens] + mixed[tokens:]).astype(BF16).reshape(chips, own, part)
-    combined = jnp.swapaxes(chip_move(mixed), 0, 1).reshape(own, width)
+    combined = chip_move(mixed)
+    combined = jnp.swapaxes(combined, 0, 1).reshape(own, width)
 
     grad_rows = [scaled[0]] + [shift(scaled[(chips - i) % chips], -i) for i in order[1:]]
+    hidden, _ = lax.optimization_barrier((hidden, mixed))
     gradient = sum(
         lax.dot_general(
             h, jnp.concatenate(g, axis=0), (((0,), (0,)), ((), ())), preferred_element_type=F32
@@ -149,9 +152,8 @@
         for h, g in zip(hidden, (grad_rows[:early], grad_rows[early:]))
     )
     kept = lax.dynamic_slice_in_dim(gradient, core * half, half, 1)
-    gradient = kept + lax.ppermute(
-        lax.dynamic_slice_in_dim(gradient, (1 - core) * half, half, 1), "dp", swap
-    )
+    given = lax.dynamic_slice_in_dim(gradient, (1 - core) * half, half, 1)
+    gradient = kept + lax.ppermute(given, "dp", swap)
     return (combined, gradient[None])
 
 
@@ -164,4 +166,4 @@
         P(("dp", "ctx", "tp"), None),
     )
     out_specs = (P(("dp", "ctx", "tp"), None), P(("ctx", "tp"), None, "dp"))
-    return jax.shard_map(body, mesh=mesh, in_specs=in_specs, out_specs=out_specs, check_vma=False)
+    return jax.shard_map(layer, mesh=mesh, in_specs=in_specs, out_specs=out_specs, check_vma=False)

time: 162 us -> 173 us (1.068)
  the two profiles are of different devices: /device:TPU:6 before, /device:TPU:1 now
where the time goes in v3:
time: 173 us; the launch traced here: 172 us
  starting transfers between devices  96.6 us (56%)
  waiting for transfers between devices  45.6 us (26%)
  local copies, waits for them, and re-layouts  11.7 us (7%)
  matrix products  8.8 us (5%)
  other arithmetic  7.72 us (4%)
    ppermute x15, starting transfers between devices, shift(): lax.ppermute(block, 'dp', [(d, (d + CORES * by) % dp) for d in range(dp)])  64.4 us
    ppermute x15, waiting for transfers between devices, shift(): lax.ppermute(block, 'dp', [(d, (d + CORES * by) % dp) for d in range(dp)])  32.3 us
    all_to_all x2, starting transfers between devices, expert_move(): lax.all_to_all(buffer, ('ctx', 'tp'), split_axis=0, concat_axis=0, tiled=...  20.2 us
    all_to_all x1, waiting for transfers between devices, chip_move(): lax.all_to_all(blocks, 'dp', split_axis=0, concat_axis=0, tiled=True, axi...  8.46 us
    unnamed x31, local copies, waits for them, and re-layouts  6.78 us
    all_to_all x1, starting transfers between devices, chip_move(): lax.all_to_all(blocks, 'dp', split_axis=0, concat_axis=0, tiled=True, axi...  6.03 us
    all_to_all x2, waiting for transfers between devices, expert_move(): lax.all_to_all(buffer, ('ctx', 'tp'), split_axis=0, concat_axis=0, tiled=...  4.81 us
    dot_general x2, matrix products, layer(): lax.dot_general(h, jnp.concatenate(g, axis=0), (((0,), (0,)), ((), ())),...  4.03 us
  transfers between devices with their start and end apart: 20, of which 9 were waited for; matrix products, arithmetic and copies ran while one was open for 11% of the time, Pallas kernels for 0%

profile of v3, /device:TPU:1, one launch (start us, length us, event | category | flops | bytes accessed | tf_op | source)
XLA Modules:
  0.0 171.6 jit_solution(10809073055863488536)
XLA Ops:
  4.0 5.7 %collective-permute-start.1 = (bf16[208,768]{1,0:T(8,128)(2,1)S(1)}, bf16[208,768]{1,0:T(8,128)(2,1)}, u32[]{:S(2)}, u32[]{:S(2)}) collective-permute-start(bf16[208,768]{1,0:T(8,128)(2,1)S(1)} %pad_maximum_fusion.2), channel_id=1, source_target_pairs={{0,128},{64,192},{128,256},{192,320},{256,384},{320,448},{384,512}... | collective-permute-start | bytes 958472 | tf_op jit(solution)/shard_map/ppermute | solution.py:66
  9.7 14.0 %collective-permute-start = (bf16[208,768]{1,0:T(8,128)(2,1)S(1)}, bf16[208,768]{1,0:T(8,128)(2,1)S(1)}, u32[]{:S(2)}, u32[]{:S(2)}) collective-permute-start(bf16[208,768]{1,0:T(8,128)(2,1)S(1)} %pad_maximum_fusion.2), channel_id=1, source_target_pairs={{0,896},{64,960},{128,0},{192,64},{256,128},{320,192},{384,256},{4... | collective-permute-start | bytes 958472 | tf_op jit(solution)/shard_map/ppermute | solution.py:66
  23.8 3.3 %collective-permute-start.4 = (bf16[768,256]{1,0:T(8,128)(2,1)}, bf16[768,256]{1,0:T(8,128)(2,1)S(1)}, u32[]{:S(2)}, u32[]{:S(2)}) collective-permute-start(bf16[768,256]{1,0:T(8,128)(2,1)} %bitcast.83), channel_id=1, source_target_pairs={{0,64},{64,0},{128,192},{192,128},{256,320},{320,256},{384,448},{4... | collective-permute-start | bytes 1179656 | tf_op jit(solution)/shard_map/ppermute | solution.py:112
  29.9 1.7 %convolution_convert_fusion = bf16[1536,512]{1,0:T(8,128)(2,1)} fusion(bf16[1536,128]{1,0:T(8,128)(2,1)S(1)} %get-tuple-element.24, bf16[1536,128]{1,0:T(8,128)(2,1)S(1)} %get-tuple-element.23, bf16[128,512]{1,0:T(8,128)(2,1)S(1)} %bitcast.85), kind=kOutput, calls=%fused_computation | convolution fusion | flops 405536768 | bytes 2490368 | tf_op jit(solution)/shard_map/dot_general | solution.py:89
  31.6 12.9 %all-to-all-start = ((bf16[64,24,512]{2,1,0:T(8,128)(2,1)}), bf16[64,24,512]{2,1,0:T(8,128)(2,1)S(1)}, u32[]{:S(2)}, u32[]{:S(2)}) async-start(bf16[64,24,512]{2,1,0:T(8,128)(2,1)} %bitcast.14), calls=%async_computation | async-start | bytes 3145728 | tf_op jit(solution)/shard_map/all_to_all | solution.py:15
  44.6 2.1 %collective-permute-start.3 = (bf16[208,768]{1,0:T(8,128)(2,1)}, bf16[208,768]{1,0:T(8,128)(2,1)S(1)}, u32[]{:S(2)}, u32[]{:S(2)}) collective-permute-start(bf16[208,768]{1,0:T(8,128)(2,1)} %collective-permute-done.1), channel_id=1, source_target_pairs={{0,128},{64,192},{128,256},{192,320},{256,384},{320,448},{384,512}... | collective-permute-start | bytes 958472 | tf_op jit(solution)/shard_map/ppermute | solution.py:66
  46.6 4.6 %collective-permute-start.2 = (bf16[208,768]{1,0:T(8,128)(2,1)S(1)}, bf16[208,768]{1,0:T(8,128)(2,1)S(1)}, u32[]{:S(2)}, u32[]{:S(2)}) collective-permute-start(bf16[208,768]{1,0:T(8,128)(2,1)S(1)} %collective-permute-done), channel_id=1, source_target_pairs={{0,896},{64,960},{128,0},{192,64},{256,128},{320,192},{384,256},{4... | collective-permute-start | bytes 958472 | tf_op jit(solution)/shard_map/ppermute | solution.py:66
  53.1 3.8 %collective-permute-done.3 = bf16[208,768]{1,0:T(8,128)(2,1)S(1)} collective-permute-done((bf16[208,768]{1,0:T(8,128)(2,1)}, bf16[208,768]{1,0:T(8,128)(2,1)S(1)}, u32[]{:S(2)}, u32[]{:S(2)}) %collective-permute-start.3) | collective-permute-done | bytes 319520 | tf_op jit(solution)/shard_map/ppermute | solution.py:66
  56.8 1.9 %collective-permute-start.6 = (bf16[208,768]{1,0:T(8,128)(2,1)S(1)}, bf16[208,768]{1,0:T(8,128)(2,1)S(1)}, u32[]{:S(2)}, u32[]{:S(2)}) collective-permute-start(bf16[208,768]{1,0:T(8,128)(2,1)S(1)} %collective-permute-done.3), channel_id=1, source_target_pairs={{0,128},{64,192},{128,256},{192,320},{256,384},{320,448},{384,512}... | collective-permute-start | bytes 958472 | tf_op jit(solution)/shard_map/ppermute | solution.py:66
  58.7 4.6 %collective-permute-start.5 = (bf16[208,768]{1,0:T(8,128)(2,1)S(1)}, bf16[208,768]{1,0:T(8,128)(2,1)S(1)}, u32[]{:S(2)}, u32[]{:S(2)}) collective-permute-start(bf16[208,768]{1,0:T(8,128)(2,1)S(1)} %collective-permute-done.2), channel_id=1, source_target_pairs={{0,896},{64,960},{128,0},{192,64},{256,128},{320,192},{384,256},{4... | collective-permute-start | bytes 958472 | tf_op jit(solution)/shard_map/ppermute | solution.py:66
  65.1 2.8 %collective-permute-done.6 = bf16[208,768]{1,0:T(8,128)(2,1)S(1)} collective-permute-done((bf16[208,768]{1,0:T(8,128)(2,1)S(1)}, bf16[208,768]{1,0:T(8,128)(2,1)S(1)}, u32[]{:S(2)}, u32[]{:S(2)}) %collective-permute-start.6) | collective-permute-done | bytes 319520 | tf_op jit(solution)/shard_map/ppermute | solution.py:66
  67.9 1.9 %collective-permute-start.7 = (bf16[104,768]{1,0:T(8,128)(2,1)S(1)}, bf16[104,768]{1,0:T(8,128)(2,1)S(1)}, u32[]{:S(2)}, u32[]{:S(2)}) collective-permute-start(bf16[104,768]{1,0:T(8,128)(2,1)S(1)} %slice.135), channel_id=1, source_target_pairs={{0,128},{64,192},{128,256},{192,320},{256,384},{320,448},{384,512}... | collective-permute-start | bytes 479240 | tf_op jit(solution)/shard_map/ppermute | solution.py:66
  69.8 4.6 %collective-permute-start.8 = (bf16[104,768]{1,0:T(8,128)(2,1)S(1)}, bf16[104,768]{1,0:T(8,128)(2,1)S(1)}, u32[]{:S(2)}, u32[]{:S(2)}) collective-permute-start(bf16[104,768]{1,0:T(8,128)(2,1)S(1)} %slice.136), channel_id=1, source_target_pairs={{0,896},{64,960},{128,0},{192,64},{256,128},{320,192},{384,256},{4... | collective-permute-start | bytes 479240 | tf_op jit(solution)/shard_map/ppermute | solution.py:66
  75.4 1.2 collective-permute-done.8
  78.0 1.7 maximum_bitcast_fusion
  79.7 4.8 %all-to-all-done = bf16[64,24,512]{2,1,0:T(8,128)(2,1)S(1)} async-done(((bf16[64,24,512]{2,1,0:T(8,128)(2,1)}), bf16[64,24,512]{2,1,0:T(8,128)(2,1)S(1)}, u32[]{:S(2)}, u32[]{:S(2)}) %all-to-all-start) | async-done | bytes 1572896 | tf_op jit(solution)/shard_map/all_to_all | solution.py:15
  85.0 7.3 %all-to-all-start.1 = ((bf16[64,24,512]{2,1,0:T(8,128)(2,1)}), bf16[64,24,512]{2,1,0:T(8,128)(2,1)S(1)}, u32[]{:S(2)}, u32[]{:S(2)}) async-start(bf16[64,24,512]{2,1,0:T(8,128)(2,1)} %maximum_bitcast_fusion), calls=%async_computation.1 | async-start | bytes 3145728 | tf_op jit(solution)/shard_map/all_to_all | solution.py:15
  93.2 1.9 %collective-permute-start.12 = (bf16[192,512]{1,0:T(8,128)(2,1)S(1)}, bf16[192,512]{1,0:T(8,128)(2,1)S(1)}, u32[]{:S(2)}, u32[]{:S(2)}) collective-permute-start(bf16[192,512]{1,0:T(8,128)(2,1)S(1)} %get-tuple-element.12), channel_id=1, source_target_pairs={{0,256},{64,320},{128,384},{192,448},{256,512},{320,576},{384,640}... | collective-permute-start | bytes 589832 | tf_op jit(solution)/shard_map/ppermute | solution.py:66
  95.1 5.3 %collective-permute-start.15 = (bf16[192,512]{1,0:T(8,128)(2,1)}, bf16[192,512]{1,0:T(8,128)(2,1)}, u32[]{:S(2)}, u32[]{:S(2)}) collective-permute-start(bf16[192,512]{1,0:T(8,128)(2,1)} %get-tuple-element.13), channel_id=1, source_target_pairs={{0,512},{64,576},{128,640},{192,704},{256,768},{320,832},{384,896}... | collective-permute-start | bytes 589832 | tf_op jit(solution)/shard_map/ppermute | solution.py:66
  100.4 4.3 %collective-permute-start.14 = (bf16[192,512]{1,0:T(8,128)(2,1)}, bf16[192,512]{1,0:T(8,128)(2,1)}, u32[]{:S(2)}, u32[]{:S(2)}) collective-permute-start(bf16[192,512]{1,0:T(8,128)(2,1)} %get-tuple-element.14), channel_id=1, source_target_pairs={{0,384},{64,448},{128,512},{192,576},{256,640},{320,704},{384,768}... | collective-permute-start | bytes 589832 | tf_op jit(solution)/shard_map/ppermute | solution.py:66
  104.7 2.2 %collective-permute-start.10 = (bf16[192,512]{1,0:T(8,128)(2,1)S(1)}, bf16[192,512]{1,0:T(8,128)(2,1)S(1)}, u32[]{:S(2)}, u32[]{:S(2)}) collective-permute-start(bf16[192,512]{1,0:T(8,128)(2,1)S(1)} %get-tuple-element.17), channel_id=1, source_target_pairs={{0,128},{64,192},{128,256},{192,320},{256,384},{320,448},{384,512}... | collective-permute-start | bytes 589832 | tf_op jit(solution)/shard_map/ppermute | solution.py:66
  106.9 4.3 %collective-permute-start.9 = (bf16[192,512]{1,0:T(8,128)(2,1)S(1)}, bf16[192,512]{1,0:T(8,128)(2,1)S(1)}, u32[]{:S(2)}, u32[]{:S(2)}) collective-permute-start(bf16[192,512]{1,0:T(8,128)(2,1)S(1)} %get-tuple-element.18), channel_id=1, source_target_pairs={{0,896},{64,960},{128,0},{192,64},{256,128},{320,192},{384,256},{4... | collective-permute-start | bytes 589832 | tf_op jit(solution)/shard_map/ppermute | solution.py:66
  113.6 1.5 collective-permute-done.9
  115.1 5.2 %collective-permute-start.11 = (bf16[192,512]{1,0:T(8,128)(2,1)S(1)}, bf16[192,512]{1,0:T(8,128)(2,1)S(1)}, u32[]{:S(2)}, u32[]{:S(2)}) collective-permute-start(bf16[192,512]{1,0:T(8,128)(2,1)S(1)} %get-tuple-element.16), channel_id=1, source_target_pairs={{0,768},{64,832},{128,896},{192,960},{256,0},{320,64},{384,128},{4... | collective-permute-start | bytes 589832 | tf_op jit(solution)/shard_map/ppermute | solution.py:66
  121.0 11.8 %collective-permute-done.10 = bf16[192,512]{1,0:T(8,128)(2,1)S(1)} collective-permute-done((bf16[192,512]{1,0:T(8,128)(2,1)S(1)}, bf16[192,512]{1,0:T(8,128)(2,1)S(1)}, u32[]{:S(2)}, u32[]{:S(2)}) %collective-permute-start.10) | collective-permute-done | bytes 196640 | tf_op jit(solution)/shard_map/ppermute | solution.py:66
  132.8 1.9 %collective-permute-start.13 = (bf16[192,512]{1,0:T(8,128)(2,1)}, bf16[192,512]{1,0:T(8,128)(2,1)S(1)}, u32[]{:S(2)}, u32[]{:S(2)}) collective-permute-start(bf16[192,512]{1,0:T(8,128)(2,1)} %get-tuple-element.15), channel_id=1, source_target_pairs={{0,640},{64,704},{128,768},{192,832},{256,896},{320,960},{384,0},{... | collective-permute-start | bytes 589832 | tf_op jit(solution)/shard_map/ppermute | solution.py:66
  138.2 10.4 %collective-permute-done.13 = bf16[192,512]{1,0:T(8,128)(2,1)S(1)} collective-permute-done((bf16[192,512]{1,0:T(8,128)(2,1)}, bf16[192,512]{1,0:T(8,128)(2,1)S(1)}, u32[]{:S(2)}, u32[]{:S(2)}) %collective-permute-start.13) | collective-permute-done | bytes 196640 | tf_op jit(solution)/shard_map/ppermute | solution.py:66
  148.6 1.8 %fusion.16 = f32[768,512]{1,0:T(8,128)S(1)} fusion(bf16[576,768]{1,0:T(8,128)(2,1)S(1)} %copy-done.2, bf16[192,512]{1,0:T(8,128)(2,1)} %collective-permute-done.15, bf16[192,512]{1,0:T(8,128)(2,1)} %collective-permute-done.14, bf16[192,512]{1,0:T(8,128)(2,1)S(1)} %collective-permute-done.13), kind=kOutput, calls=%fused_computation.27 | convolution fusion | flops 454754304 | bytes 3047424 | tf_op jit(solution)/shard_map/dot_general | solution.py:149
  150.4 2.2 %convolution_add_fusion = f32[768,512]{1,0:T(8,128)S(1)} fusion(f32[768,512]{1,0:T(8,128)S(1)} %fusion.16, bf16[960,768]{1,0:T(8,128)(2,1)S(1)} %copy-done.6, bf16[960,512]{1,0:T(8,128)(2,1)} %constant_dynamic-update-slice_fusion.9), kind=kOutput, calls=%fused_computation.4 | convolution fusion | flops 755367936 | bytes 5603328 | tf_op jit(solution)/shard_map/dot_general | solution.py:149
  152.7 2.6 %collective-permute-start.16 = (f32[768,256]{1,0:T(8,128)S(1)}, f32[768,256]{1,0:T(8,128)S(1)}, u32[]{:S(2)}, u32[]{:S(2)}) collective-permute-start(f32[768,256]{1,0:T(8,128)S(1)} %constant_dynamic-slice_fusion), channel_id=1, source_target_pairs={{0,64},{64,0},{128,192},{192,128},{256,320},{320,256},{384,448},{4... | collective-permute-start | bytes 2359304 | tf_op jit(solution)/shard_map/ppermute | solution.py:156
  155.4 6.0 %all-to-all-start.2 = ((bf16[8,16,512]{2,1,0:T(8,128)(2,1)}), bf16[8,16,512]{2,1,0:T(8,128)(2,1)S(1)}, u32[]{:S(2)}, u32[]{:S(2)}) async-start(bf16[8,16,512]{2,1,0:T(8,128)(2,1)} %bitcast.20), calls=%async_computation.2 | async-start | bytes 262144 | tf_op jit(solution)/shard_map/all_to_all | solution.py:70
  161.4 8.5 %all-to-all-done.2 = bf16[8,16,512]{2,1,0:T(8,128)(2,1)S(1)} async-done(((bf16[8,16,512]{2,1,0:T(8,128)(2,1)}), bf16[8,16,512]{2,1,0:T(8,128)(2,1)S(1)}, u32[]{:S(2)}, u32[]{:S(2)}) %all-to-all-start.2) | async-done | bytes 131104 | tf_op jit(solution)/shard_map/all_to_all | solution.py:70
  (95 shorter events, 21.7 us)
Async XLA Ops:
  4.0 40.6 %collective-permute-start.1 = (bf16[208,768]{1,0:T(8,128)(2,1)S(1)}, bf16[208,768]{1,0:T(8,128)(2,1)}, u32[]{:S(2)}, u32[]{:S(2)}) collective-permute-start(bf16[208,768]{1,0:T(8,128)(2,1)S(1)} %pad_maximum_fusion.2), channel_id=1, source_target_pairs={{0,128},{64,192},{128,256},{192,320},{256,384},{320,448},{384,512}... | collective-permute-start | bytes 958472 | tf_op jit(solution)/shard_map/ppermute | solution.py:66
  9.7 36.9 %collective-permute-start = (bf16[208,768]{1,0:T(8,128)(2,1)S(1)}, bf16[208,768]{1,0:T(8,128)(2,1)S(1)}, u32[]{:S(2)}, u32[]{:S(2)}) collective-permute-start(bf16[208,768]{1,0:T(8,128)(2,1)S(1)} %pad_maximum_fusion.2), channel_id=1, source_target_pairs={{0,896},{64,960},{128,0},{192,64},{256,128},{320,192},{384,256},{4... | collective-permute-start | bytes 958472 | tf_op jit(solution)/shard_map/ppermute | solution.py:66
  23.8 29.1 %collective-permute-start.4 = (bf16[768,256]{1,0:T(8,128)(2,1)}, bf16[768,256]{1,0:T(8,128)(2,1)S(1)}, u32[]{:S(2)}, u32[]{:S(2)}) collective-permute-start(bf16[768,256]{1,0:T(8,128)(2,1)} %bitcast.83), channel_id=1, source_target_pairs={{0,64},{64,0},{128,192},{192,128},{256,320},{320,256},{384,448},{4... | collective-permute-start | bytes 1179656 | tf_op jit(solution)/shard_map/ppermute | solution.py:112
  31.6 12.9 %copy-start = (bf16[1,1,64,3,768]{4,2,3,1,0:T(8,128)(2,1)S(1)}, bf16[1,1,64,3,768]{4,2,3,1,0:T(8,128)(2,1)}, u32[]{:S(2)}) copy-start(bf16[1,1,64,3,768]{4,2,3,1,0:T(8,128)(2,1)} %param.7) | copy-start | bytes 884740
  31.6 52.9 %all-to-all-start = ((bf16[64,24,512]{2,1,0:T(8,128)(2,1)}), bf16[64,24,512]{2,1,0:T(8,128)(2,1)S(1)}, u32[]{:S(2)}, u32[]{:S(2)}) async-start(bf16[64,24,512]{2,1,0:T(8,128)(2,1)} %bitcast.14), calls=%async_computation | async-start | bytes 3145728 | tf_op jit(solution)/shard_map/all_to_all | solution.py:15
  44.5 8.4 %copy-start.4 = (bf16[1,768,256]{2,1,0:T(8,128)(2,1)S(1)}, bf16[1,768,256]{2,1,0:T(8,128)(2,1)}, u32[]{:S(2)}) copy-start(bf16[1,768,256]{2,1,0:T(8,128)(2,1)} %param.8) | copy-start | bytes 1179652
  44.6 12.2 %collective-permute-start.3 = (bf16[208,768]{1,0:T(8,128)(2,1)}, bf16[208,768]{1,0:T(8,128)(2,1)S(1)}, u32[]{:S(2)}, u32[]{:S(2)}) collective-permute-start(bf16[208,768]{1,0:T(8,128)(2,1)} %collective-permute-done.1), channel_id=1, source_target_pairs={{0,128},{64,192},{128,256},{192,320},{256,384},{320,448},{384,512}... | collective-permute-start | bytes 958472 | tf_op jit(solution)/shard_map/ppermute | solution.py:66
  46.6 12.1 %collective-permute-start.2 = (bf16[208,768]{1,0:T(8,128)(2,1)S(1)}, bf16[208,768]{1,0:T(8,128)(2,1)S(1)}, u32[]{:S(2)}, u32[]{:S(2)}) collective-permute-start(bf16[208,768]{1,0:T(8,128)(2,1)S(1)} %collective-permute-done), channel_id=1, source_target_pairs={{0,896},{64,960},{128,0},{192,64},{256,128},{320,192},{384,256},{4... | collective-permute-start | bytes 958472 | tf_op jit(solution)/shard_map/ppermute | solution.py:66
  56.8 11.0 %collective-permute-start.6 = (bf16[208,768]{1,0:T(8,128)(2,1)S(1)}, bf16[208,768]{1,0:T(8,128)(2,1)S(1)}, u32[]{:S(2)}, u32[]{:S(2)}) collective-permute-start(bf16[208,768]{1,0:T(8,128)(2,1)S(1)} %collective-permute-done.3), channel_id=1, source_target_pairs={{0,128},{64,192},{128,256},{192,320},{256,384},{320,448},{384,512}... | collective-permute-start | bytes 958472 | tf_op jit(solution)/shard_map/ppermute | solution.py:66
  58.7 11.1 %collective-permute-start.5 = (bf16[208,768]{1,0:T(8,128)(2,1)S(1)}, bf16[208,768]{1,0:T(8,128)(2,1)S(1)}, u32[]{:S(2)}, u32[]{:S(2)}) collective-permute-start(bf16[208,768]{1,0:T(8,128)(2,1)S(1)} %collective-permute-done.2), channel_id=1, source_target_pairs={{0,896},{64,960},{128,0},{192,64},{256,128},{320,192},{384,256},{4... | collective-permute-start | bytes 958472 | tf_op jit(solution)/shard_map/ppermute | solution.py:66
  63.4 1.1 copy-start.5
  67.9 7.5 %collective-permute-start.7 = (bf16[104,768]{1,0:T(8,128)(2,1)S(1)}, bf16[104,768]{1,0:T(8,128)(2,1)S(1)}, u32[]{:S(2)}, u32[]{:S(2)}) collective-permute-start(bf16[104,768]{1,0:T(8,128)(2,1)S(1)} %slice.135), channel_id=1, source_target_pairs={{0,128},{64,192},{128,256},{192,320},{256,384},{320,448},{384,512}... | collective-permute-start | bytes 479240 | tf_op jit(solution)/shard_map/ppermute | solution.py:66
  69.8 6.8 %collective-permute-start.8 = (bf16[104,768]{1,0:T(8,128)(2,1)S(1)}, bf16[104,768]{1,0:T(8,128)(2,1)S(1)}, u32[]{:S(2)}, u32[]{:S(2)}) collective-permute-start(bf16[104,768]{1,0:T(8,128)(2,1)S(1)} %slice.136), channel_id=1, source_target_pairs={{0,896},{64,960},{128,0},{192,64},{256,128},{320,192},{384,256},{4... | collective-permute-start | bytes 479240 | tf_op jit(solution)/shard_map/ppermute | solution.py:66
  76.7 0.9 copy-start.1
  85.0 51.8 %all-to-all-start.1 = ((bf16[64,24,512]{2,1,0:T(8,128)(2,1)}), bf16[64,24,512]{2,1,0:T(8,128)(2,1)S(1)}, u32[]{:S(2)}, u32[]{:S(2)}) async-start(bf16[64,24,512]{2,1,0:T(8,128)(2,1)} %maximum_bitcast_fusion), calls=%async_computation.1 | async-start | bytes 3145728 | tf_op jit(solution)/shard_map/all_to_all | solution.py:15
  93.2 42.9 %collective-permute-start.12 = (bf16[192,512]{1,0:T(8,128)(2,1)S(1)}, bf16[192,512]{1,0:T(8,128)(2,1)S(1)}, u32[]{:S(2)}, u32[]{:S(2)}) collective-permute-start(bf16[192,512]{1,0:T(8,128)(2,1)S(1)} %get-tuple-element.12), channel_id=1, source_target_pairs={{0,256},{64,320},{128,384},{192,448},{256,512},{320,576},{384,640}... | collective-permute-start | bytes 589832 | tf_op jit(solution)/shard_map/ppermute | solution.py:66
  95.1 43.0 %collective-permute-start.15 = (bf16[192,512]{1,0:T(8,128)(2,1)}, bf16[192,512]{1,0:T(8,128)(2,1)}, u32[]{:S(2)}, u32[]{:S(2)}) collective-permute-start(bf16[192,512]{1,0:T(8,128)(2,1)} %get-tuple-element.13), channel_id=1, source_target_pairs={{0,512},{64,576},{128,640},{192,704},{256,768},{320,832},{384,896}... | collective-permute-start | bytes 589832 | tf_op jit(solution)/shard_map/ppermute | solution.py:66
  100.4 37.8 %collective-permute-start.14 = (bf16[192,512]{1,0:T(8,128)(2,1)}, bf16[192,512]{1,0:T(8,128)(2,1)}, u32[]{:S(2)}, u32[]{:S(2)}) collective-permute-start(bf16[192,512]{1,0:T(8,128)(2,1)} %get-tuple-element.14), channel_id=1, source_target_pairs={{0,384},{64,448},{128,512},{192,576},{256,640},{320,704},{384,768}... | collective-permute-start | bytes 589832 | tf_op jit(solution)/shard_map/ppermute | solution.py:66
  104.7 28.1 %collective-permute-start.10 = (bf16[192,512]{1,0:T(8,128)(2,1)S(1)}, bf16[192,512]{1,0:T(8,128)(2,1)S(1)}, u32[]{:S(2)}, u32[]{:S(2)}) collective-permute-start(bf16[192,512]{1,0:T(8,128)(2,1)S(1)} %get-tuple-element.17), channel_id=1, source_target_pairs={{0,128},{64,192},{128,256},{192,320},{256,384},{320,448},{384,512}... | collective-permute-start | bytes 589832 | tf_op jit(solution)/shard_map/ppermute | solution.py:66
  106.9 8.2 %collective-permute-start.9 = (bf16[192,512]{1,0:T(8,128)(2,1)S(1)}, bf16[192,512]{1,0:T(8,128)(2,1)S(1)}, u32[]{:S(2)}, u32[]{:S(2)}) collective-permute-start(bf16[192,512]{1,0:T(8,128)(2,1)S(1)} %get-tuple-element.18), channel_id=1, source_target_pairs={{0,896},{64,960},{128,0},{192,64},{256,128},{320,192},{384,256},{4... | collective-permute-start | bytes 589832 | tf_op jit(solution)/shard_map/ppermute | solution.py:66
  113.6 23.1 %copy-start.3 = (bf16[64,24,128]{2,0,1:T(8,128)(2,1)S(1)}, bf16[64,24,128]{2,0,1:T(8,128)(2,1)}, u32[]{:S(2)}) copy-start(bf16[64,24,128]{2,0,1:T(8,128)(2,1)} %get-tuple-element.26) | copy-start | bytes 1179652
  115.1 20.3 %collective-permute-start.11 = (bf16[192,512]{1,0:T(8,128)(2,1)S(1)}, bf16[192,512]{1,0:T(8,128)(2,1)S(1)}, u32[]{:S(2)}, u32[]{:S(2)}) collective-permute-start(bf16[192,512]{1,0:T(8,128)(2,1)S(1)} %get-tuple-element.16), channel_id=1, source_target_pairs={{0,768},{64,832},{128,896},{192,960},{256,0},{320,64},{384,128},{4... | collective-permute-start | bytes 589832 | tf_op jit(solution)/shard_map/ppermute | solution.py:66
  132.8 15.8 %collective-permute-start.13 = (bf16[192,512]{1,0:T(8,128)(2,1)}, bf16[192,512]{1,0:T(8,128)(2,1)S(1)}, u32[]{:S(2)}, u32[]{:S(2)}) collective-permute-start(bf16[192,512]{1,0:T(8,128)(2,1)} %get-tuple-element.15), channel_id=1, source_target_pairs={{0,640},{64,704},{128,768},{192,832},{256,896},{320,960},{384,0},{... | collective-permute-start | bytes 589832 | tf_op jit(solution)/shard_map/ppermute | solution.py:66
  136.8 11.8 %copy-start.2 = (bf16[576,768]{1,0:T(8,128)(2,1)S(1)}, bf16[576,768]{1,0:T(8,128)(2,1)}, u32[]{:S(2)}) copy-start(bf16[576,768]{1,0:T(8,128)(2,1)} %copy-done.1) | copy-start | bytes 2654212
  138.2 12.3 %copy-start.6 = (bf16[960,768]{1,0:T(8,128)(2,1)S(1)}, bf16[960,768]{1,0:T(8,128)(2,1)}, u32[]{:S(2)}) copy-start(bf16[960,768]{1,0:T(8,128)(2,1)} %copy-done.5) | copy-start | bytes 4423684
  152.7 17.8 %collective-permute-start.16 = (f32[768,256]{1,0:T(8,128)S(1)}, f32[768,256]{1,0:T(8,128)S(1)}, u32[]{:S(2)}, u32[]{:S(2)}) collective-permute-start(f32[768,256]{1,0:T(8,128)S(1)} %constant_dynamic-slice_fusion), channel_id=1, source_target_pairs={{0,64},{64,0},{128,192},{192,128},{256,320},{320,256},{384,448},{4... | collective-permute-start | bytes 2359304 | tf_op jit(solution)/shard_map/ppermute | solution.py:156
  155.4 14.5 %all-to-all-start.2 = ((bf16[8,16,512]{2,1,0:T(8,128)(2,1)}), bf16[8,16,512]{2,1,0:T(8,128)(2,1)S(1)}, u32[]{:S(2)}, u32[]{:S(2)}) async-start(bf16[8,16,512]{2,1,0:T(8,128)(2,1)} %bitcast.20), calls=%async_computation.2 | async-start | bytes 262144 | tf_op jit(solution)/shard_map/all_to_all | solution.py:70

commit v4 on v3

--- a/solution.py
+++ b/solution.py
@@ -71,42 +71,35 @@
             blocks, "dp", split_axis=0, concat_axis=0, tiled=True, axis_index_groups=column
         )
 
-    def along(group):
-        return (group + chips - chip) % chips
-
     def in_order(group):
-        ahead = along(group)
+        ahead = (group + chips - chip) % chips
         return jnp.where(
             ahead > chips // 2, 2 * (chips - ahead), jnp.maximum(2 * ahead - 1, 0)
         )
 
-    named = routed_experts.astype(F32)
+    table = jnp.concatenate(
+        [routed_experts.astype(F32).astype(BF16), *parts_of(route_gates, 3)], axis=1
+    )
+    table = jnp.pad(table, ((0, 0), (0, LANES - table.shape[1])))
+    blocks = jnp.swapaxes(output_grad.reshape(own, chips, part), 0, 1)
+    blocks = jnp.concatenate([blocks, jnp.broadcast_to(table, (chips, own, LANES))], axis=2)
+    arrived = chip_move(blocks)
+    grads = arrived[:, :, :part].reshape(tokens, part)
+    tables = arrived[:, :, part:].reshape(tokens, LANES).astype(F32)
+    gates = sum(tables[:, topk * i : topk * (i + 1)] for i in (1, 2, 3))
+    placer = placer_of(tables[:, :topk], gates, experts, own, capacity, in_order)
+    outgoing = jnp.dot(placer, jnp.concatenate([grads, grads], axis=0), preferred_element_type=F32)
+    outgoing = outgoing.astype(BF16).reshape(experts, lines, part)
+    scaled = expert_move(outgoing)
 
-    blocks = jnp.swapaxes(output_grad.reshape(own, chips, part), 0, 1).reshape(tokens, part)
-    placer = placer_of(
-        jnp.tile(named, (chips, 1)), jnp.tile(route_gates, (chips, 1)), experts, own, capacity, along
-    )
-    outgoing = jnp.dot(placer, jnp.concatenate([blocks, blocks], axis=0), preferred_element_type=F32)
-    outgoing = outgoing.astype(BF16).reshape(experts, lines, part)
-
-    table = jnp.concatenate([named.astype(BF16), *parts_of(route_gates, 3)], axis=1)
-    table = jnp.pad(table, ((0, 0), (0, depth - table.shape[1])))
-    rows = jnp.swapaxes(expert_hidden[0, 0], 0, 1).reshape(held, depth)
-    mine = with_layout_constraint(jnp.concatenate([rows, table], axis=0), Layout((0, 1)))
-    order = [0]
+    mine = jnp.swapaxes(expert_hidden[0, 0], 0, 1).reshape(held, depth)
     up = down = mine
     around = [mine]
-    for step in range(1, chips // 2):
+    for _ in range(1, chips // 2):
         up, down = shift(up, 1), shift(down, -1)
-        order += [step, chips - step]
         around += [down, up]
-    middle = mine.shape[0] // 2
-    order.append(chips // 2)
+    middle = held // 2
     around.append(jnp.concatenate([shift(up[:middle], 1), shift(down[middle:], -1)], axis=0))
-
-    scaled = expert_move(outgoing)
-    scaled = jnp.swapaxes(scaled, 0, 1)
-    scaled = scaled.reshape(chips, held, part)
 
     weight = down_weight[0]
     other = lax.ppermute(weight, "dp", swap)
@@ -116,25 +109,15 @@
     weight = lax.optimization_barrier(weight)
     early = chips // 2 + 1
     hidden = [
-        jnp.concatenate([block[:held] for block in blocks], axis=0)
+        jnp.concatenate(blocks, axis=0)
         for blocks in (around[:early], around[early:])
     ]
     produced = [jnp.dot(h, weight, preferred_element_type=F32).astype(BF16) for h in hidden]
     produced = jnp.concatenate([p.reshape(-1, experts, part) for p in produced], axis=0)
-    tables = jnp.concatenate([block[held:, :LANES] for block in around], axis=0)
-    produced, scaled, tables = lax.optimization_barrier(
-        (jnp.swapaxes(produced, 0, 1), scaled, tables)
-    )
-    returned = expert_move(produced)
+    returned = expert_move(jnp.swapaxes(produced, 0, 1))
 
-    wanted = lax.broadcasted_iota(jnp.int32, (tokens, tokens), 0)
-    source = in_order(wanted // own) * own + wanted % own
-    turn = (source == lax.broadcasted_iota(jnp.int32, (tokens, tokens), 1)).astype(BF16)
-    tables = jnp.dot(turn, tables, preferred_element_type=F32)
-    gates = sum(tables[:, topk * i : topk * (i + 1)] for i in (1, 2, 3))
-    mixer = placer_of(tables[:, :topk], gates, experts, own, capacity, in_order)
     mixed = lax.dot_general(
-        mixer,
+        placer,
         returned.reshape(experts * lines, part),
         (((0,), (0,)), ((), ())),
         preferred_element_type=F32,
@@ -143,13 +126,11 @@
     combined = chip_move(mixed)
     combined = jnp.swapaxes(combined, 0, 1).reshape(own, width)
 
-    grad_rows = [scaled[0]] + [shift(scaled[(chips - i) % chips], -i) for i in order[1:]]
-    hidden, _ = lax.optimization_barrier((hidden, mixed))
+    grad_rows = jnp.swapaxes(scaled, 0, 1).reshape(lines * experts, part)
+    cut = early * held
     gradient = sum(
-        lax.dot_general(
-            h, jnp.concatenate(g, axis=0), (((0,), (0,)), ((), ())), preferred_element_type=F32
-        )
-        for h, g in zip(hidden, (grad_rows[:early], grad_rows[early:]))
+        lax.dot_general(h, g, (((0,), (0,)), ((), ())), preferred_element_type=F32)
+        for h, g in zip(hidden, (grad_rows[:cut], grad_rows[cut:]))
     )
     kept = lax.dynamic_slice_in_dim(gradient, core * half, half, 1)
     given = lax.dynamic_slice_in_dim(gradient, (1 - core) * half, half, 1)

time: 173 us -> 164 us (0.948)
  the two profiles are of different devices: /device:TPU:1 before, /device:TPU:16 now
where the time goes in v4:
time: 164 us; the launch traced here: 163 us
  starting transfers between devices  76.6 us (47%)
  waiting for transfers between devices  62.1 us (38%)
  other arithmetic  8.42 us (5%)
  local copies, waits for them, and re-layouts  7.64 us (5%)
  matrix products  7.03 us (4%)
    all_to_all x2, waiting for transfers between devices, expert_move(): lax.all_to_all(buffer, ('ctx', 'tp'), split_axis=0, concat_axis=0, tiled=...  31.3 us
    all_to_all x2, starting transfers between devices, expert_move(): lax.all_to_all(buffer, ('ctx', 'tp'), split_axis=0, concat_axis=0, tiled=...  26.1 us
    ppermute x8, starting transfers between devices, shift(): lax.ppermute(block, 'dp', [(d, (d + CORES * by) % dp) for d in range(dp)])  25 us
    all_to_all x2, starting transfers between devices, chip_move(): lax.all_to_all(blocks, 'dp', split_axis=0, concat_axis=0, tiled=True, axi...  21.8 us
    all_to_all x2, waiting for transfers between devices, chip_move(): lax.all_to_all(blocks, 'dp', split_axis=0, concat_axis=0, tiled=True, axi...  16 us
    ppermute x8, waiting for transfers between devices, shift(): lax.ppermute(block, 'dp', [(d, (d + CORES * by) % dp) for d in range(dp)])  14.8 us
    unnamed x27, local copies, waits for them, and re-layouts  3.54 us
  transfers between devices with their start and end apart: 14, of which 8 were waited for; matrix products, arithmetic and copies ran while one was open for 9% of the time, Pallas kernels for 0%

profile of v4, /device:TPU:16, one launch (start us, length us, event | category | flops | bytes accessed | tf_op | source)
XLA Modules:
  0.0 162.9 jit_solution(14570366854316911503)
XLA Ops:
  2.1 1.0 copy.58
  3.8 16.7 %all-to-all-start = ((bf16[8,16,640]{2,1,0:T(8,128)(2,1)}), bf16[8,16,640]{2,1,0:T(8,128)(2,1)S(1)}, u32[]{:S(2)}, u32[]{:S(2)}) async-start(bf16[8,16,640]{2,1,0:T(8,128)(2,1)} %copy.42), calls=%async_computation | async-start | bytes 327680 | tf_op jit(solution)/shard_map/all_to_all | solution.py:70
  21.1 9.1 %all-to-all-done = bf16[8,16,640]{2,1,0:T(8,128)(2,1)S(1)} async-done(((bf16[8,16,640]{2,1,0:T(8,128)(2,1)}), bf16[8,16,640]{2,1,0:T(8,128)(2,1)S(1)}, u32[]{:S(2)}, u32[]{:S(2)}) %all-to-all-start) | async-done | bytes 163872 | tf_op jit(solution)/shard_map/all_to_all | solution.py:70
  31.6 1.7 %convolution_convert_fusion = bf16[1536,512]{1,0:T(8,128)(2,1)} fusion(bf16[1536,128]{1,0:T(8,128)(2,1)S(1)} %get-tuple-element.7, bf16[1536,128]{1,0:T(8,128)(2,1)S(1)} %get-tuple-element.6, bf16[128,512]{1,0:T(8,128)(2,1)S(1)} %bitcast.71), kind=kOutput, calls=%fused_computation | convolution fusion | flops 405536768 | bytes 2490368 | tf_op jit(solution)/shard_map/dot_general | solution.py:91
  33.4 13.5 %all-to-all-start.3 = ((bf16[64,24,512]{2,1,0:T(8,128)(2,1)}), bf16[64,24,512]{2,1,0:T(8,128)(2,1)S(1)}, u32[]{:S(2)}, u32[]{:S(2)}) async-start(bf16[64,24,512]{2,1,0:T(8,128)(2,1)} %bitcast.21), calls=%async_computation.3 | async-start | bytes 3145728 | tf_op jit(solution)/shard_map/all_to_all | solution.py:15
  46.9 1.9 %collective-permute-start = (bf16[192,768]{1,0:T(8,128)(2,1)S(1)}, bf16[192,768]{1,0:T(8,128)(2,1)S(1)}, u32[]{:S(2)}, u32[]{:S(2)}) collective-permute-start(bf16[192,768]{1,0:T(8,128)(2,1)S(1)} %bitcast.66), channel_id=1, source_target_pairs={{0,896},{64,960},{128,0},{192,64},{256,128},{320,192},{384,256},{4... | collective-permute-start | bytes 884744 | tf_op jit(solution)/shard_map/ppermute | solution.py:66
  48.8 3.9 %collective-permute-start.1 = (bf16[192,768]{1,0:T(8,128)(2,1)S(1)}, bf16[192,768]{1,0:T(8,128)(2,1)S(1)}, u32[]{:S(2)}, u32[]{:S(2)}) collective-permute-start(bf16[192,768]{1,0:T(8,128)(2,1)S(1)} %bitcast.67), channel_id=1, source_target_pairs={{0,128},{64,192},{128,256},{192,320},{256,384},{320,448},{384,512}... | collective-permute-start | bytes 884744 | tf_op jit(solution)/shard_map/ppermute | solution.py:66
  52.7 1.9 %collective-permute-start.4 = (bf16[768,256]{1,0:T(8,128)(2,1)S(1)}, bf16[768,256]{1,0:T(8,128)(2,1)S(1)}, u32[]{:S(2)}, u32[]{:S(2)}) collective-permute-start(bf16[768,256]{1,0:T(8,128)(2,1)S(1)} %bitcast.65), channel_id=1, source_target_pairs={{0,64},{64,0},{128,192},{192,128},{256,320},{320,256},{384,448},{4... | collective-permute-start | bytes 1179656 | tf_op jit(solution)/shard_map/ppermute | solution.py:105
  55.5 3.1 %collective-permute-start.2 = (bf16[192,768]{1,0:T(8,128)(2,1)S(1)}, bf16[192,768]{1,0:T(8,128)(2,1)S(1)}, u32[]{:S(2)}, u32[]{:S(2)}) collective-permute-start(bf16[192,768]{1,0:T(8,128)(2,1)S(1)} %collective-permute-done), channel_id=1, source_target_pairs={{0,896},{64,960},{128,0},{192,64},{256,128},{320,192},{384,256},{4... | collective-permute-start | bytes 884744 | tf_op jit(solution)/shard_map/ppermute | solution.py:66
  58.6 2.7 %collective-permute-start.3 = (bf16[192,768]{1,0:T(8,128)(2,1)S(1)}, bf16[192,768]{1,0:T(8,128)(2,1)S(1)}, u32[]{:S(2)}, u32[]{:S(2)}) collective-permute-start(bf16[192,768]{1,0:T(8,128)(2,1)S(1)} %collective-permute-done.1), channel_id=1, source_target_pairs={{0,128},{64,192},{128,256},{192,320},{256,384},{320,448},{384,512}... | collective-permute-start | bytes 884744 | tf_op jit(solution)/shard_map/ppermute | solution.py:66
  61.5 4.5 %collective-permute-done.2 = bf16[192,768]{1,0:T(8,128)(2,1)S(1)} collective-permute-done((bf16[192,768]{1,0:T(8,128)(2,1)S(1)}, bf16[192,768]{1,0:T(8,128)(2,1)S(1)}, u32[]{:S(2)}, u32[]{:S(2)}) %collective-permute-start.2) | collective-permute-done | bytes 294944 | tf_op jit(solution)/shard_map/ppermute | solution.py:66
  66.0 4.3 %collective-permute-start.5 = (bf16[192,768]{1,0:T(8,128)(2,1)S(1)}, bf16[192,768]{1,0:T(8,128)(2,1)S(1)}, u32[]{:S(2)}, u32[]{:S(2)}) collective-permute-start(bf16[192,768]{1,0:T(8,128)(2,1)S(1)} %collective-permute-done.2), channel_id=1, source_target_pairs={{0,896},{64,960},{128,0},{192,64},{256,128},{320,192},{384,256},{4... | collective-permute-start | bytes 884744 | tf_op jit(solution)/shard_map/ppermute | solution.py:66
  70.4 1.9 %collective-permute-start.6 = (bf16[192,768]{1,0:T(8,128)(2,1)S(1)}, bf16[192,768]{1,0:T(8,128)(2,1)S(1)}, u32[]{:S(2)}, u32[]{:S(2)}) collective-permute-start(bf16[192,768]{1,0:T(8,128)(2,1)S(1)} %collective-permute-done.3), channel_id=1, source_target_pairs={{0,128},{64,192},{128,256},{192,320},{256,384},{320,448},{384,512}... | collective-permute-start | bytes 884744 | tf_op jit(solution)/shard_map/ppermute | solution.py:66
  72.4 0.9 convolution_convert_fusion.1
  74.0 7.0 %collective-permute-done.6 = bf16[192,768]{1,0:T(8,128)(2,1)S(1)} collective-permute-done((bf16[192,768]{1,0:T(8,128)(2,1)S(1)}, bf16[192,768]{1,0:T(8,128)(2,1)S(1)}, u32[]{:S(2)}, u32[]{:S(2)}) %collective-permute-start.6) | collective-permute-done | bytes 294944 | tf_op jit(solution)/shard_map/ppermute | solution.py:66
  81.0 1.9 %collective-permute-start.7 = (bf16[96,768]{1,0:T(8,128)(2,1)S(1)}, bf16[96,768]{1,0:T(8,128)(2,1)S(1)}, u32[]{:S(2)}, u32[]{:S(2)}) collective-permute-start(bf16[96,768]{1,0:T(8,128)(2,1)S(1)} %slice.61), channel_id=1, source_target_pairs={{0,128},{64,192},{128,256},{192,320},{256,384},{320,448},{384,512}... | collective-permute-start | bytes 442376 | tf_op jit(solution)/shard_map/ppermute | solution.py:66
  83.0 5.1 %collective-permute-start.8 = (bf16[96,768]{1,0:T(8,128)(2,1)S(1)}, bf16[96,768]{1,0:T(8,128)(2,1)S(1)}, u32[]{:S(2)}, u32[]{:S(2)}) collective-permute-start(bf16[96,768]{1,0:T(8,128)(2,1)S(1)} %slice.62), channel_id=1, source_target_pairs={{0,896},{64,960},{128,0},{192,64},{256,128},{320,192},{384,256},{4... | collective-permute-start | bytes 442376 | tf_op jit(solution)/shard_map/ppermute | solution.py:66
  88.1 1.1 collective-permute-done.7
  89.3 1.5 collective-permute-done.8
  92.1 1.7 %maximum_bitcast_fusion = bf16[64,24,512]{2,1,0:T(8,128)(2,1)} fusion(bf16[9,64,512]{2,0,1:T(8,128)(2,1)S(1)} %copy.46, bf16[15,64,512]{2,0,1:T(8,128)(2,1)S(1)} %copy.45), kind=kLoop, calls=%fused_computation.1 | loop fusion | flops 3145728 | bytes 3145728 | tf_op jit(solution)/shard_map/transpose | solution.py:117
  93.8 12.6 %all-to-all-start.1 = ((bf16[64,24,512]{2,1,0:T(8,128)(2,1)}), bf16[64,24,512]{2,1,0:T(8,128)(2,1)S(1)}, u32[]{:S(2)}, u32[]{:S(2)}) async-start(bf16[64,24,512]{2,1,0:T(8,128)(2,1)} %maximum_bitcast_fusion), calls=%async_computation.1 | async-start | bytes 3145728 | tf_op jit(solution)/shard_map/all_to_all | solution.py:15
  107.0 1.0 copy-done.1
  108.0 0.8 fusion.35
  108.8 1.0 convolution_add_fusion
  109.9 1.0 constant_dynamic-slice_fusion
  110.8 1.9 %collective-permute-start.9 = (f32[768,256]{1,0:T(8,128)}, f32[768,256]{1,0:T(8,128)}, u32[]{:S(2)}, u32[]{:S(2)}) collective-permute-start(f32[768,256]{1,0:T(8,128)} %constant_dynamic-slice_fusion), channel_id=1, source_target_pairs={{0,64},{64,0},{128,192},{192,128},{256,320},{320,256},{384,448},{4... | collective-permute-start | bytes 2359304 | tf_op jit(solution)/shard_map/ppermute | solution.py:137
  112.7 1.7 %compare_select_fusion.1 = (bf16[64,24,128]{2,0,1:T(8,128)(2,1)S(1)}, bf16[64,24,128]{2,0,1:T(8,128)(2,1)}) fusion(f32[64,128]{1,0:T(8,128)} %copy-done.5, f32[24]{0:T(128)} %copy-done.8, bf16[64,128]{1,0:T(8,128)(2,1)S(1)} %get-tuple-element.10, bf16[64,128]{1,0:T(8,128)(2,1)} %copy-done.4), kind=kLoop, calls=%fused_computation.12 | loop fusion | flops 589824 | bytes 852064 | tf_op jit(solution)/shard_map/jit(_where)/select_n | solution.py:44
  114.4 31.3 %all-to-all-done.1 = bf16[64,24,512]{2,1,0:T(8,128)(2,1)S(1)} async-done(((bf16[64,24,512]{2,1,0:T(8,128)(2,1)}), bf16[64,24,512]{2,1,0:T(8,128)(2,1)S(1)}, u32[]{:S(2)}, u32[]{:S(2)}) %all-to-all-start.1) | async-done | bytes 1572896 | tf_op jit(solution)/shard_map/all_to_all | solution.py:15
  145.7 1.7 %fusion.2 = f32[256,512]{1,0:T(8,128)S(1)} fusion(bf16[64,24,512]{2,1,0:T(8,128)(2,1)S(1)} %all-to-all-done.1, bf16[64,24,128]{2,0,1:T(8,128)(2,1)} %get-tuple-element.9, bf16[64,24,128]{2,0,1:T(8,128)(2,1)S(1)} %get-tuple-element.8), kind=kOutput, calls=%fused_computation.8 | convolution fusion | flops 404226048 | bytes 2883584 | tf_op jit(solution)/shard_map/dot_general | solution.py:119
  148.1 5.1 %all-to-all-start.2 = ((bf16[8,16,512]{2,1,0:T(8,128)(2,1)}), bf16[8,16,512]{2,1,0:T(8,128)(2,1)S(1)}, u32[]{:S(2)}, u32[]{:S(2)}) async-start(bf16[8,16,512]{2,1,0:T(8,128)(2,1)} %bitcast.15), calls=%async_computation.2 | async-start | bytes 262144 | tf_op jit(solution)/shard_map/all_to_all | solution.py:70
  153.2 2.2 %add_bitcast_fusion = f32[1,768,256]{2,1,0:T(8,128)} fusion(f32[768,256]{1,0:T(8,128)} %collective-permute-done.9, f32[768,512]{1,0:T(8,128)S(1)} %convolution_add_fusion, s32[]{:T(128)S(6)} %select_n.81), kind=kLoop, calls=%fused_computation.23 | loop fusion | flops 196608 | bytes 2359300 | tf_op jit(solution)/shard_map/broadcast_in_dim | solution.py:138
  155.4 6.9 %all-to-all-done.2 = bf16[8,16,512]{2,1,0:T(8,128)(2,1)S(1)} async-done(((bf16[8,16,512]{2,1,0:T(8,128)(2,1)}), bf16[8,16,512]{2,1,0:T(8,128)(2,1)S(1)}, u32[]{:S(2)}, u32[]{:S(2)}) %all-to-all-start.2) | async-done | bytes 131104 | tf_op jit(solution)/shard_map/all_to_all | solution.py:70
  (70 shorter events, 9.2 us)
Async XLA Ops:
  3.8 26.5 %all-to-all-start = ((bf16[8,16,640]{2,1,0:T(8,128)(2,1)}), bf16[8,16,640]{2,1,0:T(8,128)(2,1)S(1)}, u32[]{:S(2)}, u32[]{:S(2)}) async-start(bf16[8,16,640]{2,1,0:T(8,128)(2,1)} %copy.42), calls=%async_computation | async-start | bytes 327680 | tf_op jit(solution)/shard_map/all_to_all | solution.py:70
  20.5 0.5 copy-start.8
  30.8 0.6 copy-start.4
  31.0 0.6 copy-start.5
  33.3 13.5 %copy-start.3 = (bf16[1,1,64,3,768]{4,2,3,1,0:T(8,128)(2,1)S(1)}, bf16[1,1,64,3,768]{4,2,3,1,0:T(8,128)(2,1)}, u32[]{:S(2)}) copy-start(bf16[1,1,64,3,768]{4,2,3,1,0:T(8,128)(2,1)} %param.7) | copy-start | bytes 884740
  33.3 19.4 %copy-start.2 = (bf16[1,768,256]{2,1,0:T(8,128)(2,1)S(1)}, bf16[1,768,256]{2,1,0:T(8,128)(2,1)}, u32[]{:S(2)}) copy-start(bf16[1,768,256]{2,1,0:T(8,128)(2,1)} %param.8) | copy-start | bytes 1179652
  33.4 60.4 %all-to-all-start.3 = ((bf16[64,24,512]{2,1,0:T(8,128)(2,1)}), bf16[64,24,512]{2,1,0:T(8,128)(2,1)S(1)}, u32[]{:S(2)}, u32[]{:S(2)}) async-start(bf16[64,24,512]{2,1,0:T(8,128)(2,1)} %bitcast.21), calls=%async_computation.3 | async-start | bytes 3145728 | tf_op jit(solution)/shard_map/all_to_all | solution.py:15
  46.9 8.6 %collective-permute-start = (bf16[192,768]{1,0:T(8,128)(2,1)S(1)}, bf16[192,768]{1,0:T(8,128)(2,1)S(1)}, u32[]{:S(2)}, u32[]{:S(2)}) collective-permute-start(bf16[192,768]{1,0:T(8,128)(2,1)S(1)} %bitcast.66), channel_id=1, source_target_pairs={{0,896},{64,960},{128,0},{192,64},{256,128},{320,192},{384,256},{4... | collective-permute-start | bytes 884744 | tf_op jit(solution)/shard_map/ppermute | solution.py:66
  48.8 9.8 %collective-permute-start.1 = (bf16[192,768]{1,0:T(8,128)(2,1)S(1)}, bf16[192,768]{1,0:T(8,128)(2,1)S(1)}, u32[]{:S(2)}, u32[]{:S(2)}) collective-permute-start(bf16[192,768]{1,0:T(8,128)(2,1)S(1)} %bitcast.67), channel_id=1, source_target_pairs={{0,128},{64,192},{128,256},{192,320},{256,384},{320,448},{384,512}... | collective-permute-start | bytes 884744 | tf_op jit(solution)/shard_map/ppermute | solution.py:66
  52.7 8.7 %collective-permute-start.4 = (bf16[768,256]{1,0:T(8,128)(2,1)S(1)}, bf16[768,256]{1,0:T(8,128)(2,1)S(1)}, u32[]{:S(2)}, u32[]{:S(2)}) collective-permute-start(bf16[768,256]{1,0:T(8,128)(2,1)S(1)} %bitcast.65), channel_id=1, source_target_pairs={{0,64},{64,0},{128,192},{192,128},{256,320},{320,256},{384,448},{4... | collective-permute-start | bytes 1179656 | tf_op jit(solution)/shard_map/ppermute | solution.py:105
  55.5 10.5 %collective-permute-start.2 = (bf16[192,768]{1,0:T(8,128)(2,1)S(1)}, bf16[192,768]{1,0:T(8,128)(2,1)S(1)}, u32[]{:S(2)}, u32[]{:S(2)}) collective-permute-start(bf16[192,768]{1,0:T(8,128)(2,1)S(1)} %collective-permute-done), channel_id=1, source_target_pairs={{0,896},{64,960},{128,0},{192,64},{256,128},{320,192},{384,256},{4... | collective-permute-start | bytes 884744 | tf_op jit(solution)/shard_map/ppermute | solution.py:66
  58.6 11.7 %collective-permute-start.3 = (bf16[192,768]{1,0:T(8,128)(2,1)S(1)}, bf16[192,768]{1,0:T(8,128)(2,1)S(1)}, u32[]{:S(2)}, u32[]{:S(2)}) collective-permute-start(bf16[192,768]{1,0:T(8,128)(2,1)S(1)} %collective-permute-done.1), channel_id=1, source_target_pairs={{0,128},{64,192},{128,256},{192,320},{256,384},{320,448},{384,512}... | collective-permute-start | bytes 884744 | tf_op jit(solution)/shard_map/ppermute | solution.py:66
  66.0 16.9 %collective-permute-start.5 = (bf16[192,768]{1,0:T(8,128)(2,1)S(1)}, bf16[192,768]{1,0:T(8,128)(2,1)S(1)}, u32[]{:S(2)}, u32[]{:S(2)}) collective-permute-start(bf16[192,768]{1,0:T(8,128)(2,1)S(1)} %collective-permute-done.2), channel_id=1, source_target_pairs={{0,896},{64,960},{128,0},{192,64},{256,128},{320,192},{384,256},{4... | collective-permute-start | bytes 884744 | tf_op jit(solution)/shard_map/ppermute | solution.py:66
  70.4 10.6 %collective-permute-start.6 = (bf16[192,768]{1,0:T(8,128)(2,1)S(1)}, bf16[192,768]{1,0:T(8,128)(2,1)S(1)}, u32[]{:S(2)}, u32[]{:S(2)}) collective-permute-start(bf16[192,768]{1,0:T(8,128)(2,1)S(1)} %collective-permute-done.3), channel_id=1, source_target_pairs={{0,128},{64,192},{128,256},{192,320},{256,384},{320,448},{384,512}... | collective-permute-start | bytes 884744 | tf_op jit(solution)/shard_map/ppermute | solution.py:66
  72.4 1.1 copy-start.6
  81.0 8.2 %collective-permute-start.7 = (bf16[96,768]{1,0:T(8,128)(2,1)S(1)}, bf16[96,768]{1,0:T(8,128)(2,1)S(1)}, u32[]{:S(2)}, u32[]{:S(2)}) collective-permute-start(bf16[96,768]{1,0:T(8,128)(2,1)S(1)} %slice.61), channel_id=1, source_target_pairs={{0,128},{64,192},{128,256},{192,320},{256,384},{320,448},{384,512}... | collective-permute-start | bytes 442376 | tf_op jit(solution)/shard_map/ppermute | solution.py:66
  83.0 7.8 %collective-permute-start.8 = (bf16[96,768]{1,0:T(8,128)(2,1)S(1)}, bf16[96,768]{1,0:T(8,128)(2,1)S(1)}, u32[]{:S(2)}, u32[]{:S(2)}) collective-permute-start(bf16[96,768]{1,0:T(8,128)(2,1)S(1)} %slice.62), channel_id=1, source_target_pairs={{0,896},{64,960},{128,0},{192,64},{256,128},{320,192},{384,256},{4... | collective-permute-start | bytes 442376 | tf_op jit(solution)/shard_map/ppermute | solution.py:66
  90.8 1.0 copy-start
  93.8 51.9 %all-to-all-start.1 = ((bf16[64,24,512]{2,1,0:T(8,128)(2,1)}), bf16[64,24,512]{2,1,0:T(8,128)(2,1)S(1)}, u32[]{:S(2)}, u32[]{:S(2)}) async-start(bf16[64,24,512]{2,1,0:T(8,128)(2,1)} %maximum_bitcast_fusion), calls=%async_computation.1 | async-start | bytes 3145728 | tf_op jit(solution)/shard_map/all_to_all | solution.py:15
  106.9 1.2 copy-start.1
  107.0 1.8 %copy-start.7 = (bf16[960,768]{1,0:T(8,128)(2,1)S(1)}, bf16[960,768]{1,0:T(8,128)(2,1)}, u32[]{:S(2)}) copy-start(bf16[960,768]{1,0:T(8,128)(2,1)} %copy-done.6) | copy-start | bytes 4423684
  110.8 42.4 %collective-permute-start.9 = (f32[768,256]{1,0:T(8,128)}, f32[768,256]{1,0:T(8,128)}, u32[]{:S(2)}, u32[]{:S(2)}) collective-permute-start(f32[768,256]{1,0:T(8,128)} %constant_dynamic-slice_fusion), channel_id=1, source_target_pairs={{0,64},{64,0},{128,192},{192,128},{256,320},{320,256},{384,448},{4... | collective-permute-start | bytes 2359304 | tf_op jit(solution)/shard_map/ppermute | solution.py:137
  148.1 14.2 %all-to-all-start.2 = ((bf16[8,16,512]{2,1,0:T(8,128)(2,1)}), bf16[8,16,512]{2,1,0:T(8,128)(2,1)S(1)}, u32[]{:S(2)}, u32[]{:S(2)}) async-start(bf16[8,16,512]{2,1,0:T(8,128)(2,1)} %bitcast.15), calls=%async_computation.2 | async-start | bytes 262144 | tf_op jit(solution)/shard_map/all_to_all | solution.py:70

commit v5 on v4

--- a/solution.py
+++ b/solution.py
@@ -98,8 +98,9 @@
     for _ in range(1, chips // 2):
         up, down = shift(up, 1), shift(down, -1)
         around += [down, up]
-    middle = held // 2
-    around.append(jnp.concatenate([shift(up[:middle], 1), shift(down[middle:], -1)], axis=0))
+    last = [(d, (d + (CORES if d % CORES == 0 else -CORES)) % dp) for d in range(dp)]
+    far = lax.ppermute(jnp.where(core == 0, up, down), "dp", last)
+    around.append(with_layout_constraint(far, Layout((0, 1))))
 
     weight = down_weight[0]
     other = lax.ppermute(weight, "dp", swap)

time: 164 us -> 164 us (level)
  starting transfers between devices: 76.6 us -> 74.4 us
  waiting for transfers between devices: 62.1 us -> 64.1 us
    ppermute x0 -> x1, waiting for transfers between devices: none -> 6.85 us  [layer(): far = lax.ppermute(jnp.where(core == 0, up, down), 'dp', last)]
    ppermute x8 -> x6, waiting for transfers between devices: 14.8 us -> 10.2 us  [shift(): lax.ppermute(block, 'dp', [(d, (d + CORES * by) % dp) for d in range(dp)])]
    ppermute x8 -> x6, starting transfers between devices: 25 us -> 21.1 us  [shift(): lax.ppermute(block, 'dp', [(d, (d + CORES * by) % dp) for d in range(dp)])]
    ppermute x0 -> x1, starting transfers between devices: none -> 1.92 us  [layer(): far = lax.ppermute(jnp.where(core == 0, up, down), 'dp', last)]
    unnamed x27 -> x25, local copies, waits for them, and re-layouts: 3.54 us -> 3.33 us
  transfers between devices with their start and end apart: 14 -> 13, of which waited for: 8 -> 8; matrix products, arithmetic and copies ran while one was open for 9% -> 9% of each run, Pallas kernels for 0% -> 0%
where the time goes in v5:
time: 164 us; the launch traced here: 163 us
  starting transfers between devices  74.4 us (45%)
  waiting for transfers between devices  64.1 us (39%)
  other arithmetic  8.49 us (5%)
  local copies, waits for them, and re-layouts  7.42 us (5%)
  matrix products  7.03 us (4%)
    all_to_all x2, waiting for transfers between devices, expert_move(): lax.all_to_all(buffer, ('ctx', 'tp'), split_axis=0, concat_axis=0, tiled=...  31.1 us
    all_to_all x2, starting transfers between devices, expert_move(): lax.all_to_all(buffer, ('ctx', 'tp'), split_axis=0, concat_axis=0, tiled=...  26.1 us
    all_to_all x2, starting transfers between devices, chip_move(): lax.all_to_all(blocks, 'dp', split_axis=0, concat_axis=0, tiled=True, axi...  21.4 us
    ppermute x6, starting transfers between devices, shift(): lax.ppermute(block, 'dp', [(d, (d + CORES * by) % dp) for d in range(dp)])  21.1 us
    all_to_all x2, waiting for transfers between devices, chip_move(): lax.all_to_all(blocks, 'dp', split_axis=0, concat_axis=0, tiled=True, axi...  16 us
    ppermute x6, waiting for transfers between devices, shift(): lax.ppermute(block, 'dp', [(d, (d + CORES * by) % dp) for d in range(dp)])  10.2 us
    ppermute x1, waiting for transfers between devices, layer(): far = lax.ppermute(jnp.where(core == 0, up, down), 'dp', last)  6.85 us
    unnamed x25, local copies, waits for them, and re-layouts  3.33 us
  transfers between devices with their start and end apart: 13, of which 8 were waited for; matrix products, arithmetic and copies ran while one was open for 9% of the time, Pallas kernels for 0%

profile of v5, /device:TPU:16, one launch (start us, length us, event | category | flops | bytes accessed | tf_op | source)
XLA Modules:
  0.0 162.6 jit_solution(4277044162191991733)
XLA Ops:
  2.1 1.0 copy.58
  3.8 16.7 %all-to-all-start = ((bf16[8,16,640]{2,1,0:T(8,128)(2,1)}), bf16[8,16,640]{2,1,0:T(8,128)(2,1)S(1)}, u32[]{:S(2)}, u32[]{:S(2)}) async-start(bf16[8,16,640]{2,1,0:T(8,128)(2,1)} %copy.42), calls=%async_computation | async-start | bytes 327680 | tf_op jit(solution)/shard_map/all_to_all | solution.py:70
  21.1 9.1 %all-to-all-done = bf16[8,16,640]{2,1,0:T(8,128)(2,1)S(1)} async-done(((bf16[8,16,640]{2,1,0:T(8,128)(2,1)}), bf16[8,16,640]{2,1,0:T(8,128)(2,1)S(1)}, u32[]{:S(2)}, u32[]{:S(2)}) %all-to-all-start) | async-done | bytes 163872 | tf_op jit(solution)/shard_map/all_to_all | solution.py:70
  31.6 1.7 %convolution_convert_fusion = bf16[1536,512]{1,0:T(8,128)(2,1)} fusion(bf16[1536,128]{1,0:T(8,128)(2,1)S(1)} %get-tuple-element.9, bf16[1536,128]{1,0:T(8,128)(2,1)S(1)} %get-tuple-element.8, bf16[128,512]{1,0:T(8,128)(2,1)S(1)} %bitcast.71), kind=kOutput, calls=%fused_computation | convolution fusion | flops 405536768 | bytes 2490368 | tf_op jit(solution)/shard_map/dot_general | solution.py:91
  33.4 13.5 %all-to-all-start.3 = ((bf16[64,24,512]{2,1,0:T(8,128)(2,1)}), bf16[64,24,512]{2,1,0:T(8,128)(2,1)S(1)}, u32[]{:S(2)}, u32[]{:S(2)}) async-start(bf16[64,24,512]{2,1,0:T(8,128)(2,1)} %bitcast.21), calls=%async_computation.3 | async-start | bytes 3145728 | tf_op jit(solution)/shard_map/all_to_all | solution.py:15
  46.9 2.5 %collective-permute-start.1 = (bf16[192,768]{1,0:T(8,128)(2,1)S(1)}, bf16[192,768]{1,0:T(8,128)(2,1)S(1)}, u32[]{:S(2)}, u32[]{:S(2)}) collective-permute-start(bf16[192,768]{1,0:T(8,128)(2,1)S(1)} %bitcast.66), channel_id=1, source_target_pairs={{0,128},{64,192},{128,256},{192,320},{256,384},{320,448},{384,512}... | collective-permute-start | bytes 884744 | tf_op jit(solution)/shard_map/ppermute | solution.py:66
  49.3 4.6 %collective-permute-start = (bf16[192,768]{1,0:T(8,128)(2,1)S(1)}, bf16[192,768]{1,0:T(8,128)(2,1)S(1)}, u32[]{:S(2)}, u32[]{:S(2)}) collective-permute-start(bf16[192,768]{1,0:T(8,128)(2,1)S(1)} %bitcast.67), channel_id=1, source_target_pairs={{0,896},{64,960},{128,0},{192,64},{256,128},{320,192},{384,256},{4... | collective-permute-start | bytes 884744 | tf_op jit(solution)/shard_map/ppermute | solution.py:66
  53.9 1.9 %collective-permute-start.4 = (bf16[768,256]{1,0:T(8,128)(2,1)S(1)}, bf16[768,256]{1,0:T(8,128)(2,1)S(1)}, u32[]{:S(2)}, u32[]{:S(2)}) collective-permute-start(bf16[768,256]{1,0:T(8,128)(2,1)S(1)} %bitcast.65), channel_id=1, source_target_pairs={{0,64},{64,0},{128,192},{192,128},{256,320},{320,256},{384,448},{4... | collective-permute-start | bytes 1179656 | tf_op jit(solution)/shard_map/ppermute | solution.py:106
  55.9 0.8 collective-permute-done.1
  56.7 1.9 %collective-permute-start.3 = (bf16[192,768]{1,0:T(8,128)(2,1)S(1)}, bf16[192,768]{1,0:T(8,128)(2,1)S(1)}, u32[]{:S(2)}, u32[]{:S(2)}) collective-permute-start(bf16[192,768]{1,0:T(8,128)(2,1)S(1)} %collective-permute-done.1), channel_id=1, source_target_pairs={{0,128},{64,192},{128,256},{192,320},{256,384},{320,448},{384,512}... | collective-permute-start | bytes 884744 | tf_op jit(solution)/shard_map/ppermute | solution.py:66
  58.6 5.1 %collective-permute-start.2 = (bf16[192,768]{1,0:T(8,128)(2,1)S(1)}, bf16[192,768]{1,0:T(8,128)(2,1)S(1)}, u32[]{:S(2)}, u32[]{:S(2)}) collective-permute-start(bf16[192,768]{1,0:T(8,128)(2,1)S(1)} %collective-permute-done), channel_id=1, source_target_pairs={{0,896},{64,960},{128,0},{192,64},{256,128},{320,192},{384,256},{4... | collective-permute-start | bytes 884744 | tf_op jit(solution)/shard_map/ppermute | solution.py:66
  63.9 4.5 %collective-permute-done.3 = bf16[192,768]{1,0:T(8,128)(2,1)S(1)} collective-permute-done((bf16[192,768]{1,0:T(8,128)(2,1)S(1)}, bf16[192,768]{1,0:T(8,128)(2,1)S(1)}, u32[]{:S(2)}, u32[]{:S(2)}) %collective-permute-start.3) | collective-permute-done | bytes 294944 | tf_op jit(solution)/shard_map/ppermute | solution.py:66
  68.4 1.9 %collective-permute-start.6 = (bf16[192,768]{1,0:T(8,128)(2,1)S(1)}, bf16[192,768]{1,0:T(8,128)(2,1)S(1)}, u32[]{:S(2)}, u32[]{:S(2)}) collective-permute-start(bf16[192,768]{1,0:T(8,128)(2,1)S(1)} %collective-permute-done.3), channel_id=1, source_target_pairs={{0,128},{64,192},{128,256},{192,320},{256,384},{320,448},{384,512}... | collective-permute-start | bytes 884744 | tf_op jit(solution)/shard_map/ppermute | solution.py:66
  70.4 5.1 %collective-permute-start.5 = (bf16[192,768]{1,0:T(8,128)(2,1)S(1)}, bf16[192,768]{1,0:T(8,128)(2,1)S(1)}, u32[]{:S(2)}, u32[]{:S(2)}) collective-permute-start(bf16[192,768]{1,0:T(8,128)(2,1)S(1)} %collective-permute-done.2), channel_id=1, source_target_pairs={{0,896},{64,960},{128,0},{192,64},{256,128},{320,192},{384,256},{4... | collective-permute-start | bytes 884744 | tf_op jit(solution)/shard_map/ppermute | solution.py:66
  75.6 3.7 %collective-permute-done.6 = bf16[192,768]{1,0:T(8,128)(2,1)S(1)} collective-permute-done((bf16[192,768]{1,0:T(8,128)(2,1)S(1)}, bf16[192,768]{1,0:T(8,128)(2,1)S(1)}, u32[]{:S(2)}, u32[]{:S(2)}) %collective-permute-start.6) | collective-permute-done | bytes 294944 | tf_op jit(solution)/shard_map/ppermute | solution.py:66
  79.3 1.2 collective-permute-done.5
  80.6 1.9 %collective-permute-start.7 = (bf16[192,768]{1,0:T(8,128)(2,1)S(1)}, bf16[192,768]{1,0:T(8,128)(2,1)S(1)}, u32[]{:S(2)}, u32[]{:S(2)}) collective-permute-start(bf16[192,768]{1,0:T(8,128)(2,1)S(1)} %get-tuple-element.4), channel_id=1, source_target_pairs={{0,128},{64,960},{128,256},{192,64},{256,384},{320,192},{384,512},... | collective-permute-start | bytes 884744 | tf_op jit(solution)/shard_map/ppermute | solution.py:102
  82.5 0.9 convolution_convert_fusion.1
  84.0 6.8 %collective-permute-done.7 = bf16[192,768]{1,0:T(8,128)(2,1)S(1)} collective-permute-done((bf16[192,768]{1,0:T(8,128)(2,1)S(1)}, bf16[192,768]{1,0:T(8,128)(2,1)S(1)}, u32[]{:S(2)}, u32[]{:S(2)}) %collective-permute-start.7) | collective-permute-done | bytes 294944 | tf_op jit(solution)/shard_map/ppermute | solution.py:102
  92.2 1.7 %maximum_bitcast_fusion = bf16[64,24,512]{2,1,0:T(8,128)(2,1)} fusion(bf16[9,64,512]{2,0,1:T(8,128)(2,1)S(1)} %copy.46, bf16[15,64,512]{2,0,1:T(8,128)(2,1)S(1)} %copy.45), kind=kLoop, calls=%fused_computation.1 | loop fusion | flops 3145728 | bytes 3145728 | tf_op jit(solution)/shard_map/transpose | solution.py:118
  93.9 12.6 %all-to-all-start.1 = ((bf16[64,24,512]{2,1,0:T(8,128)(2,1)}), bf16[64,24,512]{2,1,0:T(8,128)(2,1)S(1)}, u32[]{:S(2)}, u32[]{:S(2)}) async-start(bf16[64,24,512]{2,1,0:T(8,128)(2,1)} %maximum_bitcast_fusion), calls=%async_computation.1 | async-start | bytes 3145728 | tf_op jit(solution)/shard_map/all_to_all | solution.py:15
  107.1 1.0 copy-done.1
  108.2 0.8 fusion.35
  109.0 1.0 convolution_add_fusion
  110.0 1.0 constant_dynamic-slice_fusion
  111.0 1.9 %collective-permute-start.8 = (f32[768,256]{1,0:T(8,128)}, f32[768,256]{1,0:T(8,128)}, u32[]{:S(2)}, u32[]{:S(2)}) collective-permute-start(f32[768,256]{1,0:T(8,128)} %constant_dynamic-slice_fusion), channel_id=1, source_target_pairs={{0,64},{64,0},{128,192},{192,128},{256,320},{320,256},{384,448},{4... | collective-permute-start | bytes 2359304 | tf_op jit(solution)/shard_map/ppermute | solution.py:138
  112.9 1.7 %compare_select_fusion.1 = (bf16[64,24,128]{2,0,1:T(8,128)(2,1)S(1)}, bf16[64,24,128]{2,0,1:T(8,128)(2,1)}) fusion(f32[64,128]{1,0:T(8,128)} %copy-done.5, f32[24]{0:T(128)} %copy-done.8, bf16[64,128]{1,0:T(8,128)(2,1)S(1)} %get-tuple-element.12, bf16[64,128]{1,0:T(8,128)(2,1)} %copy-done.4), kind=kLoop, calls=%fused_computation.12 | loop fusion | flops 589824 | bytes 852064 | tf_op jit(solution)/shard_map/jit(_where)/select_n | solution.py:44
  114.6 31.1 %all-to-all-done.1 = bf16[64,24,512]{2,1,0:T(8,128)(2,1)S(1)} async-done(((bf16[64,24,512]{2,1,0:T(8,128)(2,1)}), bf16[64,24,512]{2,1,0:T(8,128)(2,1)S(1)}, u32[]{:S(2)}, u32[]{:S(2)}) %all-to-all-start.1) | async-done | bytes 1572896 | tf_op jit(solution)/shard_map/all_to_all | solution.py:15
  145.7 1.7 %fusion.2 = f32[256,512]{1,0:T(8,128)S(1)} fusion(bf16[64,24,512]{2,1,0:T(8,128)(2,1)S(1)} %all-to-all-done.1, bf16[64,24,128]{2,0,1:T(8,128)(2,1)} %get-tuple-element.11, bf16[64,24,128]{2,0,1:T(8,128)(2,1)S(1)} %get-tuple-element.10), kind=kOutput, calls=%fused_computation.8 | convolution fusion | flops 404226048 | bytes 2883584 | tf_op jit(solution)/shard_map/dot_general | solution.py:120
  148.1 4.7 %all-to-all-start.2 = ((bf16[8,16,512]{2,1,0:T(8,128)(2,1)}), bf16[8,16,512]{2,1,0:T(8,128)(2,1)S(1)}, u32[]{:S(2)}, u32[]{:S(2)}) async-start(bf16[8,16,512]{2,1,0:T(8,128)(2,1)} %bitcast.15), calls=%async_computation.2 | async-start | bytes 262144 | tf_op jit(solution)/shard_map/all_to_all | solution.py:70
  152.8 2.2 %add_bitcast_fusion = f32[1,768,256]{2,1,0:T(8,128)} fusion(f32[768,256]{1,0:T(8,128)} %collective-permute-done.8, f32[768,512]{1,0:T(8,128)S(1)} %convolution_add_fusion, s32[]{:T(128)S(6)} %select_n.91), kind=kLoop, calls=%fused_computation.23 | loop fusion | flops 196608 | bytes 2359300 | tf_op jit(solution)/shard_map/broadcast_in_dim | solution.py:139
  155.0 6.9 %all-to-all-done.2 = bf16[8,16,512]{2,1,0:T(8,128)(2,1)S(1)} async-done(((bf16[8,16,512]{2,1,0:T(8,128)(2,1)}), bf16[8,16,512]{2,1,0:T(8,128)(2,1)S(1)}, u32[]{:S(2)}, u32[]{:S(2)}) %all-to-all-start.2) | async-done | bytes 131104 | tf_op jit(solution)/shard_map/all_to_all | solution.py:70
  (65 shorter events, 8.3 us)
Async XLA Ops:
  3.8 26.5 %all-to-all-start = ((bf16[8,16,640]{2,1,0:T(8,128)(2,1)}), bf16[8,16,640]{2,1,0:T(8,128)(2,1)S(1)}, u32[]{:S(2)}, u32[]{:S(2)}) async-start(bf16[8,16,640]{2,1,0:T(8,128)(2,1)} %copy.42), calls=%async_computation | async-start | bytes 327680 | tf_op jit(solution)/shard_map/all_to_all | solution.py:70
  20.5 0.5 copy-start.8
  30.8 0.6 copy-start.4
  31.0 0.6 copy-start.5
  33.3 13.5 %copy-start.3 = (bf16[1,1,64,3,768]{4,2,3,1,0:T(8,128)(2,1)S(1)}, bf16[1,1,64,3,768]{4,2,3,1,0:T(8,128)(2,1)}, u32[]{:S(2)}) copy-start(bf16[1,1,64,3,768]{4,2,3,1,0:T(8,128)(2,1)} %param.7) | copy-start | bytes 884740
  33.3 20.6 %copy-start.2 = (bf16[1,768,256]{2,1,0:T(8,128)(2,1)S(1)}, bf16[1,768,256]{2,1,0:T(8,128)(2,1)}, u32[]{:S(2)}) copy-start(bf16[1,768,256]{2,1,0:T(8,128)(2,1)} %param.8) | copy-start | bytes 1179652
  33.4 60.6 %all-to-all-start.3 = ((bf16[64,24,512]{2,1,0:T(8,128)(2,1)}), bf16[64,24,512]{2,1,0:T(8,128)(2,1)S(1)}, u32[]{:S(2)}, u32[]{:S(2)}) async-start(bf16[64,24,512]{2,1,0:T(8,128)(2,1)} %bitcast.21), calls=%async_computation.3 | async-start | bytes 3145728 | tf_op jit(solution)/shard_map/all_to_all | solution.py:15
  46.9 9.8 %collective-permute-start.1 = (bf16[192,768]{1,0:T(8,128)(2,1)S(1)}, bf16[192,768]{1,0:T(8,128)(2,1)S(1)}, u32[]{:S(2)}, u32[]{:S(2)}) collective-permute-start(bf16[192,768]{1,0:T(8,128)(2,1)S(1)} %bitcast.66), channel_id=1, source_target_pairs={{0,128},{64,192},{128,256},{192,320},{256,384},{320,448},{384,512}... | collective-permute-start | bytes 884744 | tf_op jit(solution)/shard_map/ppermute | solution.py:66
  49.3 9.3 %collective-permute-start = (bf16[192,768]{1,0:T(8,128)(2,1)S(1)}, bf16[192,768]{1,0:T(8,128)(2,1)S(1)}, u32[]{:S(2)}, u32[]{:S(2)}) collective-permute-start(bf16[192,768]{1,0:T(8,128)(2,1)S(1)} %bitcast.67), channel_id=1, source_target_pairs={{0,896},{64,960},{128,0},{192,64},{256,128},{320,192},{384,256},{4... | collective-permute-start | bytes 884744 | tf_op jit(solution)/shard_map/ppermute | solution.py:66
  53.9 9.9 %collective-permute-start.4 = (bf16[768,256]{1,0:T(8,128)(2,1)S(1)}, bf16[768,256]{1,0:T(8,128)(2,1)S(1)}, u32[]{:S(2)}, u32[]{:S(2)}) collective-permute-start(bf16[768,256]{1,0:T(8,128)(2,1)S(1)} %bitcast.65), channel_id=1, source_target_pairs={{0,64},{64,0},{128,192},{192,128},{256,320},{320,256},{384,448},{4... | collective-permute-start | bytes 1179656 | tf_op jit(solution)/shard_map/ppermute | solution.py:106
  56.7 11.7 %collective-permute-start.3 = (bf16[192,768]{1,0:T(8,128)(2,1)S(1)}, bf16[192,768]{1,0:T(8,128)(2,1)S(1)}, u32[]{:S(2)}, u32[]{:S(2)}) collective-permute-start(bf16[192,768]{1,0:T(8,128)(2,1)S(1)} %collective-permute-done.1), channel_id=1, source_target_pairs={{0,128},{64,192},{128,256},{192,320},{256,384},{320,448},{384,512}... | collective-permute-start | bytes 884744 | tf_op jit(solution)/shard_map/ppermute | solution.py:66
  58.6 11.7 %collective-permute-start.2 = (bf16[192,768]{1,0:T(8,128)(2,1)S(1)}, bf16[192,768]{1,0:T(8,128)(2,1)S(1)}, u32[]{:S(2)}, u32[]{:S(2)}) collective-permute-start(bf16[192,768]{1,0:T(8,128)(2,1)S(1)} %collective-permute-done), channel_id=1, source_target_pairs={{0,896},{64,960},{128,0},{192,64},{256,128},{320,192},{384,256},{4... | collective-permute-start | bytes 884744 | tf_op jit(solution)/shard_map/ppermute | solution.py:66
  68.4 10.9 %collective-permute-start.6 = (bf16[192,768]{1,0:T(8,128)(2,1)S(1)}, bf16[192,768]{1,0:T(8,128)(2,1)S(1)}, u32[]{:S(2)}, u32[]{:S(2)}) collective-permute-start(bf16[192,768]{1,0:T(8,128)(2,1)S(1)} %collective-permute-done.3), channel_id=1, source_target_pairs={{0,128},{64,192},{128,256},{192,320},{256,384},{320,448},{384,512}... | collective-permute-start | bytes 884744 | tf_op jit(solution)/shard_map/ppermute | solution.py:66
  70.4 10.1 %collective-permute-start.5 = (bf16[192,768]{1,0:T(8,128)(2,1)S(1)}, bf16[192,768]{1,0:T(8,128)(2,1)S(1)}, u32[]{:S(2)}, u32[]{:S(2)}) collective-permute-start(bf16[192,768]{1,0:T(8,128)(2,1)S(1)} %collective-permute-done.2), channel_id=1, source_target_pairs={{0,896},{64,960},{128,0},{192,64},{256,128},{320,192},{384,256},{4... | collective-permute-start | bytes 884744 | tf_op jit(solution)/shard_map/ppermute | solution.py:66
  75.6 7.8 %copy-start.6 = (bf16[960,768]{1,0:T(8,128)(2,1)}, bf16[960,768]{1,0:T(8,128)(2,1)S(1)}, u32[]{:S(2)}) copy-start(bf16[960,768]{1,0:T(8,128)(2,1)S(1)} %constant_dynamic-update-slice_fusion) | copy-start | bytes 4423684
  80.6 10.3 %collective-permute-start.7 = (bf16[192,768]{1,0:T(8,128)(2,1)S(1)}, bf16[192,768]{1,0:T(8,128)(2,1)S(1)}, u32[]{:S(2)}, u32[]{:S(2)}) collective-permute-start(bf16[192,768]{1,0:T(8,128)(2,1)S(1)} %get-tuple-element.4), channel_id=1, source_target_pairs={{0,128},{64,960},{128,256},{192,64},{256,384},{320,192},{384,512},... | collective-permute-start | bytes 884744 | tf_op jit(solution)/shard_map/ppermute | solution.py:102
  90.9 1.0 copy-start
  93.9 51.7 %all-to-all-start.1 = ((bf16[64,24,512]{2,1,0:T(8,128)(2,1)}), bf16[64,24,512]{2,1,0:T(8,128)(2,1)S(1)}, u32[]{:S(2)}, u32[]{:S(2)}) async-start(bf16[64,24,512]{2,1,0:T(8,128)(2,1)} %maximum_bitcast_fusion), calls=%async_computation.1 | async-start | bytes 3145728 | tf_op jit(solution)/shard_map/all_to_all | solution.py:15
  107.0 1.2 copy-start.1
  107.1 1.8 %copy-start.7 = (bf16[960,768]{1,0:T(8,128)(2,1)S(1)}, bf16[960,768]{1,0:T(8,128)(2,1)}, u32[]{:S(2)}) copy-start(bf16[960,768]{1,0:T(8,128)(2,1)} %copy-done.6) | copy-start | bytes 4423684
  111.0 41.9 %collective-permute-start.8 = (f32[768,256]{1,0:T(8,128)}, f32[768,256]{1,0:T(8,128)}, u32[]{:S(2)}, u32[]{:S(2)}) collective-permute-start(f32[768,256]{1,0:T(8,128)} %constant_dynamic-slice_fusion), channel_id=1, source_target_pairs={{0,64},{64,0},{128,192},{192,128},{256,320},{320,256},{384,448},{4... | collective-permute-start | bytes 2359304 | tf_op jit(solution)/shard_map/ppermute | solution.py:138
  148.1 13.8 %all-to-all-start.2 = ((bf16[8,16,512]{2,1,0:T(8,128)(2,1)}), bf16[8,16,512]{2,1,0:T(8,128)(2,1)S(1)}, u32[]{:S(2)}, u32[]{:S(2)}) async-start(bf16[8,16,512]{2,1,0:T(8,128)(2,1)} %bitcast.15), calls=%async_computation.2 | async-start | bytes 262144 | tf_op jit(solution)/shard_map/all_to_all | solution.py:70

commit v6 on v5

--- a/solution.py
+++ b/solution.py
@@ -1,6 +1,7 @@
 import jax
 import jax.numpy as jnp
 from jax import lax
+from jax.experimental import pallas as pl
 from jax.experimental.layout import Layout, with_layout_constraint
 from jax.sharding import PartitionSpec as P
 
@@ -22,6 +23,23 @@
         parts.append(part.astype(BF16))
         values = values - part
     return parts
+
+
+def pack_kernel(routes_ref, gates_ref, grad_ref, out_ref):
+    chips, own, length = out_ref.shape
+    part = length - LANES
+    gates = gates_ref[...]
+    high = gates.astype(BF16)
+    rest = gates - high.astype(F32)
+    middle = rest.astype(BF16)
+    low = (rest - middle.astype(F32)).astype(BF16)
+    rows = [routes_ref[...].astype(F32), high.astype(F32), middle.astype(F32), low.astype(F32)]
+    rows = jnp.concatenate(rows, axis=0)
+    rows = jnp.concatenate([rows, jnp.zeros((LANES - rows.shape[0], own), F32)], axis=0)
+    table = rows.T.astype(BF16)
+    for chip in range(chips):
+        out_ref[chip, :, :part] = grad_ref[:, chip * part : (chip + 1) * part]
+        out_ref[chip, :, part:] = table
 
 
 def placer_of(named, gates, experts, own, capacity, place_of):
@@ -77,12 +95,11 @@
             ahead > chips // 2, 2 * (chips - ahead), jnp.maximum(2 * ahead - 1, 0)
         )
 
-    table = jnp.concatenate(
-        [routed_experts.astype(F32).astype(BF16), *parts_of(route_gates, 3)], axis=1
-    )
-    table = jnp.pad(table, ((0, 0), (0, LANES - table.shape[1])))
-    blocks = jnp.swapaxes(output_grad.reshape(own, chips, part), 0, 1)
-    blocks = jnp.concatenate([blocks, jnp.broadcast_to(table, (chips, own, LANES))], axis=2)
+    blocks = pl.pallas_call(
+        pack_kernel,
+        out_shape=jax.ShapeDtypeStruct((chips, own, part + LANES), BF16),
+        name="pack_columns",
+    )(routed_experts.T, route_gates.T, output_grad)
     arrived = chip_move(blocks)
     grads = arrived[:, :, :part].reshape(tokens, part)
     tables = arrived[:, :, part:].reshape(tokens, LANES).astype(F32)

time: 164 us -> 162 us (0.988)
  local copies, waits for them, and re-layouts: 7.42 us -> 5.17 us
  Pallas kernels: 0 us -> 1.68 us
    pallas_call x0 -> x1, Pallas kernels: none -> 1.68 us  [layer(): pl.pallas_call(pack_kernel, out_shape=jax.ShapeDtypeStruct((chips, own, p...]
    unnamed x25 -> x23, local copies, waits for them, and re-layouts: 3.33 us -> 1.78 us
where the time goes in v6:
time: 162 us; the launch traced here: 161 us
  starting transfers between devices  74.4 us (46%)
  waiting for transfers between devices  64.6 us (40%)
  other arithmetic  7.09 us (4%)
  matrix products  7.04 us (4%)
  local copies, waits for them, and re-layouts  5.17 us (3%)
  Pallas kernels  1.68 us (1%)
    all_to_all x2, waiting for transfers between devices, expert_move(): lax.all_to_all(buffer, ('ctx', 'tp'), split_axis=0, concat_axis=0, tiled=...  31.1 us
    all_to_all x2, starting transfers between devices, expert_move(): lax.all_to_all(buffer, ('ctx', 'tp'), split_axis=0, concat_axis=0, tiled=...  26.1 us
    all_to_all x2, starting transfers between devices, chip_move(): lax.all_to_all(blocks, 'dp', split_axis=0, concat_axis=0, tiled=True, axi...  21.4 us
    ppermute x6, starting transfers between devices, shift(): lax.ppermute(block, 'dp', [(d, (d + CORES * by) % dp) for d in range(dp)])  21.1 us
    all_to_all x2, waiting for transfers between devices, chip_move(): lax.all_to_all(blocks, 'dp', split_axis=0, concat_axis=0, tiled=True, axi...  16.5 us
    ppermute x6, waiting for transfers between devices, shift(): lax.ppermute(block, 'dp', [(d, (d + CORES * by) % dp) for d in range(dp)])  10.2 us
    ppermute x1, waiting for transfers between devices, layer(): far = lax.ppermute(jnp.where(core == 0, up, down), 'dp', last)  6.85 us
  transfers between devices with their start and end apart: 13, of which 8 were waited for; matrix products, arithmetic and copies ran while one was open for 9% of the time, Pallas kernels for 0%

profile of v6, /device:TPU:16, one launch (start us, length us, event | category | flops | bytes accessed | tf_op | source)
XLA Modules:
  0.0 161.1 jit_solution(5146007479419293756)
XLA Ops:
  0.6 1.7 %pack_columns.1 = bf16[8,16,640]{2,1,0:T(8,128)(2,1)} custom-call(s32[8,16]{1,0:T(8,128)} %bitcast.68, f32[8,16]{1,0:T(8,128)} %bitcast.69, bf16[16,4096]{1,0:T(8,128)(2,1)} %grad_ref.1), custom_call_target="tpu_custom_call" | custom-call | tf_op jit(solution)/shard_map/pack_columns/pallas_call | solution.py:98
  2.3 16.7 %all-to-all-start = ((bf16[8,16,640]{2,1,0:T(8,128)(2,1)}), bf16[8,16,640]{2,1,0:T(8,128)(2,1)S(1)}, u32[]{:S(2)}, u32[]{:S(2)}) async-start(bf16[8,16,640]{2,1,0:T(8,128)(2,1)} %pack_columns.1), calls=%async_computation | async-start | bytes 327680 | tf_op jit(solution)/shard_map/all_to_all | solution.py:88
  19.2 9.6 %all-to-all-done = bf16[8,16,640]{2,1,0:T(8,128)(2,1)S(1)} async-done(((bf16[8,16,640]{2,1,0:T(8,128)(2,1)}), bf16[8,16,640]{2,1,0:T(8,128)(2,1)S(1)}, u32[]{:S(2)}, u32[]{:S(2)}) %all-to-all-start) | async-done | bytes 163872 | tf_op jit(solution)/shard_map/all_to_all | solution.py:88
  30.2 1.7 %convolution_convert_fusion = bf16[1536,512]{1,0:T(8,128)(2,1)} fusion(bf16[1536,128]{1,0:T(8,128)(2,1)S(1)} %get-tuple-element.9, bf16[1536,128]{1,0:T(8,128)(2,1)S(1)} %get-tuple-element.8, bf16[128,512]{1,0:T(8,128)(2,1)S(1)} %bitcast.67), kind=kOutput, calls=%fused_computation | convolution fusion | flops 405536768 | bytes 2490368 | tf_op jit(solution)/shard_map/dot_general | solution.py:108
  31.9 13.5 %all-to-all-start.3 = ((bf16[64,24,512]{2,1,0:T(8,128)(2,1)}), bf16[64,24,512]{2,1,0:T(8,128)(2,1)S(1)}, u32[]{:S(2)}, u32[]{:S(2)}) async-start(bf16[64,24,512]{2,1,0:T(8,128)(2,1)} %bitcast.22), calls=%async_computation.3 | async-start | bytes 3145728 | tf_op jit(solution)/shard_map/all_to_all | solution.py:16
  45.4 2.5 %collective-permute-start.1 = (bf16[192,768]{1,0:T(8,128)(2,1)S(1)}, bf16[192,768]{1,0:T(8,128)(2,1)S(1)}, u32[]{:S(2)}, u32[]{:S(2)}) collective-permute-start(bf16[192,768]{1,0:T(8,128)(2,1)S(1)} %bitcast.63), channel_id=1, source_target_pairs={{0,128},{64,192},{128,256},{192,320},{256,384},{320,448},{384,512}... | collective-permute-start | bytes 884744 | tf_op jit(solution)/shard_map/ppermute | solution.py:84
  47.9 4.6 %collective-permute-start = (bf16[192,768]{1,0:T(8,128)(2,1)S(1)}, bf16[192,768]{1,0:T(8,128)(2,1)S(1)}, u32[]{:S(2)}, u32[]{:S(2)}) collective-permute-start(bf16[192,768]{1,0:T(8,128)(2,1)S(1)} %bitcast.64), channel_id=1, source_target_pairs={{0,896},{64,960},{128,0},{192,64},{256,128},{320,192},{384,256},{4... | collective-permute-start | bytes 884744 | tf_op jit(solution)/shard_map/ppermute | solution.py:84
  52.5 1.9 %collective-permute-start.4 = (bf16[768,256]{1,0:T(8,128)(2,1)S(1)}, bf16[768,256]{1,0:T(8,128)(2,1)S(1)}, u32[]{:S(2)}, u32[]{:S(2)}) collective-permute-start(bf16[768,256]{1,0:T(8,128)(2,1)S(1)} %bitcast.62), channel_id=1, source_target_pairs={{0,64},{64,0},{128,192},{192,128},{256,320},{320,256},{384,448},{4... | collective-permute-start | bytes 1179656 | tf_op jit(solution)/shard_map/ppermute | solution.py:123
  54.4 0.8 collective-permute-done.1
  55.2 1.9 %collective-permute-start.3 = (bf16[192,768]{1,0:T(8,128)(2,1)S(1)}, bf16[192,768]{1,0:T(8,128)(2,1)S(1)}, u32[]{:S(2)}, u32[]{:S(2)}) collective-permute-start(bf16[192,768]{1,0:T(8,128)(2,1)S(1)} %collective-permute-done.1), channel_id=1, source_target_pairs={{0,128},{64,192},{128,256},{192,320},{256,384},{320,448},{384,512}... | collective-permute-start | bytes 884744 | tf_op jit(solution)/shard_map/ppermute | solution.py:84
  57.1 5.1 %collective-permute-start.2 = (bf16[192,768]{1,0:T(8,128)(2,1)S(1)}, bf16[192,768]{1,0:T(8,128)(2,1)S(1)}, u32[]{:S(2)}, u32[]{:S(2)}) collective-permute-start(bf16[192,768]{1,0:T(8,128)(2,1)S(1)} %collective-permute-done), channel_id=1, source_target_pairs={{0,896},{64,960},{128,0},{192,64},{256,128},{320,192},{384,256},{4... | collective-permute-start | bytes 884744 | tf_op jit(solution)/shard_map/ppermute | solution.py:84
  62.4 4.5 %collective-permute-done.3 = bf16[192,768]{1,0:T(8,128)(2,1)S(1)} collective-permute-done((bf16[192,768]{1,0:T(8,128)(2,1)S(1)}, bf16[192,768]{1,0:T(8,128)(2,1)S(1)}, u32[]{:S(2)}, u32[]{:S(2)}) %collective-permute-start.3) | collective-permute-done | bytes 294944 | tf_op jit(solution)/shard_map/ppermute | solution.py:84
  67.0 1.9 %collective-permute-start.6 = (bf16[192,768]{1,0:T(8,128)(2,1)S(1)}, bf16[192,768]{1,0:T(8,128)(2,1)S(1)}, u32[]{:S(2)}, u32[]{:S(2)}) collective-permute-start(bf16[192,768]{1,0:T(8,128)(2,1)S(1)} %collective-permute-done.3), channel_id=1, source_target_pairs={{0,128},{64,192},{128,256},{192,320},{256,384},{320,448},{384,512}... | collective-permute-start | bytes 884744 | tf_op jit(solution)/shard_map/ppermute | solution.py:84
  68.9 5.1 %collective-permute-start.5 = (bf16[192,768]{1,0:T(8,128)(2,1)S(1)}, bf16[192,768]{1,0:T(8,128)(2,1)S(1)}, u32[]{:S(2)}, u32[]{:S(2)}) collective-permute-start(bf16[192,768]{1,0:T(8,128)(2,1)S(1)} %collective-permute-done.2), channel_id=1, source_target_pairs={{0,896},{64,960},{128,0},{192,64},{256,128},{320,192},{384,256},{4... | collective-permute-start | bytes 884744 | tf_op jit(solution)/shard_map/ppermute | solution.py:84
  74.2 3.7 %collective-permute-done.6 = bf16[192,768]{1,0:T(8,128)(2,1)S(1)} collective-permute-done((bf16[192,768]{1,0:T(8,128)(2,1)S(1)}, bf16[192,768]{1,0:T(8,128)(2,1)S(1)}, u32[]{:S(2)}, u32[]{:S(2)}) %collective-permute-start.6) | collective-permute-done | bytes 294944 | tf_op jit(solution)/shard_map/ppermute | solution.py:84
  77.8 1.2 collective-permute-done.5
  79.1 1.9 %collective-permute-start.7 = (bf16[192,768]{1,0:T(8,128)(2,1)S(1)}, bf16[192,768]{1,0:T(8,128)(2,1)S(1)}, u32[]{:S(2)}, u32[]{:S(2)}) collective-permute-start(bf16[192,768]{1,0:T(8,128)(2,1)S(1)} %get-tuple-element.4), channel_id=1, source_target_pairs={{0,128},{64,960},{128,256},{192,64},{256,384},{320,192},{384,512},... | collective-permute-start | bytes 884744 | tf_op jit(solution)/shard_map/ppermute | solution.py:119
  81.0 0.9 convolution_convert_fusion.1
  82.6 6.8 %collective-permute-done.7 = bf16[192,768]{1,0:T(8,128)(2,1)S(1)} collective-permute-done((bf16[192,768]{1,0:T(8,128)(2,1)S(1)}, bf16[192,768]{1,0:T(8,128)(2,1)S(1)}, u32[]{:S(2)}, u32[]{:S(2)}) %collective-permute-start.7) | collective-permute-done | bytes 294944 | tf_op jit(solution)/shard_map/ppermute | solution.py:119
  90.7 1.7 %maximum_bitcast_fusion = bf16[64,24,512]{2,1,0:T(8,128)(2,1)} fusion(bf16[9,64,512]{2,0,1:T(8,128)(2,1)S(1)} %copy.30, bf16[15,64,512]{2,0,1:T(8,128)(2,1)S(1)} %copy.29), kind=kLoop, calls=%fused_computation.1 | loop fusion | flops 3145728 | bytes 3145728 | tf_op jit(solution)/shard_map/transpose | solution.py:135
  92.4 12.6 %all-to-all-start.1 = ((bf16[64,24,512]{2,1,0:T(8,128)(2,1)}), bf16[64,24,512]{2,1,0:T(8,128)(2,1)S(1)}, u32[]{:S(2)}, u32[]{:S(2)}) async-start(bf16[64,24,512]{2,1,0:T(8,128)(2,1)} %maximum_bitcast_fusion), calls=%async_computation.1 | async-start | bytes 3145728 | tf_op jit(solution)/shard_map/all_to_all | solution.py:16
  105.7 1.0 copy-done.1
  106.7 0.8 fusion.33
  107.5 1.0 convolution_add_fusion
  108.5 1.0 constant_dynamic-slice_fusion
  109.5 1.9 %collective-permute-start.8 = (f32[768,256]{1,0:T(8,128)}, f32[768,256]{1,0:T(8,128)}, u32[]{:S(2)}, u32[]{:S(2)}) collective-permute-start(f32[768,256]{1,0:T(8,128)} %constant_dynamic-slice_fusion), channel_id=1, source_target_pairs={{0,64},{64,0},{128,192},{192,128},{256,320},{320,256},{384,448},{4... | collective-permute-start | bytes 2359304 | tf_op jit(solution)/shard_map/ppermute | solution.py:155
  111.4 1.7 %compare_select_fusion.1 = (bf16[64,24,128]{2,0,1:T(8,128)(2,1)S(1)}, bf16[64,24,128]{2,0,1:T(8,128)(2,1)}) fusion(f32[64,128]{1,0:T(8,128)} %copy-done.5, f32[24]{0:T(128)} %copy-done.8, bf16[64,128]{1,0:T(8,128)(2,1)S(1)} %get-tuple-element.12, bf16[64,128]{1,0:T(8,128)(2,1)} %copy-done.4), kind=kLoop, calls=%fused_computation.12 | loop fusion | flops 589824 | bytes 852064 | tf_op jit(solution)/shard_map/jit(_where)/select_n | solution.py:62
  113.1 31.1 %all-to-all-done.1 = bf16[64,24,512]{2,1,0:T(8,128)(2,1)S(1)} async-done(((bf16[64,24,512]{2,1,0:T(8,128)(2,1)}), bf16[64,24,512]{2,1,0:T(8,128)(2,1)S(1)}, u32[]{:S(2)}, u32[]{:S(2)}) %all-to-all-start.1) | async-done | bytes 1572896 | tf_op jit(solution)/shard_map/all_to_all | solution.py:16
  144.2 1.7 %fusion.2 = f32[256,512]{1,0:T(8,128)S(1)} fusion(bf16[64,24,512]{2,1,0:T(8,128)(2,1)S(1)} %all-to-all-done.1, bf16[64,24,128]{2,0,1:T(8,128)(2,1)} %get-tuple-element.11, bf16[64,24,128]{2,0,1:T(8,128)(2,1)S(1)} %get-tuple-element.10), kind=kOutput, calls=%fused_computation.8 | convolution fusion | flops 404226048 | bytes 2883584 | tf_op jit(solution)/shard_map/dot_general | solution.py:137
  146.6 4.7 %all-to-all-start.2 = ((bf16[8,16,512]{2,1,0:T(8,128)(2,1)}), bf16[8,16,512]{2,1,0:T(8,128)(2,1)S(1)}, u32[]{:S(2)}, u32[]{:S(2)}) async-start(bf16[8,16,512]{2,1,0:T(8,128)(2,1)} %bitcast.16), calls=%async_computation.2 | async-start | bytes 262144 | tf_op jit(solution)/shard_map/all_to_all | solution.py:88
  151.3 2.2 %add_bitcast_fusion = f32[1,768,256]{2,1,0:T(8,128)} fusion(f32[768,256]{1,0:T(8,128)} %collective-permute-done.8, f32[768,512]{1,0:T(8,128)S(1)} %convolution_add_fusion, s32[]{:T(128)S(6)} %select_n.91), kind=kLoop, calls=%fused_computation.23 | loop fusion | flops 196608 | bytes 2359300 | tf_op jit(solution)/shard_map/broadcast_in_dim | solution.py:156
  153.5 6.9 %all-to-all-done.2 = bf16[8,16,512]{2,1,0:T(8,128)(2,1)S(1)} async-done(((bf16[8,16,512]{2,1,0:T(8,128)(2,1)}), bf16[8,16,512]{2,1,0:T(8,128)(2,1)S(1)}, u32[]{:S(2)}, u32[]{:S(2)}) %all-to-all-start.2) | async-done | bytes 131104 | tf_op jit(solution)/shard_map/all_to_all | solution.py:88
  (57 shorter events, 5.6 us)
Async XLA Ops:
  2.3 26.5 %all-to-all-start = ((bf16[8,16,640]{2,1,0:T(8,128)(2,1)}), bf16[8,16,640]{2,1,0:T(8,128)(2,1)S(1)}, u32[]{:S(2)}, u32[]{:S(2)}) async-start(bf16[8,16,640]{2,1,0:T(8,128)(2,1)} %pack_columns.1), calls=%async_computation | async-start | bytes 327680 | tf_op jit(solution)/shard_map/all_to_all | solution.py:88
  19.0 9.9 %copy-start.8 = (f32[24]{0:T(128)}, f32[24]{0:T(128)S(1)}, u32[]{:S(2)}) copy-start(f32[24]{0:T(128)S(1)} %iota_convert_fusion) | copy-start | bytes 292
  29.3 0.6 copy-start.4
  29.5 0.6 copy-start.5
  31.9 13.5 %copy-start.3 = (bf16[1,1,64,3,768]{4,2,3,1,0:T(8,128)(2,1)S(1)}, bf16[1,1,64,3,768]{4,2,3,1,0:T(8,128)(2,1)}, u32[]{:S(2)}) copy-start(bf16[1,1,64,3,768]{4,2,3,1,0:T(8,128)(2,1)} %param.7) | copy-start | bytes 884740
  31.9 20.6 %copy-start.2 = (bf16[1,768,256]{2,1,0:T(8,128)(2,1)S(1)}, bf16[1,768,256]{2,1,0:T(8,128)(2,1)}, u32[]{:S(2)}) copy-start(bf16[1,768,256]{2,1,0:T(8,128)(2,1)} %param.8) | copy-start | bytes 1179652
  31.9 60.6 %all-to-all-start.3 = ((bf16[64,24,512]{2,1,0:T(8,128)(2,1)}), bf16[64,24,512]{2,1,0:T(8,128)(2,1)S(1)}, u32[]{:S(2)}, u32[]{:S(2)}) async-start(bf16[64,24,512]{2,1,0:T(8,128)(2,1)} %bitcast.22), calls=%async_computation.3 | async-start | bytes 3145728 | tf_op jit(solution)/shard_map/all_to_all | solution.py:16
  45.4 9.8 %collective-permute-start.1 = (bf16[192,768]{1,0:T(8,128)(2,1)S(1)}, bf16[192,768]{1,0:T(8,128)(2,1)S(1)}, u32[]{:S(2)}, u32[]{:S(2)}) collective-permute-start(bf16[192,768]{1,0:T(8,128)(2,1)S(1)} %bitcast.63), channel_id=1, source_target_pairs={{0,128},{64,192},{128,256},{192,320},{256,384},{320,448},{384,512}... | collective-permute-start | bytes 884744 | tf_op jit(solution)/shard_map/ppermute | solution.py:84
  47.9 9.3 %collective-permute-start = (bf16[192,768]{1,0:T(8,128)(2,1)S(1)}, bf16[192,768]{1,0:T(8,128)(2,1)S(1)}, u32[]{:S(2)}, u32[]{:S(2)}) collective-permute-start(bf16[192,768]{1,0:T(8,128)(2,1)S(1)} %bitcast.64), channel_id=1, source_target_pairs={{0,896},{64,960},{128,0},{192,64},{256,128},{320,192},{384,256},{4... | collective-permute-start | bytes 884744 | tf_op jit(solution)/shard_map/ppermute | solution.py:84
  52.5 9.9 %collective-permute-start.4 = (bf16[768,256]{1,0:T(8,128)(2,1)S(1)}, bf16[768,256]{1,0:T(8,128)(2,1)S(1)}, u32[]{:S(2)}, u32[]{:S(2)}) collective-permute-start(bf16[768,256]{1,0:T(8,128)(2,1)S(1)} %bitcast.62), channel_id=1, source_target_pairs={{0,64},{64,0},{128,192},{192,128},{256,320},{320,256},{384,448},{4... | collective-permute-start | bytes 1179656 | tf_op jit(solution)/shard_map/ppermute | solution.py:123
  55.2 11.7 %collective-permute-start.3 = (bf16[192,768]{1,0:T(8,128)(2,1)S(1)}, bf16[192,768]{1,0:T(8,128)(2,1)S(1)}, u32[]{:S(2)}, u32[]{:S(2)}) collective-permute-start(bf16[192,768]{1,0:T(8,128)(2,1)S(1)} %collective-permute-done.1), channel_id=1, source_target_pairs={{0,128},{64,192},{128,256},{192,320},{256,384},{320,448},{384,512}... | collective-permute-start | bytes 884744 | tf_op jit(solution)/shard_map/ppermute | solution.py:84
  57.1 11.7 %collective-permute-start.2 = (bf16[192,768]{1,0:T(8,128)(2,1)S(1)}, bf16[192,768]{1,0:T(8,128)(2,1)S(1)}, u32[]{:S(2)}, u32[]{:S(2)}) collective-permute-start(bf16[192,768]{1,0:T(8,128)(2,1)S(1)} %collective-permute-done), channel_id=1, source_target_pairs={{0,896},{64,960},{128,0},{192,64},{256,128},{320,192},{384,256},{4... | collective-permute-start | bytes 884744 | tf_op jit(solution)/shard_map/ppermute | solution.py:84
  67.0 10.9 %collective-permute-start.6 = (bf16[192,768]{1,0:T(8,128)(2,1)S(1)}, bf16[192,768]{1,0:T(8,128)(2,1)S(1)}, u32[]{:S(2)}, u32[]{:S(2)}) collective-permute-start(bf16[192,768]{1,0:T(8,128)(2,1)S(1)} %collective-permute-done.3), channel_id=1, source_target_pairs={{0,128},{64,192},{128,256},{192,320},{256,384},{320,448},{384,512}... | collective-permute-start | bytes 884744 | tf_op jit(solution)/shard_map/ppermute | solution.py:84
  68.9 10.1 %collective-permute-start.5 = (bf16[192,768]{1,0:T(8,128)(2,1)S(1)}, bf16[192,768]{1,0:T(8,128)(2,1)S(1)}, u32[]{:S(2)}, u32[]{:S(2)}) collective-permute-start(bf16[192,768]{1,0:T(8,128)(2,1)S(1)} %collective-permute-done.2), channel_id=1, source_target_pairs={{0,896},{64,960},{128,0},{192,64},{256,128},{320,192},{384,256},{4... | collective-permute-start | bytes 884744 | tf_op jit(solution)/shard_map/ppermute | solution.py:84
  74.2 7.8 %copy-start.6 = (bf16[960,768]{1,0:T(8,128)(2,1)}, bf16[960,768]{1,0:T(8,128)(2,1)S(1)}, u32[]{:S(2)}) copy-start(bf16[960,768]{1,0:T(8,128)(2,1)S(1)} %constant_dynamic-update-slice_fusion) | copy-start | bytes 4423684
  79.1 10.3 %collective-permute-start.7 = (bf16[192,768]{1,0:T(8,128)(2,1)S(1)}, bf16[192,768]{1,0:T(8,128)(2,1)S(1)}, u32[]{:S(2)}, u32[]{:S(2)}) collective-permute-start(bf16[192,768]{1,0:T(8,128)(2,1)S(1)} %get-tuple-element.4), channel_id=1, source_target_pairs={{0,128},{64,960},{128,256},{192,64},{256,384},{320,192},{384,512},... | collective-permute-start | bytes 884744 | tf_op jit(solution)/shard_map/ppermute | solution.py:119
  89.4 0.9 copy-start
  92.4 51.7 %all-to-all-start.1 = ((bf16[64,24,512]{2,1,0:T(8,128)(2,1)}), bf16[64,24,512]{2,1,0:T(8,128)(2,1)S(1)}, u32[]{:S(2)}, u32[]{:S(2)}) async-start(bf16[64,24,512]{2,1,0:T(8,128)(2,1)} %maximum_bitcast_fusion), calls=%async_computation.1 | async-start | bytes 3145728 | tf_op jit(solution)/shard_map/all_to_all | solution.py:16
  105.5 1.2 copy-start.1
  105.6 1.8 %copy-start.7 = (bf16[960,768]{1,0:T(8,128)(2,1)S(1)}, bf16[960,768]{1,0:T(8,128)(2,1)}, u32[]{:S(2)}) copy-start(bf16[960,768]{1,0:T(8,128)(2,1)} %copy-done.6) | copy-start | bytes 4423684
  109.5 41.9 %collective-permute-start.8 = (f32[768,256]{1,0:T(8,128)}, f32[768,256]{1,0:T(8,128)}, u32[]{:S(2)}, u32[]{:S(2)}) collective-permute-start(f32[768,256]{1,0:T(8,128)} %constant_dynamic-slice_fusion), channel_id=1, source_target_pairs={{0,64},{64,0},{128,192},{192,128},{256,320},{320,256},{384,448},{4... | collective-permute-start | bytes 2359304 | tf_op jit(solution)/shard_map/ppermute | solution.py:155
  146.6 13.8 %all-to-all-start.2 = ((bf16[8,16,512]{2,1,0:T(8,128)(2,1)}), bf16[8,16,512]{2,1,0:T(8,128)(2,1)S(1)}, u32[]{:S(2)}, u32[]{:S(2)}) async-start(bf16[8,16,512]{2,1,0:T(8,128)(2,1)} %bitcast.16), calls=%async_computation.2 | async-start | bytes 262144 | tf_op jit(solution)/shard_map/all_to_all | solution.py:88
